TPU v7x, 32 devices: a whole 2x2x4 slice. The times are simulated.
32 devices in a mesh: seq: 8 (over z, x), head: 4 (over y, core).
Axes of the slice: x: 2, y: 2, z: 4, core: 2. Of those that a mesh axis runs over, the one named last changes fastest.
Arguments:
- x_in: bfloat16 [2048, 4096], P('seq', 'head'), may hold values from -6 to 6
- z_gate: bfloat16 [2048, 4096], P('seq', 'head'), may hold values from -8 to 8
- b_proj: bfloat16 [2048, 4, 256], P('seq', 'head'), may hold values from -6 to 6
- c_proj: bfloat16 [2048, 4, 256], P('seq', 'head'), may hold values from -6 to 6
- log_decay: float32 [2048, 64], P('seq', 'head'), may hold values from -1 to 0
- norm_gain: float32 [4096], P('head'), may hold values from 0.5 to 1.5
- w_out: bfloat16 [4096, 8192], P('head', 'seq'), may hold values from -0.125 to 0.125
Outputs:
- mixed: bfloat16 [2048, 8192], P('seq', 'head')
All inputs are finite; a program needn't handle non-finite values.
Results may differ from a plain program's by a relative error of at most 0.015.
Values may be sent and summed in bfloat16 or wider, within the bound.
No kernel may reach another device: no remote copies, remote signals or barrier semaphores. Data moves between devices by JAX's collectives and lax.ppermute only.
A program may use at most 128 MiB of HBM per device.

v0:
```python
import jax
import jax.numpy as jnp
from jax import lax
from jax.sharding import PartitionSpec as P


def carried_in(value, axis, combine, identity):
    count, place = (lax.axis_size(axis), lax.axis_index(axis))
    everything = jax.tree.map(
        lambda part, kind: lax.all_gather(part.astype(kind), axis),
        value,
        (jnp.bfloat16, jnp.bfloat16),
    )
    start = jax.tree.map(
        lambda part, zero: jnp.broadcast_to(jnp.asarray(zero, part.dtype), part.shape),
        value,
        identity,
    )

    def hop(k, before):
        reached = k < place
        new = combine(
            before, jax.tree.map(lambda part, own: part[k].astype(own.dtype), everything, value)
        )
        return jax.tree.map(lambda a, b: jnp.where(reached, a, b), new, before)

    return lax.fori_loop(0, count, hop, start)


def combine(earlier, later):
    return (earlier[0] * later[0], later[0][:, None, None] * earlier[1] + later[1])


def carry_in(decay_total, state):
    identity = (jnp.ones_like(decay_total), jnp.zeros_like(state))
    return carried_in((decay_total, state), "seq", combine, identity)


def body(x_in, z_gate, b_proj, c_proj, log_decay, norm_gain, w_out):
    rows = x_in.shape[0]
    heads = log_decay.shape[1]
    head_dim = x_in.shape[1] // heads
    b_local = b_proj[:, 0, :]
    c_local = c_proj[:, 0, :]
    x_heads = x_in.reshape(rows, heads, head_dim)
    cum = jnp.cumsum(log_decay, axis=0)
    total = cum[-1]
    scores = jnp.dot(c_local, b_local.T, preferred_element_type=jnp.float32)
    index = jnp.arange(rows)
    causal = (index[:, None] >= index[None, :])[None]
    cum_t = cum.T
    diff = cum_t[:, :, None] - cum_t[:, None, :]
    mask = jnp.where(causal, jnp.exp(jnp.where(causal, diff, 0.0)), 0.0)
    weighted = (mask * scores[None]).astype(jnp.bfloat16)
    y_intra = jnp.einsum("hij,jhp->ihp", weighted, x_heads, preferred_element_type=jnp.float32)
    weights = jnp.exp(total[None, :] - cum)
    scaled = (weights[:, :, None] * x_heads.astype(jnp.float32)).astype(jnp.bfloat16)
    state = jnp.einsum("thp,tn->hpn", scaled, b_local, preferred_element_type=jnp.float32)
    carried = carry_in(jnp.exp(total), state)
    state_in = carried[1].astype(jnp.bfloat16)
    y_state = jnp.exp(cum)[:, :, None] * jnp.einsum(
        "tn,hpn->thp", c_local, state_in, preferred_element_type=jnp.float32
    )
    y_all = (y_intra + y_state).reshape(rows, heads * head_dim)
    gated = y_all * jax.nn.silu(z_gate.astype(jnp.float32))
    mean_sq = jnp.mean(gated * gated, axis=1, keepdims=True)
    hidden = (gated * lax.rsqrt(mean_sq + 1e-05) * norm_gain[None, :]).astype(jnp.bfloat16)
    partial_terms = jnp.dot(
        hidden, lax.all_gather(w_out, "seq", axis=1, tiled=True), preferred_element_type=jnp.float32
    )
    mixed = lax.psum_scatter(
        partial_terms.astype(jnp.bfloat16), "head", scatter_dimension=1, tiled=True
    )
    return mixed


def solution(mesh):
    placed = (
        P("seq", "head"),
        P("seq", "head"),
        P("seq", "head", None),
        P("seq", "head", None),
        P("seq", "head"),
        P("head"),
        P("head", "seq"),
    )
    return jax.shard_map(
        body, mesh=mesh, in_specs=placed, out_specs=P("seq", "head"), check_vma=False
    )
```

profile of v0, /device:TPU:1, one launch (start us, length us, event | category | flops | bytes accessed | tf_op | source)
XLA Modules:
  0.0 376.7 jit_solution(7258897654931674551)
XLA Ops:
  6.5 0.0 copy-start
  6.5 0.0 copy-start.1
  6.5 0.0 all-gather.7.cloned.1.call-start
  6.5 0.8 copy_bitcast_fusion.1
  7.3 0.6 reduce-window.6
  7.9 0.2 slice_reduce_fusion
  8.1 0.1 fusion.25
  8.2 0.2 slice_reduce_fusion.1
  8.3 0.1 bitcast_exponential_fusion
  8.4 1.2 copy.27
  9.7 0.1 fusion.14
  9.8 0.0 copy-done
  9.8 1.1 convolution_convert_fusion.1
  10.9 0.0 all-gather.7.cloned.1.call-update
  10.9 0.0 all-gather.5.cloned.1.call-start
  11.0 0.7 all-gather.5.cloned.1.call-update
  11.7 0.0 reduce-scatter.2.cloned.1.call-start
  11.7 0.2 fusion.23
  11.9 17.9 %all-gather.1 = bf16[8,1,16]{2,1,0:T(2,128)(2,1)S(1)} all-gather(bf16[1,1,16]{2,1,0:T(2,128)(2,1)S(1)} %bitcast.72), channel_id=1, replica_groups=mesh['seq'=8,'head'=4] {'seq'}, dimensions={0}, use_global_device_ids=true | all-gather | bytes 288 | tf_op jit(solution)/shard_map/all_gather | solution.py:10
  29.8 0.0 copy-done.1
  29.8 0.2 fusion.20
  30.0 1.2 fusion.7
  31.3 54.1 %all-gather.7.cloned.1.call-done = bf16[128,64,256]{2,1,0:T(8,128)(2,1)} async-done(((bf16[16,64,256]{2,1,0:T(8,128)(2,1)}), bf16[128,64,256]{2,1,0:T(8,128)(2,1)}) %all-gather.7.cloned.1.call-update) | async-done | bytes 4194320 | tf_op jit(solution)/shard_map/all_gather | solution.py:10
  85.4 10.7 %while.14 = (s32[]{:T(128)}, f32[16,64,256]{2,1,0:T(8,128)S(1)}, s32[]{:T(128)}, bf16[8,16]{1,0:T(8,128)(2,1)S(1)}, bf16[8,16,64,256]{3,2,1,0:T(8,128)(2,1)}, /*index=5*/s32[]{:T(128)}, s32[]{:T(128)}) while((s32[]{:T(128)}, f32[16,64,256]{2,1,0:T(8,128)S(1)}, s32[]{:T(128)}, bf16[8,16]{1,0:T(8,128)(2,1)S(1)}, ...), condition=%wide.region_3.4_spmd.clone, body=%wide.region_2.3_spmd.clone.sunk | while | flops 1310740 | bytes 2621705 | solution.py:27
  85.4 1.3 fusion.32
  86.7 1.3 fusion.32
  88.0 1.3 fusion.32
  89.4 1.3 fusion.32
  90.7 1.3 fusion.32
  92.0 1.3 fusion.32
  93.4 1.3 fusion.32
  94.7 1.4 fusion.32
  96.1 0.0 copy-start.2
  96.1 0.3 fusion.9
  96.5 0.3 copy.29
  96.8 1.5 multiply_reduce_fusion
  98.3 215.9 %all-gather.5.cloned.1.call-done = bf16[1024,8192]{1,0:T(8,128)(2,1)} async-done(((bf16[1024,1024]{1,0:T(8,128)(2,1)}), bf16[1024,8192]{1,0:T(8,128)(2,1)}) %all-gather.5.cloned.1.call-update) | async-done | bytes 16777232 | tf_op jit(solution)/shard_map/all_gather | solution.py:69
  314.2 0.0 copy-done.2
  314.2 12.6 %convolution_convert_fusion = bf16[256,8192]{1,0:T(8,128)(2,1)} fusion(bf16[1024,8192]{1,0:T(8,128)(2,1)} %all-gather.5.cloned.1.call-done, f32[1024]{0:T(1024)S(1)} %copy-done.2, f32[256]{0:T(256)S(1)} %add_rsqrt_fusion, f32[256,1024]{1,0:T(8,128)S(1)} %copy.29, bf16[256,1024]{1,0:T(8,128)(2,1)} %param.10), kind=kOutput, calls=%fused_computation.3 | convolution fusion | flops 4299423744 | bytes 22549504 | tf_op jit(solution)/shard_map/dot_general | solution.py:68
  326.9 0.0 reduce-scatter.2.cloned.1.call-update
  326.9 43.3 %reduce-scatter.2.cloned.1.call-done = bf16[256,2048]{1,0:T(8,128)(2,1)} async-done(((bf16[256,8192]{1,0:T(8,128)(2,1)}), bf16[256,2048]{1,0:T(8,128)(2,1)}) %reduce-scatter.2.cloned.1.call-update) | async-done | bytes 1048592 | tf_op jit(solution)/shard_map/reduce_scatter | solution.py:71
  (14 shorter events, 0.1 us)
Async XLA Ops:
  6.5 3.3 copy-start
  6.5 23.3 %copy-start.1 = (bf16[256,1,256]{2,0,1:T(8,128)(2,1)S(1)}, bf16[256,1,256]{2,0,1:T(8,128)(2,1)}, u32[]{:S(2)}) copy-start(bf16[256,1,256]{2,0,1:T(8,128)(2,1)} %param.12) | copy-start | bytes 393220
  6.5 78.8 %all-gather.7.cloned.1.call-start = ((), (), s32[]{:S(2)}) async-start(), calls=%async_computation.3 | async-start | bytes 4718592 | tf_op jit(solution)/shard_map/all_gather | solution.py:10
  10.9 303.3 %all-gather.5.cloned.1.call-start = ((), (), s32[]{:S(2)}) async-start(), calls=%async_computation.1 | async-start | bytes 18874368 | tf_op jit(solution)/shard_map/all_gather | solution.py:69
  11.7 358.5 %reduce-scatter.2.cloned.1.call-start = ((), (), s32[]{:S(2)}) async-start(), calls=%async_computation.2 | async-start | bytes 5242880 | tf_op jit(solution)/shard_map/reduce_scatter | solution.py:71
  96.1 218.1 %copy-start.2 = (f32[1024]{0:T(1024)S(1)}, f32[1024]{0:T(1024)}, u32[]{:S(2)}) copy-start(f32[1024]{0:T(1024)} %param.14) | copy-start | bytes 12292
Sparse Core Ops, SparseCore 0:
  11.0 74.2 all-gather.6
  87.6 226.6 all-gather.4
  327.0 43.0 reduce-scatter.1
where the time goes:
time: 378 us; the launch traced here: 377 us
  waiting for transfers between devices  314 us (83%)
  blocking collectives  17.9 us (5%)
  matrix products  15.5 us (4%)
  between operations  13.2 us (3%)
  other arithmetic  13.1 us (3%)
    all_gather x1, waiting for transfers between devices, body(): lax.all_gather(w_out, 'seq', axis=1, tiled=True)  216 us
    all_gather x1, waiting for transfers between devices, carried_in(): lax.all_gather(part.astype(kind), axis)  54.1 us
    reduce_scatter x1, waiting for transfers between devices, body(): lax.psum_scatter(partial_terms.astype(jnp.bfloat16), 'head', scatter_dime...  43.3 us
    all_gather x1, blocking collectives, carried_in(): lax.all_gather(part.astype(kind), axis)  17.9 us
    dot_general x1, matrix products, body(): jnp.dot(hidden, lax.all_gather(w_out, 'seq', axis=1, tiled=True), preferr...  12.6 us
    select_n x8, other arithmetic, hop(): return jax.tree.map(lambda a, b: jnp.where(reached, a, b), new, before)  10.4 us
  transfers between devices with their start and end apart: 3, of which 3 were waited for; matrix products, arithmetic and copies ran while one was open for 4% of the time, Pallas kernels for 0%

commit v1 on v0

v1 whole, which is shorter than its diff:
```python
import jax
import jax.numpy as jnp
from jax import lax
from jax.sharding import PartitionSpec as P

BF = jnp.bfloat16
F32 = jnp.float32


def decay_rows(decay, width):
    high = decay.astype(BF)
    low = (decay - high.astype(F32)).astype(BF)
    rows = jnp.concatenate([high, low])
    return jnp.broadcast_to(rows[:, None], (rows.shape[0], width))


def pack(state, decay):
    n, p, m = state.shape
    return jnp.concatenate([state.astype(BF).reshape(n * p, m), decay_rows(decay, m)])


def unpack(message, n):
    rows = message.shape[0] - 2 * n
    state = message[:rows].reshape(n, rows // n, -1).astype(F32)
    tail = message[rows:, 0].astype(F32)
    return state, tail[:n] + tail[n:]


def body(x_in, z_gate, b_proj, c_proj, log_decay, norm_gain, w_out):
    rows = x_in.shape[0]
    heads = log_decay.shape[1]
    head_dim = x_in.shape[1] // heads
    n_seq, n_head = lax.axis_size("seq"), lax.axis_size("head")
    r = n_seq // n_head
    n_y = n_head // 2
    me_seq, me_head = lax.axis_index("seq"), lax.axis_index("head")
    me_h, me_b = me_seq // r, me_seq % r

    def rot_b(v, j):
        pairs = [(h * r + b, h * r + (b + j) % r) for h in range(n_head) for b in range(r)]
        return lax.ppermute(v, "seq", pairs)

    def rot_h(v, k):
        pairs = [(h * r + b, (h + k) % n_head * r + b) for h in range(n_head) for b in range(r)]
        return lax.ppermute(v, "seq", pairs)

    def shift_h(v, k):
        pairs = [(h * r + b, (h + k) * r + b) for h in range(n_head - k) for b in range(r)]
        return lax.ppermute(v, "seq", pairs)

    def swap_core(v):
        return lax.ppermute(v, "head", [(i, i ^ 1) for i in range(n_head)])

    def rot_y(v, j):
        pairs = [(y * 2 + c, (y + j) % n_y * 2 + c) for y in range(n_y) for c in range(2)]
        return lax.ppermute(v, "head", pairs)

    def rot_head(v, j):
        return lax.ppermute(v, "head", [(i, (i + j) % n_head) for i in range(n_head)])

    pick = lambda v, i: lax.dynamic_index_in_dim(v, i, 0, keepdims=False)
    core = me_head % 2

    b_local = b_proj[:, 0, :]
    c_local = c_proj[:, 0, :]
    x_heads = x_in.reshape(rows, heads, head_dim)
    cum = jnp.cumsum(log_decay, axis=0)
    total = cum[-1]
    weights = jnp.exp(total[None, :] - cum)
    scaled = (weights[:, :, None] * x_heads.astype(F32)).astype(BF)
    state = jnp.einsum("thp,tn->hpn", scaled, b_local, preferred_element_type=F32)
    decay = jnp.exp(total)

    part = heads // r
    groups = jnp.stack(
        [pack(state[j * part : (j + 1) * part], decay[j * part : (j + 1) * part]) for j in range(r)]
    )
    got = [pick(groups, me_b)]
    for j in range(1, r):
        got.append(rot_b(pick(groups, (me_b + j) % r), j))
    got = jnp.stack(got)
    blocks = [unpack(pick(got, (me_b - i) % r), part) for i in range(r)]
    scale = lambda d, s: d[:, None, None] * s
    run, run_decay = blocks[0]
    for s, d in blocks[1:]:
        run, run_decay = scale(d, run) + s, d * run_decay
    before, before_decay = jnp.zeros_like(run), jnp.ones_like(run_decay)
    k = 1
    while k < n_head:
        s, d = unpack(shift_h(pack(run, run_decay), k), part)
        before, before_decay = before + scale(before_decay, s), before_decay * d
        run, run_decay = run + scale(run_decay, s), run_decay * d
        k *= 2
    entering = []
    for s, d in blocks:
        entering.append(before.astype(BF))
        before = scale(d, before) + s
    entering = jnp.stack(entering)
    back = [pick(entering, me_b)]
    for j in range(1, r):
        back.append(rot_b(pick(entering, (me_b + j) % r), j))
    back = jnp.stack(back)
    state_in = jnp.concatenate([pick(back, (me_b - i) % r) for i in range(r)])

    width = w_out.shape[1] // 2
    halves = jnp.stack([w_out[:, :width], w_out[:, width:]])
    w_mine = pick(halves, core)
    w_other = swap_core(pick(halves, 1 - core))
    w_pieces = [(w_mine, w_other)]
    for j in range(1, r):
        w_pieces.append((rot_b(w_mine, j), rot_b(w_other, j)))

    scores = jnp.dot(c_local, b_local.T, preferred_element_type=F32)
    index = jnp.arange(rows)
    causal = (index[:, None] >= index[None, :])[None]
    cum_t = cum.T
    diff = cum_t[:, :, None] - cum_t[:, None, :]
    mask = jnp.where(causal, jnp.exp(jnp.where(causal, diff, 0.0)), 0.0)
    weighted = (mask * scores[None]).astype(BF)
    y_intra = jnp.einsum("hij,jhp->ihp", weighted, x_heads, preferred_element_type=F32)
    y_state = jnp.exp(cum)[:, :, None] * jnp.einsum(
        "tn,hpn->thp", c_local, state_in, preferred_element_type=F32
    )
    y_all = (y_intra + y_state).reshape(rows, heads * head_dim)
    gated = y_all * jax.nn.silu(z_gate.astype(F32))
    mean_sq = jnp.mean(gated * gated, axis=1, keepdims=True)
    hidden = (gated * lax.rsqrt(mean_sq + 1e-05) * norm_gain[None, :]).astype(BF)

    piece = rows // n_y
    me_y = me_head // 2
    home = []
    for k in range(n_head):
        if k:
            hidden = rot_h(hidden, 1)
        other = swap_core(hidden)
        terms = [
            jnp.dot(hidden, w0, preferred_element_type=F32)
            + jnp.dot(other, w1, preferred_element_type=F32)
            for w0, w1 in w_pieces
        ]
        terms = jnp.stack(terms).reshape(r, n_y, piece, width)
        mine = lax.dynamic_index_in_dim(terms, me_y, 1, keepdims=False)
        for j in range(1, n_y):
            send = lax.dynamic_index_in_dim(terms, (me_y + j) % n_y, 1, keepdims=False)
            mine = mine + rot_y(send.astype(BF), j).astype(F32)
        mine = mine.astype(BF)
        home.append(rot_h(mine, -k) if k else mine)
    home = jnp.stack(home)
    final = [pick(home, (me_head - me_h) % n_head)]
    for j in range(1, n_head):
        final.append(rot_head(pick(home, (me_head + j - me_h) % n_head), j))
    final = jnp.stack(final)
    final = jnp.stack([pick(final, (me_head - i) % n_head) for i in range(n_head)])
    final = jnp.stack([lax.dynamic_index_in_dim(final, (me_b - i) % r, 1, False) for i in range(r)])
    final = final.reshape(r, n_y, 2, piece, width)
    return final.transpose(1, 3, 0, 2, 4).reshape(rows, r * 2 * width)


def solution(mesh):
    placed = (
        P("seq", "head"),
        P("seq", "head"),
        P("seq", "head", None),
        P("seq", "head", None),
        P("seq", "head"),
        P("head"),
        P("head", "seq"),
    )
    return jax.shard_map(
        body, mesh=mesh, in_specs=placed, out_specs=P("seq", "head"), check_vma=False
    )
```

time: 378 us -> 163 us (0.43)
  waiting for transfers between devices: 314 us -> 73.5 us
  starting transfers between devices: 0.08 us -> 37 us
  blocking collectives: 17.9 us -> 0 us
  between operations: 13.2 us -> 0.77 us
  local copies, waits for them, and re-layouts: 2.7 us -> 12.4 us
  other arithmetic: 13.1 us -> 21.4 us
    all_gather x2 -> x0, waiting for transfers between devices: 270 us -> none  [the longest x1 216 us: body(): lax.all_gather(w_out, 'seq', axis=1, tiled=True)]
    ppermute x0 -> x24, waiting for transfers between devices: none -> 73.5 us  [the longest x6 47.3 us: rot_h(): return lax.ppermute(v, 'seq', pairs)]
    reduce_scatter x1 -> x0, waiting for transfers between devices: 43.3 us -> none  [body(): lax.psum_scatter(partial_terms.astype(jnp.bfloat16), 'head', scatter_dime...]
    ppermute x0 -> x24, starting transfers between devices: none -> 37 us  [the longest x5 10.9 us: swap_core(): return lax.ppermute(v, 'head', [(i, i ^ 1) for i in range(n_head)])]
    all_gather x1 -> x0, blocking collectives: 17.9 us -> none  [carried_in(): lax.all_gather(part.astype(kind), axis)]
    select_n x8 -> x0, other arithmetic: 10.4 us -> none  [hop(): return jax.tree.map(lambda a, b: jnp.where(reached, a, b), new, before)]
    convert_element_type x10 -> x21, other arithmetic: 0.34 us -> 8.55 us  [the longest x2 2.34 us: pack(): state.astype(BF).reshape(n * p, m)]
    dot_general x5 -> x20, matrix products: 15.5 us -> 16.7 us  [the longest x8 8.64 us: body(): jnp.dot(other, w1, preferred_element_type=F32)]
  transfers between devices with their start and end apart: 3 -> 24, of which waited for: 3 -> 14; matrix products, arithmetic and copies ran while one was open for 4% -> 24% of each run, Pallas kernels for 0% -> 0%
where the time goes in v1:
time: 163 us; the launch traced here: 162 us
  waiting for transfers between devices  73.5 us (45%)
  starting transfers between devices  37 us (23%)
  other arithmetic  21.4 us (13%)
  matrix products  16.7 us (10%)
  local copies, waits for them, and re-layouts  12.4 us (8%)
    ppermute x6, waiting for transfers between devices, rot_h(): return lax.ppermute(v, 'seq', pairs)  47.3 us
    ppermute x3, waiting for transfers between devices, rot_head(): lax.ppermute(v, 'head', [(i, (i + j) % n_head) for i in range(n_head)])  12.2 us
    ppermute x5, starting transfers between devices, swap_core(): return lax.ppermute(v, 'head', [(i, i ^ 1) for i in range(n_head)])  10.9 us
    ppermute x2, starting transfers between devices, shift_h(): return lax.ppermute(v, 'seq', pairs)  8.66 us
    dot_general x8, matrix products, body(): jnp.dot(other, w1, preferred_element_type=F32)  8.64 us
    ppermute x6, starting transfers between devices, rot_h(): return lax.ppermute(v, 'seq', pairs)  6.76 us
    ppermute x4, waiting for transfers between devices, rot_y(): return lax.ppermute(v, 'head', pairs)  5.96 us
    ppermute x4, waiting for transfers between devices, rot_b(): return lax.ppermute(v, 'seq', pairs)  4.44 us
  transfers between devices with their start and end apart: 24, of which 14 were waited for; matrix products, arithmetic and copies ran while one was open for 24% of the time, Pallas kernels for 0%

profile of v1, /device:TPU:1, one launch (start us, length us, event | category | flops | bytes accessed | tf_op | source)
XLA Modules:
  0.0 161.9 jit_solution(16021749891766903656)
XLA Ops:
  0.0 0.8 copy_bitcast_fusion.1
  0.8 0.6 reduce-window.6
  1.5 0.7 fusion.75
  2.5 0.7 bitcast_exponential_fusion
  3.2 1.2 copy.55
  5.4 1.0 fusion.51
  6.4 2.0 %collective-permute-start = (bf16[528,256]{1,0:T(8,128)(2,1)}, bf16[528,256]{1,0:T(8,128)(2,1)S(1)}, u32[]{:S(2)}, u32[]{:S(2)}) collective-permute-start(bf16[528,256]{1,0:T(8,128)(2,1)} %get-tuple-element.25), channel_id=1, source_target_pairs={{0,4},{4,0},{8,12},{12,8},{16,20},{20,16},{24,28},{28,24},{1,5},{5... | collective-permute-start | bytes 811016 | tf_op jit(solution)/shard_map/ppermute | solution.py:41
  8.4 1.7 %slice_bitcast_fusion = (bf16[1,1024,512]{2,1,0:T(8,128)(2,1)S(1)}, bf16[1,1024,512]{2,1,0:T(8,128)(2,1)S(1)}) fusion(bf16[1024,1024]{1,0:T(8,128)(2,1)} %param.13), kind=kLoop, calls=%fused_computation.56 | loop fusion | bytes 4194304 | tf_op jit(solution)/shard_map/stack | solution.py:106
  10.1 1.7 %fusion.14 = (bf16[1024,512]{1,0:T(8,128)(2,1)}, bf16[1024,512]{1,0:T(8,128)(2,1)S(1)}) fusion(s32[]{:T(128)S(6)} %select_n.167, bf16[1,1024,512]{2,1,0:T(8,128)(2,1)S(1)} %get-tuple-element.10, bf16[1,1024,512]{2,1,0:T(8,128)(2,1)S(1)} %get-tuple-element.9, s32[]{:T(128)S(6)} %select_n.166), kind=kLoop, calls=%fused_computation.47 | loop fusion | flops 1048576 | bytes 4194312 | tf_op jit(solution)/shard_map/jit(dynamic_index_in_dim)/squeeze | solution.py:61
  11.8 1.0 collective-permute-start.5
  12.8 2.0 %collective-permute-done = bf16[528,256]{1,0:T(8,128)(2,1)S(1)} collective-permute-done((bf16[528,256]{1,0:T(8,128)(2,1)}, bf16[528,256]{1,0:T(8,128)(2,1)S(1)}, u32[]{:S(2)}, u32[]{:S(2)}) %collective-permute-start) | collective-permute-done | bytes 270368 | tf_op jit(solution)/shard_map/ppermute | solution.py:41
  14.8 0.7 copy-done.10
  15.5 1.2 fusion.48
  16.9 0.6 copy-done.6
  18.8 1.1 fusion.46
  19.9 0.7 pad_maximum_fusion.6
  20.6 0.8 pad_maximum_fusion.3
  21.4 3.8 %collective-permute-start.1 = (bf16[528,256]{1,0:T(8,128)(2,1)}, bf16[528,256]{1,0:T(8,128)(2,1)}, u32[]{:S(2)}, u32[]{:S(2)}) collective-permute-start(bf16[528,256]{1,0:T(8,128)(2,1)} %pad_maximum_fusion.3), channel_id=1, source_target_pairs={{0,8},{4,12},{8,16},{12,20},{16,24},{20,28},{1,9},{5,13},{9,17},{1... | collective-permute-start | bytes 811016 | tf_op jit(solution)/shard_map/ppermute | solution.py:49
  25.3 0.6 iota_compare_fusion
  25.9 1.8 %fusion.67 = f32[256,256]{1,0:T(8,128)} fusion(bf16[256,1,256]{2,0,1:T(8,128)(2,1)S(1)} %copy-done, bf16[256,1,256]{2,0,1:T(8,128)(2,1)} %param.10), kind=kOutput, calls=%fused_computation.141 | convolution fusion | flops 33554432 | bytes 524288 | tf_op jit(solution)/shard_map/dot_general | solution.py:113
  27.7 0.7 mul.132
  28.4 0.7 mul.133
  29.1 0.7 slice_convert_fusion.2
  29.9 0.6 multiply_convert_fusion.5
  30.5 1.2 add_convert_fusion.1
  31.9 4.8 %collective-permute-start.2 = (bf16[528,256]{1,0:T(8,128)(2,1)S(1)}, bf16[528,256]{1,0:T(8,128)(2,1)S(1)}, u32[]{:S(2)}, u32[]{:S(2)}) collective-permute-start(bf16[528,256]{1,0:T(8,128)(2,1)S(1)} %pad_maximum_fusion.4), channel_id=1, source_target_pairs={{0,16},{4,20},{8,24},{12,28},{1,17},{5,21},{9,25},{13,29},{2,18},{... | collective-permute-start | bytes 811016 | tf_op jit(solution)/shard_map/ppermute | solution.py:49
  36.8 1.1 slice_convert_fusion
  37.9 2.3 %collective-permute-done.2 = bf16[528,256]{1,0:T(8,128)(2,1)S(1)} collective-permute-done((bf16[528,256]{1,0:T(8,128)(2,1)S(1)}, bf16[528,256]{1,0:T(8,128)(2,1)S(1)}, u32[]{:S(2)}, u32[]{:S(2)}) %collective-permute-start.2) | collective-permute-done | bytes 270368 | tf_op jit(solution)/shard_map/ppermute | solution.py:49
  40.2 0.8 add_convert_fusion
  41.2 0.7 collective-permute-start.3
  41.9 1.2 fusion.6
  43.2 0.9 collective-permute-start.7
  44.1 2.4 %collective-permute-done.3 = bf16[8,64,256]{2,1,0:T(8,128)(2,1)S(1)} collective-permute-done((bf16[8,64,256]{2,1,0:T(8,128)(2,1)S(1)}, bf16[8,64,256]{2,1,0:T(8,128)(2,1)S(1)}, u32[]{:S(2)}, u32[]{:S(2)}) %collective-permute-start.3) | collective-permute-done | bytes 262176 | tf_op jit(solution)/shard_map/ppermute | solution.py:41
  46.7 1.3 fusion.8
  48.0 2.5 %copy.57 = f32[256,1024]{1,0:T(8,128)} copy(f32[256,1024]{0,1:T(8,128)} %bitcast.220) | data formatting | bytes 2097152 | tf_op jit(solution)/shard_map/reshape | solution.py:124
  50.6 1.8 %multiply_reduce_fusion = f32[256]{0:T(256)S(1)} fusion(f32[256,1024]{1,0:T(8,128)} %copy.57, bf16[256,1024]{1,0:T(8,128)(2,1)} %param.8), kind=kLoop, calls=%fused_computation.59 | loop fusion | flops 2096896 | bytes 1573888 | tf_op jit(solution)/shard_map/reduce_sum | solution.py:126
  52.4 1.4 multiply_convert_fusion.4
  53.8 7.7 %collective-permute-start.4 = (bf16[256,1024]{1,0:T(8,128)(2,1)S(1)}, bf16[256,1024]{1,0:T(8,128)(2,1)S(1)}, u32[]{:S(2)}, u32[]{:S(2)}) collective-permute-start(bf16[256,1024]{1,0:T(8,128)(2,1)S(1)} %multiply_convert_fusion.4), channel_id=1, source_target_pairs={{0,1},{1,0},{2,3},{3,2},{4,5},{5,4},{6,7},{7,6},{8,9},{9,8},{10,11... | collective-permute-start | bytes 1572872 | tf_op jit(solution)/shard_map/ppermute | solution.py:52
  61.6 6.6 %collective-permute-start.9 = (bf16[256,1024]{1,0:T(8,128)(2,1)S(1)}, bf16[256,1024]{1,0:T(8,128)(2,1)S(1)}, u32[]{:S(2)}, u32[]{:S(2)}) collective-permute-start(bf16[256,1024]{1,0:T(8,128)(2,1)S(1)} %multiply_convert_fusion.4), channel_id=1, source_target_pairs={{0,8},{4,12},{8,16},{12,20},{16,24},{20,28},{24,0},{28,4},{1,9},{5... | collective-permute-start | bytes 1572872 | tf_op jit(solution)/shard_map/ppermute | solution.py:45
  69.0 14.2 %collective-permute-done.9 = bf16[256,1024]{1,0:T(8,128)(2,1)S(1)} collective-permute-done((bf16[256,1024]{1,0:T(8,128)(2,1)S(1)}, bf16[256,1024]{1,0:T(8,128)(2,1)S(1)}, u32[]{:S(2)}, u32[]{:S(2)}) %collective-permute-start.9) | collective-permute-done | bytes 524320 | tf_op jit(solution)/shard_map/ppermute | solution.py:45
  83.2 0.6 collective-permute-start.10
  85.2 1.9 %convolution_add_fusion.6 = f32[256,512]{1,0:T(8,128)S(1)} fusion(f32[256,512]{1,0:T(8,128)S(1)} %fusion.80, bf16[256,1024]{1,0:T(8,128)(2,1)S(1)} %collective-permute-done.4, bf16[1024,512]{1,0:T(8,128)(2,1)} %collective-permute-done.7), kind=kOutput, calls=%fused_computation.40 | convolution fusion | flops 268566528 | bytes 2621440 | tf_op jit(solution)/shard_map/dot_general | solution.py:138
  87.1 1.3 collective-permute-start.8
  88.4 1.7 %convolution_add_fusion.4 = f32[256,512]{1,0:T(8,128)S(1)} fusion(f32[256,512]{1,0:T(8,128)S(1)} %fusion.82, bf16[256,1024]{1,0:T(8,128)(2,1)S(1)} %collective-permute-done.10, bf16[1024,512]{1,0:T(8,128)(2,1)} %collective-permute-done.7), kind=kOutput, calls=%fused_computation.38 | convolution fusion | flops 268566528 | bytes 2621440 | tf_op jit(solution)/shard_map/dot_general | solution.py:138
  90.9 8.3 %collective-permute-done.13 = bf16[256,1024]{1,0:T(8,128)(2,1)S(1)} collective-permute-done((bf16[256,1024]{1,0:T(8,128)(2,1)S(1)}, bf16[256,1024]{1,0:T(8,128)(2,1)S(1)}, u32[]{:S(2)}, u32[]{:S(2)}) %collective-permute-start.13) | collective-permute-done | bytes 524320 | tf_op jit(solution)/shard_map/ppermute | solution.py:45
  99.2 0.8 collective-permute-start.14
  100.9 0.7 collective-permute-done.14
  101.5 1.7 %convolution_add_fusion.2 = f32[256,512]{1,0:T(8,128)S(1)} fusion(f32[256,512]{1,0:T(8,128)S(1)} %fusion.84, bf16[256,1024]{1,0:T(8,128)(2,1)S(1)} %collective-permute-done.14, bf16[1024,512]{1,0:T(8,128)(2,1)} %collective-permute-done.7), kind=kOutput, calls=%fused_computation.36 | convolution fusion | flops 268566528 | bytes 2621440 | tf_op jit(solution)/shard_map/dot_general | solution.py:138
  103.7 1.3 collective-permute-start.15
  105.0 10.4 %collective-permute-done.17 = bf16[256,1024]{1,0:T(8,128)(2,1)S(1)} collective-permute-done((bf16[256,1024]{1,0:T(8,128)(2,1)S(1)}, bf16[256,1024]{1,0:T(8,128)(2,1)S(1)}, u32[]{:S(2)}, u32[]{:S(2)}) %collective-permute-start.17) | collective-permute-done | bytes 524320 | tf_op jit(solution)/shard_map/ppermute | solution.py:45
  115.3 0.8 collective-permute-start.18
  117.0 0.7 collective-permute-done.18
  117.7 1.7 %convolution_add_fusion = f32[256,512]{1,0:T(8,128)S(1)} fusion(f32[256,512]{1,0:T(8,128)S(1)} %fusion.86, bf16[256,1024]{1,0:T(8,128)(2,1)S(1)} %collective-permute-done.18, bf16[1024,512]{1,0:T(8,128)(2,1)} %collective-permute-done.7), kind=kOutput, calls=%fused_computation.34 | convolution fusion | flops 268566528 | bytes 2621440 | tf_op jit(solution)/shard_map/dot_general | solution.py:138
  119.9 1.3 collective-permute-start.19
  121.5 6.0 %collective-permute-done.19 = bf16[2,128,512]{2,1,0:T(8,128)(2,1)S(1)} collective-permute-done((bf16[2,128,512]{2,1,0:T(8,128)(2,1)S(1)}, bf16[2,128,512]{2,1,0:T(8,128)(2,1)S(1)}, u32[]{:S(2)}, u32[]{:S(2)}) %collective-permute-start.19) | collective-permute-done | bytes 262176 | tf_op jit(solution)/shard_map/ppermute | solution.py:56
  127.7 1.0 fusion.53
  129.1 14.2 %collective-permute-done.16 = bf16[2,128,512]{2,1,0:T(8,128)(2,1)S(1)} collective-permute-done((bf16[2,128,512]{2,1,0:T(8,128)(2,1)S(1)}, bf16[2,128,512]{2,1,0:T(8,128)(2,1)S(1)}, u32[]{:S(2)}, u32[]{:S(2)}) %collective-permute-start.16) | collective-permute-done | bytes 262176 | tf_op jit(solution)/shard_map/ppermute | solution.py:45
  143.5 1.7 %collective-permute-start.21 = (bf16[2,128,512]{2,1,0:T(8,128)(2,1)S(1)}, bf16[2,128,512]{2,1,0:T(8,128)(2,1)S(1)}, u32[]{:S(2)}, u32[]{:S(2)}) collective-permute-start(bf16[2,128,512]{2,1,0:T(8,128)(2,1)S(1)} %get-tuple-element.20), channel_id=1, source_target_pairs={{0,1},{1,2},{2,3},{3,0},{4,5},{5,6},{6,7},{7,4},{8,9},{9,10},{10,1... | collective-permute-start | bytes 786440 | tf_op jit(solution)/shard_map/ppermute | solution.py:59
  145.2 1.2 collective-permute-start.22
  146.4 4.3 %collective-permute-done.21 = bf16[2,128,512]{2,1,0:T(8,128)(2,1)S(1)} collective-permute-done((bf16[2,128,512]{2,1,0:T(8,128)(2,1)S(1)}, bf16[2,128,512]{2,1,0:T(8,128)(2,1)S(1)}, u32[]{:S(2)}, u32[]{:S(2)}) %collective-permute-start.21) | collective-permute-done | bytes 262176 | tf_op jit(solution)/shard_map/ppermute | solution.py:59
  150.7 7.3 %collective-permute-done.22 = bf16[2,128,512]{2,1,0:T(8,128)(2,1)S(1)} collective-permute-done((bf16[2,128,512]{2,1,0:T(8,128)(2,1)S(1)}, bf16[2,128,512]{2,1,0:T(8,128)(2,1)S(1)}, u32[]{:S(2)}, u32[]{:S(2)}) %collective-permute-start.22) | collective-permute-done | bytes 262176 | tf_op jit(solution)/shard_map/ppermute | solution.py:59
  158.0 0.6 collective-permute-done.23
  159.2 1.1 copy.66
  160.2 1.6 reshape.212
  (108 shorter events, 10.8 us)
Async XLA Ops:
  0.0 4.6 %copy-start = (bf16[256,1,256]{2,0,1:T(8,128)(2,1)S(1)}, bf16[256,1,256]{2,0,1:T(8,128)(2,1)}, u32[]{:S(2)}) copy-start(bf16[256,1,256]{2,0,1:T(8,128)(2,1)} %param.9) | copy-start | bytes 393220
  4.5 0.9 copy-start.7
  6.4 8.4 %collective-permute-start = (bf16[528,256]{1,0:T(8,128)(2,1)}, bf16[528,256]{1,0:T(8,128)(2,1)S(1)}, u32[]{:S(2)}, u32[]{:S(2)}) collective-permute-start(bf16[528,256]{1,0:T(8,128)(2,1)} %get-tuple-element.25), channel_id=1, source_target_pairs={{0,4},{4,0},{8,12},{12,8},{16,20},{20,16},{24,28},{28,24},{1,5},{5... | collective-permute-start | bytes 811016 | tf_op jit(solution)/shard_map/ppermute | solution.py:41
  11.8 31.3 %collective-permute-start.5 = (bf16[1024,512]{1,0:T(8,128)(2,1)}, bf16[1024,512]{1,0:T(8,128)(2,1)S(1)}, u32[]{:S(2)}, u32[]{:S(2)}) collective-permute-start(bf16[1024,512]{1,0:T(8,128)(2,1)} %get-tuple-element.7), channel_id=1, source_target_pairs={{0,1},{1,0},{2,3},{3,2},{4,5},{5,4},{6,7},{7,6},{8,9},{9,8},{10,11... | collective-permute-start | bytes 3145736 | tf_op jit(solution)/shard_map/ppermute | solution.py:52
  12.8 55.8 %collective-permute-start.6 = (bf16[1024,512]{1,0:T(8,128)(2,1)S(1)}, bf16[1024,512]{1,0:T(8,128)(2,1)S(1)}, u32[]{:S(2)}, u32[]{:S(2)}) collective-permute-start(bf16[1024,512]{1,0:T(8,128)(2,1)S(1)} %get-tuple-element.8), channel_id=1, source_target_pairs={{0,4},{4,0},{8,12},{12,8},{16,20},{20,16},{24,28},{28,24},{1,5},{5... | collective-permute-start | bytes 3145736 | tf_op jit(solution)/shard_map/ppermute | solution.py:41
  14.8 0.7 copy-start.10
  16.7 0.7 copy-start.6
  16.9 1.7 %copy-start.15 = (f32[8]{0:T(128)}, f32[8]{0:T(128)S(1)}, u32[]{:S(2)}) copy-start(f32[8]{0:T(128)S(1)} %fusion.71) | copy-start | bytes 100
  18.1 0.5 copy-start.16
  21.4 7.7 %collective-permute-start.1 = (bf16[528,256]{1,0:T(8,128)(2,1)}, bf16[528,256]{1,0:T(8,128)(2,1)}, u32[]{:S(2)}, u32[]{:S(2)}) collective-permute-start(bf16[528,256]{1,0:T(8,128)(2,1)} %pad_maximum_fusion.3), channel_id=1, source_target_pairs={{0,8},{4,12},{8,16},{12,20},{16,24},{20,28},{1,9},{5,13},{9,17},{1... | collective-permute-start | bytes 811016 | tf_op jit(solution)/shard_map/ppermute | solution.py:49
  31.9 8.2 %collective-permute-start.2 = (bf16[528,256]{1,0:T(8,128)(2,1)S(1)}, bf16[528,256]{1,0:T(8,128)(2,1)S(1)}, u32[]{:S(2)}, u32[]{:S(2)}) collective-permute-start(bf16[528,256]{1,0:T(8,128)(2,1)S(1)} %pad_maximum_fusion.4), channel_id=1, source_target_pairs={{0,16},{4,20},{8,24},{12,28},{1,17},{5,21},{9,25},{13,29},{2,18},{... | collective-permute-start | bytes 811016 | tf_op jit(solution)/shard_map/ppermute | solution.py:49
  36.8 5.1 %copy-start.8 = (bf16[256,1024]{0,1:T(8,128)(2,1)S(1)}, bf16[256,1024]{0,1:T(8,128)(2,1)}, u32[]{:S(2)}) copy-start(bf16[256,1024]{0,1:T(8,128)(2,1)} %copy-done.7) | copy-start | bytes 1572868
  36.8 5.1 %copy-start.11 = (f32[256,256]{1,0:T(8,128)S(1)}, f32[256,256]{1,0:T(8,128)}, u32[]{:S(2)}) copy-start(f32[256,256]{1,0:T(8,128)} %fusion.67) | copy-start | bytes 786436
  36.8 5.1 %copy-start.13 = (pred[256,256]{1,0:T(8,128)(4,1)S(1)}, pred[256,256]{1,0:T(8,128)(4,1)}, u32[]{:S(2)}) copy-start(pred[256,256]{1,0:T(8,128)(4,1)} %iota_compare_fusion) | copy-start | bytes 196612
  36.8 5.1 %copy-start.14 = (f32[16,256]{1,0:T(8,128)S(1)}, f32[16,256]{1,0:T(8,128)}, u32[]{:S(2)}) copy-start(f32[16,256]{1,0:T(8,128)} %get-tuple-element.36) | copy-start | bytes 49156
  41.2 5.3 %collective-permute-start.3 = (bf16[8,64,256]{2,1,0:T(8,128)(2,1)S(1)}, bf16[8,64,256]{2,1,0:T(8,128)(2,1)S(1)}, u32[]{:S(2)}, u32[]{:S(2)}) collective-permute-start(bf16[8,64,256]{2,1,0:T(8,128)(2,1)S(1)} %get-tuple-element.29), channel_id=1, source_target_pairs={{0,4},{4,0},{8,12},{12,8},{16,20},{20,16},{24,28},{28,24},{1,5},{5... | collective-permute-start | bytes 786440 | tf_op jit(solution)/shard_map/ppermute | solution.py:41
  41.9 4.8 %copy-start.9 = (bf16[256,1,256]{2,0,1:T(8,128)(2,1)S(1)}, bf16[256,1,256]{2,0,1:T(8,128)(2,1)}, u32[]{:S(2)}) copy-start(bf16[256,1,256]{2,0,1:T(8,128)(2,1)} %param.10) | copy-start | bytes 393220
  41.9 4.8 %copy-start.12 = (f32[256,16]{0,1:T(8,128)S(1)}, f32[256,16]{0,1:T(8,128)}, u32[]{:S(2)}) copy-start(f32[256,16]{0,1:T(8,128)} %get-tuple-element.33) | copy-start | bytes 49156
  43.2 42.0 %collective-permute-start.7 = (bf16[1024,512]{1,0:T(8,128)(2,1)S(1)}, bf16[1024,512]{1,0:T(8,128)(2,1)}, u32[]{:S(2)}, u32[]{:S(2)}) collective-permute-start(bf16[1024,512]{1,0:T(8,128)(2,1)S(1)} %collective-permute-done.5), channel_id=1, source_target_pairs={{0,4},{4,0},{8,12},{12,8},{16,20},{20,16},{24,28},{28,24},{1,5},{5... | collective-permute-start | bytes 3145736 | tf_op jit(solution)/shard_map/ppermute | solution.py:41
  48.0 4.4 %copy-start.17 = (f32[1024]{0:T(1024)S(1)}, f32[1024]{0:T(1024)}, u32[]{:S(2)}) copy-start(f32[1024]{0:T(1024)} %param.12) | copy-start | bytes 12292
  50.6 1.9 %copy-start.1 = (f32[256,1024]{1,0:T(8,128)S(1)}, f32[256,1024]{1,0:T(8,128)}, u32[]{:S(2)}) copy-start(f32[256,1024]{1,0:T(8,128)} %copy.57) | copy-start | bytes 3145732
  53.8 30.9 %collective-permute-start.4 = (bf16[256,1024]{1,0:T(8,128)(2,1)S(1)}, bf16[256,1024]{1,0:T(8,128)(2,1)S(1)}, u32[]{:S(2)}, u32[]{:S(2)}) collective-permute-start(bf16[256,1024]{1,0:T(8,128)(2,1)S(1)} %multiply_convert_fusion.4), channel_id=1, source_target_pairs={{0,1},{1,0},{2,3},{3,2},{4,5},{5,4},{6,7},{7,6},{8,9},{9,8},{10,11... | collective-permute-start | bytes 1572872 | tf_op jit(solution)/shard_map/ppermute | solution.py:52
  61.6 21.6 %collective-permute-start.9 = (bf16[256,1024]{1,0:T(8,128)(2,1)S(1)}, bf16[256,1024]{1,0:T(8,128)(2,1)S(1)}, u32[]{:S(2)}, u32[]{:S(2)}) collective-permute-start(bf16[256,1024]{1,0:T(8,128)(2,1)S(1)} %multiply_convert_fusion.4), channel_id=1, source_target_pairs={{0,8},{4,12},{8,16},{12,20},{16,24},{20,28},{24,0},{28,4},{1,9},{5... | collective-permute-start | bytes 1572872 | tf_op jit(solution)/shard_map/ppermute | solution.py:45
  83.2 5.2 %collective-permute-start.10 = (bf16[256,1024]{1,0:T(8,128)(2,1)S(1)}, bf16[256,1024]{1,0:T(8,128)(2,1)S(1)}, u32[]{:S(2)}, u32[]{:S(2)}) collective-permute-start(bf16[256,1024]{1,0:T(8,128)(2,1)S(1)} %collective-permute-done.9), channel_id=1, source_target_pairs={{0,1},{1,0},{2,3},{3,2},{4,5},{5,4},{6,7},{7,6},{8,9},{9,8},{10,11... | collective-permute-start | bytes 1572872 | tf_op jit(solution)/shard_map/ppermute | solution.py:52
  83.9 15.4 %collective-permute-start.13 = (bf16[256,1024]{1,0:T(8,128)(2,1)S(1)}, bf16[256,1024]{1,0:T(8,128)(2,1)S(1)}, u32[]{:S(2)}, u32[]{:S(2)}) collective-permute-start(bf16[256,1024]{1,0:T(8,128)(2,1)S(1)} %collective-permute-done.9), channel_id=1, source_target_pairs={{0,8},{4,12},{8,16},{12,20},{16,24},{20,28},{24,0},{28,4},{1,9},{5... | collective-permute-start | bytes 1572872 | tf_op jit(solution)/shard_map/ppermute | solution.py:45
  85.2 4.9 %copy-start.2 = (f32[256,512]{1,0:T(8,128)}, f32[256,512]{1,0:T(8,128)S(1)}, u32[]{:S(2)}) copy-start(f32[256,512]{1,0:T(8,128)S(1)} %convolution_add_fusion.7) | copy-start | bytes 1572868
  87.1 3.5 %copy-start.4 = (f32[256,512]{1,0:T(8,128)}, f32[256,512]{1,0:T(8,128)S(1)}, u32[]{:S(2)}) copy-start(f32[256,512]{1,0:T(8,128)S(1)} %convolution_add_fusion.6) | copy-start | bytes 1572868
  87.1 40.6 %collective-permute-start.8 = (bf16[2,128,512]{2,1,0:T(8,128)(2,1)S(1)}, bf16[2,128,512]{2,1,0:T(8,128)(2,1)}, u32[]{:S(2)}, u32[]{:S(2)}) collective-permute-start(bf16[2,128,512]{2,1,0:T(8,128)(2,1)S(1)} %fusion.54), channel_id=1, source_target_pairs={{0,2},{1,3},{2,0},{3,1},{4,6},{5,7},{6,4},{7,5},{8,10},{9,11},{10,... | collective-permute-start | bytes 786440 | tf_op jit(solution)/shard_map/ppermute | solution.py:56
  90.6 30.5 %collective-permute-start.11 = (bf16[2,128,512]{2,1,0:T(8,128)(2,1)S(1)}, bf16[2,128,512]{2,1,0:T(8,128)(2,1)S(1)}, u32[]{:S(2)}, u32[]{:S(2)}) collective-permute-start(bf16[2,128,512]{2,1,0:T(8,128)(2,1)S(1)} %fusion.55), channel_id=1, source_target_pairs={{0,2},{1,3},{2,0},{3,1},{4,6},{5,7},{6,4},{7,5},{8,10},{9,11},{10,... | collective-permute-start | bytes 786440 | tf_op jit(solution)/shard_map/ppermute | solution.py:56
  99.2 2.3 %collective-permute-start.14 = (bf16[256,1024]{1,0:T(8,128)(2,1)S(1)}, bf16[256,1024]{1,0:T(8,128)(2,1)S(1)}, u32[]{:S(2)}, u32[]{:S(2)}) collective-permute-start(bf16[256,1024]{1,0:T(8,128)(2,1)S(1)} %collective-permute-done.13), channel_id=1, source_target_pairs={{0,1},{1,0},{2,3},{3,2},{4,5},{5,4},{6,7},{7,6},{8,9},{9,8},{10,11... | collective-permute-start | bytes 1572872 | tf_op jit(solution)/shard_map/ppermute | solution.py:52
  100.0 15.4 %collective-permute-start.17 = (bf16[256,1024]{1,0:T(8,128)(2,1)S(1)}, bf16[256,1024]{1,0:T(8,128)(2,1)S(1)}, u32[]{:S(2)}, u32[]{:S(2)}) collective-permute-start(bf16[256,1024]{1,0:T(8,128)(2,1)S(1)} %collective-permute-done.13), channel_id=1, source_target_pairs={{0,8},{4,12},{8,16},{12,20},{16,24},{20,28},{24,0},{28,4},{1,9},{5... | collective-permute-start | bytes 1572872 | tf_op jit(solution)/shard_map/ppermute | solution.py:45
  103.7 17.6 %collective-permute-start.15 = (bf16[2,128,512]{2,1,0:T(8,128)(2,1)S(1)}, bf16[2,128,512]{2,1,0:T(8,128)(2,1)S(1)}, u32[]{:S(2)}, u32[]{:S(2)}) collective-permute-start(bf16[2,128,512]{2,1,0:T(8,128)(2,1)S(1)} %fusion.56), channel_id=1, source_target_pairs={{0,2},{1,3},{2,0},{3,1},{4,6},{5,7},{6,4},{7,5},{8,10},{9,11},{10,... | collective-permute-start | bytes 786440 | tf_op jit(solution)/shard_map/ppermute | solution.py:56
  115.3 2.3 %collective-permute-start.18 = (bf16[256,1024]{1,0:T(8,128)(2,1)S(1)}, bf16[256,1024]{1,0:T(8,128)(2,1)S(1)}, u32[]{:S(2)}, u32[]{:S(2)}) collective-permute-start(bf16[256,1024]{1,0:T(8,128)(2,1)S(1)} %collective-permute-done.17), channel_id=1, source_target_pairs={{0,1},{1,0},{2,3},{3,2},{4,5},{5,4},{6,7},{7,6},{8,9},{9,8},{10,11... | collective-permute-start | bytes 1572872 | tf_op jit(solution)/shard_map/ppermute | solution.py:52
  119.8 7.9 %copy-start.3 = (f32[256,512]{1,0:T(8,128)S(1)}, f32[256,512]{1,0:T(8,128)}, u32[]{:S(2)}) copy-start(f32[256,512]{1,0:T(8,128)} %copy-done.2) | copy-start | bytes 1572868
  119.9 7.9 %copy-start.5 = (f32[256,512]{1,0:T(8,128)S(1)}, f32[256,512]{1,0:T(8,128)}, u32[]{:S(2)}) copy-start(f32[256,512]{1,0:T(8,128)} %copy-done.4) | copy-start | bytes 1572868
  119.9 7.6 %collective-permute-start.19 = (bf16[2,128,512]{2,1,0:T(8,128)(2,1)S(1)}, bf16[2,128,512]{2,1,0:T(8,128)(2,1)S(1)}, u32[]{:S(2)}, u32[]{:S(2)}) collective-permute-start(bf16[2,128,512]{2,1,0:T(8,128)(2,1)S(1)} %fusion.57), channel_id=1, source_target_pairs={{0,2},{1,3},{2,0},{3,1},{4,6},{5,7},{6,4},{7,5},{8,10},{9,11},{10,... | collective-permute-start | bytes 786440 | tf_op jit(solution)/shard_map/ppermute | solution.py:56
  121.2 7.8 %collective-permute-start.12 = (bf16[2,128,512]{2,1,0:T(8,128)(2,1)S(1)}, bf16[2,128,512]{2,1,0:T(8,128)(2,1)S(1)}, u32[]{:S(2)}, u32[]{:S(2)}) collective-permute-start(bf16[2,128,512]{2,1,0:T(8,128)(2,1)S(1)} %fusion.35), channel_id=1, source_target_pairs={{0,24},{4,28},{8,0},{12,4},{16,8},{20,12},{24,16},{28,20},{1,25},{... | collective-permute-start | bytes 786440 | tf_op jit(solution)/shard_map/ppermute | solution.py:45
  121.4 21.8 %collective-permute-start.16 = (bf16[2,128,512]{2,1,0:T(8,128)(2,1)S(1)}, bf16[2,128,512]{2,1,0:T(8,128)(2,1)S(1)}, u32[]{:S(2)}, u32[]{:S(2)}) collective-permute-start(bf16[2,128,512]{2,1,0:T(8,128)(2,1)S(1)} %fusion.29), channel_id=1, source_target_pairs={{0,16},{4,20},{8,24},{12,28},{16,0},{20,4},{24,8},{28,12},{1,17},{... | collective-permute-start | bytes 786440 | tf_op jit(solution)/shard_map/ppermute | solution.py:45
  127.5 15.7 %collective-permute-start.20 = (bf16[2,128,512]{2,1,0:T(8,128)(2,1)S(1)}, bf16[2,128,512]{2,1,0:T(8,128)(2,1)S(1)}, u32[]{:S(2)}, u32[]{:S(2)}) collective-permute-start(bf16[2,128,512]{2,1,0:T(8,128)(2,1)S(1)} %fusion.23), channel_id=1, source_target_pairs={{0,8},{4,12},{8,16},{12,20},{16,24},{20,28},{24,0},{28,4},{1,9},{5... | collective-permute-start | bytes 786440 | tf_op jit(solution)/shard_map/ppermute | solution.py:45
  143.5 7.2 %collective-permute-start.21 = (bf16[2,128,512]{2,1,0:T(8,128)(2,1)S(1)}, bf16[2,128,512]{2,1,0:T(8,128)(2,1)S(1)}, u32[]{:S(2)}, u32[]{:S(2)}) collective-permute-start(bf16[2,128,512]{2,1,0:T(8,128)(2,1)S(1)} %get-tuple-element.20), channel_id=1, source_target_pairs={{0,1},{1,2},{2,3},{3,0},{4,5},{5,6},{6,7},{7,4},{8,9},{9,10},{10,1... | collective-permute-start | bytes 786440 | tf_op jit(solution)/shard_map/ppermute | solution.py:59
  145.2 12.8 %collective-permute-start.22 = (bf16[2,128,512]{2,1,0:T(8,128)(2,1)S(1)}, bf16[2,128,512]{2,1,0:T(8,128)(2,1)S(1)}, u32[]{:S(2)}, u32[]{:S(2)}) collective-permute-start(bf16[2,128,512]{2,1,0:T(8,128)(2,1)S(1)} %get-tuple-element.19), channel_id=1, source_target_pairs={{0,2},{1,3},{2,0},{3,1},{4,6},{5,7},{6,4},{7,5},{8,10},{9,11},{10,... | collective-permute-start | bytes 786440 | tf_op jit(solution)/shard_map/ppermute | solution.py:59
  146.4 12.2 %collective-permute-start.23 = (bf16[2,128,512]{2,1,0:T(8,128)(2,1)S(1)}, bf16[2,128,512]{2,1,0:T(8,128)(2,1)S(1)}, u32[]{:S(2)}, u32[]{:S(2)}) collective-permute-start(bf16[2,128,512]{2,1,0:T(8,128)(2,1)S(1)} %get-tuple-element.18), channel_id=1, source_target_pairs={{0,3},{1,0},{2,1},{3,2},{4,7},{5,4},{6,5},{7,6},{8,11},{9,8},{10,9... | collective-permute-start | bytes 786440 | tf_op jit(solution)/shard_map/ppermute | solution.py:59

commit v2 on v0

v2 whole, which is shorter than its diff:
```python
import functools
import jax
import jax.numpy as jnp
from jax import lax
from jax.experimental import pallas as pl
from jax.experimental.pallas import tpu as pltpu
from jax.sharding import PartitionSpec as P

BF = jnp.bfloat16
F32 = jnp.float32
HIGH = lax.Precision.HIGHEST
TAIL = 16
CHUNKS = 2
MINE, OTHER, EARLY = (4, 4), (3, 5), 3


def call(kernel, out_shapes, args, scratch=(), traffic=1, resident=0):
    vmem = pl.BlockSpec(memory_space=pltpu.VMEM)
    any_ = pl.BlockSpec()
    smem = pl.BlockSpec(memory_space=pltpu.SMEM)
    outs = pl.pallas_call(
        kernel,
        out_shape=[jax.ShapeDtypeStruct(s, d) for s, d in out_shapes],
        in_specs=[smem] + [any_] * (len(args) - 1 - resident) + [vmem] * resident,
        out_specs=[any_] * len(out_shapes),
        scratch_shapes=list(scratch),
        compiler_params=pltpu.CompilerParams(vmem_limit_bytes=16 << 20),
        cost_estimate=pl.CostEstimate(flops=1, transcendentals=0, bytes_accessed=traffic),
    )(*args)
    return list(outs)


def triangle(rows):
    i = lax.broadcasted_iota(jnp.int32, (rows, rows), 0)
    j = lax.broadcasted_iota(jnp.int32, (rows, rows), 1)
    return i >= j


def spread(per_head, channels):
    heads = per_head.shape[1]
    h = lax.broadcasted_iota(jnp.int32, (heads, channels), 0)
    c = lax.broadcasted_iota(jnp.int32, (heads, channels), 1)
    pick = (c // (channels // heads) == h).astype(F32)
    return jnp.dot(per_head, pick, precision=HIGH, preferred_element_type=F32)


def write_message(ref, state, decay):
    n, w = state.shape
    ref[0:n, :] = state.astype(BF)
    high = decay.astype(BF).astype(F32)
    row = lax.broadcasted_iota(jnp.int32, (TAIL, w), 0)
    tail = jnp.where(row < TAIL // 2, high, decay - high)
    ref[n : n + TAIL, :] = tail.astype(BF)


def read_message(ref):
    n = ref.shape[0] - TAIL
    tail = ref[n : n + TAIL, :].astype(F32)
    return ref[0:n, :].astype(F32), tail[0:1] + tail[TAIL // 2 : TAIL // 2 + 1]


def state_kernel(r, me, x, b, logs, keep, *sends):
    rows, channels = x.shape
    tri = triangle(rows).astype(F32)
    cum = jnp.dot(tri, logs[...], precision=HIGH, preferred_element_type=F32)
    total = cum[rows - 1 : rows, :]
    weights = spread(jnp.exp(total - cum), channels)
    decay = spread(jnp.broadcast_to(jnp.exp(total), (8, total.shape[1])), channels)[0:1]
    scaled = (weights * x[...].astype(F32)).astype(BF)
    state = lax.dot_general(b[...], scaled, (((0,), (0,)), ((), ())), preferred_element_type=F32)
    w = channels // r
    for g in range(r):

        @pl.when(me[0] == g)
        def _():
            for j, ref in enumerate((keep,) + sends):
                at = (g + j) % r * w
                write_message(ref, state[:, at : at + w], decay[:, at : at + w])


def fold_kernel(r, me, *refs):
    got, (message, run, run_decay) = refs[:r], refs[r:]
    for g in range(r):

        @pl.when(me[0] == g)
        def _():
            total, decay = read_message(got[g])
            for i in range(1, r):
                s, d = read_message(got[(g - i) % r])
                total, decay = total * d + s, decay * d
            write_message(message, total, decay)
            run[...] = total
            run_decay[...] = jnp.broadcast_to(decay, run_decay.shape)


def step_kernel(first, me, got, before, before_decay, run, run_decay, message, o_before, o_before_decay, o_run, o_run_decay):
    s, d = read_message(got)
    if first:
        o_before[...], o_before_decay[...] = s, jnp.broadcast_to(d, o_before_decay.shape)
    else:
        o_before[...] = before[...] + before_decay[0:1] * s
        o_before_decay[...] = before_decay[...] * d
    total = run[...] + run_decay[0:1] * s
    decay = run_decay[0:1] * d
    write_message(message, total, decay)
    o_run[...] = total
    o_run_decay[...] = jnp.broadcast_to(decay, o_run_decay.shape)


def enter_kernel(r, me, got, before, before_decay, *refs):
    blocks, outs = refs[:r], refs[r:]
    s, _ = read_message(got)
    start = before[...] + before_decay[0:1] * s
    for g in range(r):

        @pl.when(me[0] == g)
        def _():
            now = start
            for i in range(r):
                outs[(i - g) % r][...] = now.astype(BF)
                if i + 1 < r:
                    q, d = read_message(blocks[(g - i) % r])
                    now = now * d + q


def within_kernel(me, x, z, b, c, logs, y, silu, grow):
    rows, channels = x.shape
    heads = logs.shape[1]
    width = channels // heads
    causal = triangle(rows)
    tri = causal.astype(F32)
    cum = jnp.dot(tri, logs[...], precision=HIGH, preferred_element_type=F32)
    cum_t = lax.dot_general(
        logs[...], tri, (((0,), (1,)), ((), ())), precision=HIGH, preferred_element_type=F32
    )
    scores = lax.dot_general(
        c[...], b[...], (((1,), (1,)), ((), ())), preferred_element_type=F32
    )
    scores = jnp.where(causal, scores, 0.0)
    for h in range(heads):
        diff = cum[:, h : h + 1] - cum_t[h : h + 1, :]
        mask = jnp.exp(jnp.where(causal, diff, 0.0))
        weighted = (mask * scores).astype(BF)
        at = slice(h * width, (h + 1) * width)
        y[:, at] = jnp.dot(weighted, x[:, at], preferred_element_type=F32)
    gate = z[...].astype(F32)
    silu[...] = gate / (1.0 + jnp.exp(-gate))
    grow[...] = spread(jnp.exp(cum), channels)


def hidden_kernel(r, me, c, y, silu, grow, gain, *refs):
    parts, outs, entering = refs[:r], refs[r:-1], refs[-1]
    w = entering.shape[1] // r
    for g in range(r):

        @pl.when(me[0] == g)
        def _():
            for j in range(r):
                at = (g - j) % r * w
                entering[:, at : at + w] = parts[j][...]

    rows = c.shape[0] // len(outs)
    for i, out in enumerate(outs):
        at = slice(i * rows, (i + 1) * rows)
        carried = jnp.dot(c[at, :], entering[...], preferred_element_type=F32)
        gated = (y[at, :] + grow[at, :] * carried) * silu[at, :]
        mean_sq = jnp.mean(gated * gated, axis=1, keepdims=True)
        out[...] = (gated * lax.rsqrt(mean_sq + 1e-05) * gain[...]).astype(BF)


def split_kernel(n_mine, core, w_out, *refs):
    width = refs[0].shape[1]
    for g in range(2):

        @pl.when(core[0] == g)
        def _():
            for parts, side in ((refs[:n_mine], g), (refs[n_mine:], 1 - g)):
                at = 0
                for ref in parts:
                    rows = ref.shape[0]
                    ref[...] = w_out[at : at + rows, side * width : (side + 1) * width]
                    at += rows


def product_kernel(r, n_y, chunks, me, *refs):
    rows = [jnp.concatenate([ref[...] for ref in refs[i * chunks : (i + 1) * chunks]]) for i in range(2)]
    weights, (mine, *sends) = refs[2 * chunks : -n_y], refs[-n_y:]
    per = len(weights) // r
    shares = [ref.shape[0] for ref in weights[:per]]
    half = rows[0].shape[0] // chunks
    part = half // n_y
    for p in range(r):
        term, side, at = None, 0, 0
        for ref, share in zip(weights[p * per : (p + 1) * per], shares):
            one = jnp.dot(
                rows[side][:, at : at + share], ref[...], preferred_element_type=F32
            )
            term = one if term is None else term + one
            at += share
            if at == rows[0].shape[1]:
                side, at = 1, 0
        for g in range(n_y):

            @pl.when(me[0] == g)
            def _():
                for i in range(chunks):
                    at = i * half + g * part
                    mine[i, p] = term[at : at + part]
                    for j, ref in enumerate(sends):
                        at = i * half + (g + j + 1) % n_y * part
                        ref[i, p] = term[at : at + part].astype(BF)


def sum_kernel(me, mine, *refs):
    gots, out = refs[:-1], refs[-1]
    total = mine[...]
    for got in gots:
        total = total + got[...].astype(F32)
    out[...] = total.astype(BF)


def turn_kernel(n, chunk, by, *refs):
    ins, outs = refs[:n], refs[n:]
    for g in range(n):

        @pl.when(by[0] == g)
        def _():
            for j in range(n):
                ref = ins[(g + j) % n]
                outs[j][...] = ref[chunk if ref.shape[0] > 1 else 0]


def gather_kernel(n, me, *refs):
    ins, out = refs[:-1], refs[-1]
    r, part, width = ins[0].shape
    for t, ref in enumerate(ins):
        i, j = t // n, t % n
        source = lax.rem(me[0] + n - j, n)
        row = i * (n // 2) * part + lax.div(source, 2) * part
        row = pl.multiple_of(row, part)
        for p in range(r):
            order = lax.rem(me[1] + r - p, r)
            column = pl.multiple_of((2 * order + lax.rem(source, 2)) * width, width)
            out[pl.ds(row, part), pl.ds(column, width)] = ref[p]


def body(x_in, z_gate, b_proj, c_proj, log_decay, norm_gain, w_out):
    rows, channels = x_in.shape
    n_seq, n_head = lax.axis_size("seq"), lax.axis_size("head")
    r = n_seq // n_head
    n_y = n_head // 2
    me_seq, me_head = lax.axis_index("seq"), lax.axis_index("head")
    me_h, me_b = me_seq // r, me_seq % r
    me = me_b.reshape(1)

    def rot_b(v, j):
        pairs = [(h * r + b, h * r + (b + j) % r) for h in range(n_head) for b in range(r)]
        return lax.ppermute(v, "seq", pairs)

    def rot_h(v, k):
        pairs = [(h * r + b, (h + k) % n_head * r + b) for h in range(n_head) for b in range(r)]
        return lax.ppermute(v, "seq", pairs)

    def shift_h(v, k):
        pairs = [(h * r + b, (h + k) * r + b) for h in range(n_head - k) for b in range(r)]
        return lax.ppermute(v, "seq", pairs)

    def swap_core(v):
        return lax.ppermute(v, "head", [(i, i ^ 1) for i in range(n_head)])

    def rot_y(v, j):
        pairs = [(y * 2 + c, (y + j) % n_y * 2 + c) for y in range(n_y) for c in range(2)]
        return lax.ppermute(v, "head", pairs)

    def rot_head(v, j):
        return lax.ppermute(v, "head", [(i, (i + j) % n_head) for i in range(n_head)])

    pick = lambda v, i: lax.dynamic_index_in_dim(v, i, 0, keepdims=False)
    after = lambda v, *first: lax.optimization_barrier((v,) + first)[0]
    core = (me_head % 2).reshape(1)
    b_local = b_proj[:, 0, :]
    c_local = c_proj[:, 0, :]
    n = b_local.shape[1]
    w = channels // r
    message = ((n + TAIL, w), BF)
    full, row = ((n, w), F32), ((8, w), F32)

    sends = call(functools.partial(state_kernel, r), [message] * r, (me, x_in, b_local, log_decay))
    got = [sends[0]] + [rot_b(sends[j], j) for j in range(1, r)]
    depth, width = w_out.shape[0], w_out.shape[1] // 2
    mine_rows, other_rows = [[depth * i // 8 for i in cut] for cut in (MINE, OTHER)]
    split = call(
        functools.partial(split_kernel, len(mine_rows)),
        [((d, width), BF) for d in mine_rows + other_rows],
        (core, after(w_out, *sends)),
        traffic=4 * w_out.size * w_out.dtype.itemsize,
    )
    w_own = split[: len(mine_rows)] + [swap_core(v) for v in split[len(mine_rows) :]]
    w_parts = [w_own]
    for j in range(1, r):
        w_parts.append([rot_b(v, j) for v in w_own[:EARLY]])
    early = [v for group in w_parts[1:] for v in group]
    out, run, run_decay = call(functools.partial(fold_kernel, r), [message, full, row], (me, *got))
    before, before_decay = run, run_decay
    out = after(out, *split)
    k = 1
    while 2 * k < n_head:
        out, before, before_decay, run, run_decay = call(
            functools.partial(step_kernel, k == 1),
            [message, full, row, full, row],
            (me, shift_h(out, k), before, before_decay, run, run_decay),
        )
        k *= 2
        out = after(out, *[group[0] for group in w_parts[1:]])
    entering = call(
        functools.partial(enter_kernel, r),
        [((n, w), BF)] * r,
        (me, shift_h(out, k), before, before_decay, *got),
    )
    parts = [entering[0]] + [rot_b(after(entering[j], *early), j) for j in range(1, r)]
    y, silu, grow = call(
        within_kernel,
        [((rows, channels), F32)] * 3,
        (me, x_in, after(z_gate, *entering), b_local, c_local, log_decay),
    )
    part_rows = rows // CHUNKS
    hidden = call(
        functools.partial(hidden_kernel, r),
        [((part_rows, channels), BF)] * CHUNKS,
        (me, c_local, y, silu, grow, norm_gain.reshape(1, channels), *parts),
        scratch=[pltpu.VMEM((n, channels), BF)],
    )

    for j in range(1, r):
        w_parts[j].extend(rot_b(after(v, y), j) for v in w_own[EARLY:])
    weights = [v for group in w_parts for v in group]

    piece = part_rows // n_y
    me_y = (me_head // 2).reshape(1)
    steps = [(k, list(range(CHUNKS))) for k in range(n_head - 1)]
    steps += [(n_head - 1, [i]) for i in range(CHUNKS)]
    hidden = list(hidden)
    home, sums, back, outs = [[] for _ in range(CHUNKS)], [], [], []
    for t, (k, chunks) in enumerate(steps):
        now = [hidden[i] for i in chunks]
        if k + 1 < n_head:
            hidden = [rot_h(after(v, *outs[: max(t - 1, 0)]), 1) for v in hidden]
        other = [swap_core(v) for v in now]
        if t > 1:
            other[0] = after(other[0], sums[t - 2], *back[: max(t - 3, 0)])
        shape = (len(chunks), r, piece, width)
        mine, *send = call(
            functools.partial(product_kernel, r, n_y, len(chunks)),
            [(shape, F32)] + [(shape, BF)] * (n_y - 1),
            (me_y, *now, *other, *weights),
            resident=len(weights),
        )
        outs.append(mine)
        gots = [rot_y(v, j + 1) for j, v in enumerate(send)]
        (last,) = call(sum_kernel, [(shape, BF)], (me_y, mine, *gots))
        sums.append(last)
        if k:
            last = rot_h(last, -k)
            back.append(last)
        for i in chunks:
            home[i].append(last)
    by = lax.rem(me_head + n_head - me_h, n_head).reshape(1)
    pieces = []
    for i in range(CHUNKS):
        ready = call(
            functools.partial(turn_kernel, n_head, i),
            [((r, piece, width), BF)] * n_head,
            (by, *home[i]),
        )
        pieces.append(ready[0])
        pieces.extend(rot_head(ready[j], j) for j in range(1, n_head))
    (out,) = call(
        functools.partial(gather_kernel, n_head),
        [((rows, r * 2 * width), BF)],
        (jnp.stack([me_head, me_b]), *pieces),
    )
    return out


def solution(mesh):
    placed = (
        P("seq", "head"),
        P("seq", "head"),
        P("seq", "head", None),
        P("seq", "head", None),
        P("seq", "head"),
        P("head"),
        P("head", "seq"),
    )
    return jax.shard_map(
        body, mesh=mesh, in_specs=placed, out_specs=P("seq", "head"), check_vma=False
    )
```

time: 378 us -> 143 us (0.38)
  waiting for transfers between devices: 314 us -> 53.2 us
  starting transfers between devices: 0.08 us -> 48.6 us
  Pallas kernels: 0 us -> 22.9 us
  blocking collectives: 17.9 us -> 0 us
  matrix products: 15.5 us -> 0 us
  local copies, waits for them, and re-layouts: 2.7 us -> 17.2 us
  other arithmetic: 13.1 us -> 0.07 us
  between operations: 13.2 us -> 0.33 us
    all_gather x2 -> x0, waiting for transfers between devices: 270 us -> none  [the longest x1 216 us: body(): lax.all_gather(w_out, 'seq', axis=1, tiled=True)]
    ppermute x0 -> x39, waiting for transfers between devices: none -> 53.2 us  [the longest x6 18.6 us: rot_b(): return lax.ppermute(v, 'seq', pairs)]
    ppermute x0 -> x39, starting transfers between devices: none -> 48.6 us  [the longest x10 16.7 us: swap_core(): return lax.ppermute(v, 'head', [(i, i ^ 1) for i in range(n_head)])]
    reduce_scatter x1 -> x0, waiting for transfers between devices: 43.3 us -> none  [body(): lax.psum_scatter(partial_terms.astype(jnp.bfloat16), 'head', scatter_dime...]
    pallas_call x0 -> x20, Pallas kernels: none -> 22.9 us  [call(): pl.pallas_call(kernel, out_shape=[jax.ShapeDtypeStruct(s, d) for s, d in...]
    all_gather x1 -> x0, blocking collectives: 17.9 us -> none  [carried_in(): lax.all_gather(part.astype(kind), axis)]
    unnamed x8 -> x57, local copies, waits for them, and re-layouts: 1.26 us -> 17.2 us
    dot_general x5 -> x0, matrix products: 15.5 us -> none  [the longest x1 12.6 us: body(): jnp.dot(hidden, lax.all_gather(w_out, 'seq', axis=1, tiled=True), preferr...]
  transfers between devices with their start and end apart: 3 -> 39, of which waited for: 3 -> 18; matrix products, arithmetic and copies ran while one was open for 4% -> 0% of each run, Pallas kernels for 0% -> 13%
where the time goes in v2:
time: 143 us; the launch traced here: 142 us
  waiting for transfers between devices  53.2 us (37%)
  starting transfers between devices  48.6 us (34%)
  Pallas kernels  22.9 us (16%)
  local copies, waits for them, and re-layouts  17.2 us (12%)
    pallas_call x20, Pallas kernels, call(): pl.pallas_call(kernel, out_shape=[jax.ShapeDtypeStruct(s, d) for s, d in...  22.9 us
    ppermute x6, waiting for transfers between devices, rot_b(): return lax.ppermute(v, 'seq', pairs)  18.6 us
    unnamed x57, local copies, waits for them, and re-layouts  17.2 us
    ppermute x10, starting transfers between devices, swap_core(): return lax.ppermute(v, 'head', [(i, i ^ 1) for i in range(n_head)])  16.7 us
    ppermute x10, waiting for transfers between devices, rot_h(): return lax.ppermute(v, 'seq', pairs)  16.5 us
    ppermute x10, starting transfers between devices, rot_h(): return lax.ppermute(v, 'seq', pairs)  9.79 us
    ppermute x6, waiting for transfers between devices, rot_head(): lax.ppermute(v, 'head', [(i, (i + j) % n_head) for i in range(n_head)])  8.03 us
    ppermute x2, starting transfers between devices, shift_h(): return lax.ppermute(v, 'seq', pairs)  7.3 us
  transfers between devices with their start and end apart: 39, of which 18 were waited for; matrix products, arithmetic and copies ran while one was open for 0% of the time, Pallas kernels for 13%

profile of v2, /device:TPU:1, one launch (start us, length us, event | category | flops | bytes accessed | tf_op | source)
XLA Modules:
  0.0 142.3 jit_solution(10013710253744714618)
XLA Ops:
  0.0 0.8 copy.8.logs
  0.8 1.0 copy-done.9
  1.9 0.9 copy-done.19
  2.8 2.9 %shard_map.73 = (bf16[272,512]{1,0:T(8,128)(2,1)S(1)}, bf16[272,512]{1,0:T(8,128)(2,1)}) custom-call(s32[1]{0:T(128)} %bitcast.1.me, bf16[256,1024]{1,0:T(8,128)(2,1)S(1)} %copy-done.9, bf16[256,256]{1,0:T(8,128)(2,1)S(1)} %bitcast.10, f32[256,16]{1,0:T(8,128)S(1)} %copy.8.logs), custom_call_target="tpu_custom_call" | custom-call | flops 1 | bytes 1 | tf_op jit(solution)/shard_map/pallas_call | solution.py:21
  5.7 2.0 %collective-permute-start = (bf16[272,512]{1,0:T(8,128)(2,1)}, bf16[272,512]{1,0:T(8,128)(2,1)S(1)}, u32[]{:S(2)}, u32[]{:S(2)}) collective-permute-start(bf16[272,512]{1,0:T(8,128)(2,1)} %get-tuple-element.54), channel_id=1, source_target_pairs={{0,4},{4,0},{8,12},{12,8},{16,20},{20,16},{24,28},{28,24},{1,5},{5... | collective-permute-start | bytes 835592 | tf_op jit(solution)/shard_map/ppermute | solution.py:258
  7.7 1.6 %copy-done.8 = bf16[1024,1024]{1,0:T(8,128)(2,1)S(1)} copy-done((bf16[1024,1024]{1,0:T(8,128)(2,1)S(1)}, bf16[1024,1024]{1,0:T(8,128)(2,1)}, u32[]{:S(2)}) %copy-start.8) | copy-done | bytes 2097176
  9.7 1.0 collective-permute-start.5
  10.7 3.6 %collective-permute-done.refs_1_ = bf16[272,512]{1,0:T(8,128)(2,1)S(1)} collective-permute-done((bf16[272,512]{1,0:T(8,128)(2,1)}, bf16[272,512]{1,0:T(8,128)(2,1)S(1)}, u32[]{:S(2)}, u32[]{:S(2)}) %collective-permute-start) | collective-permute-done | bytes 278560 | tf_op jit(solution)/shard_map/ppermute | solution.py:258
  15.0 3.1 %collective-permute-start.1 = (bf16[272,512]{1,0:T(8,128)(2,1)S(1)}, bf16[272,512]{1,0:T(8,128)(2,1)S(1)}, u32[]{:S(2)}, u32[]{:S(2)}) collective-permute-start(bf16[272,512]{1,0:T(8,128)(2,1)S(1)} %get-tuple-element.61), channel_id=1, source_target_pairs={{0,8},{4,12},{8,16},{12,20},{16,24},{20,28},{1,9},{5,13},{9,17},{1... | collective-permute-start | bytes 835592 | tf_op jit(solution)/shard_map/ppermute | solution.py:266
  18.2 1.3 collective-permute-start.4
  19.7 1.9 %collective-permute-done.1.got = bf16[272,512]{1,0:T(8,128)(2,1)S(1)} collective-permute-done((bf16[272,512]{1,0:T(8,128)(2,1)S(1)}, bf16[272,512]{1,0:T(8,128)(2,1)S(1)}, u32[]{:S(2)}, u32[]{:S(2)}) %collective-permute-start.1) | collective-permute-done | bytes 278560 | tf_op jit(solution)/shard_map/ppermute | solution.py:266
  21.6 0.9 shard_map.76
  22.5 3.0 %collective-permute-done.2.refs_8_.refs_6_ = bf16[512,512]{1,0:T(8,128)(2,1)S(1)} collective-permute-done((bf16[512,512]{1,0:T(8,128)(2,1)S(1)}, bf16[512,512]{1,0:T(8,128)(2,1)S(1)}, u32[]{:S(2)}, u32[]{:S(2)}) %collective-permute-start.2) | collective-permute-done | bytes 524320 | tf_op jit(solution)/shard_map/ppermute | solution.py:258
  25.5 4.2 %collective-permute-start.3 = (bf16[272,512]{1,0:T(8,128)(2,1)S(1)}, bf16[272,512]{1,0:T(8,128)(2,1)S(1)}, u32[]{:S(2)}, u32[]{:S(2)}) collective-permute-start(bf16[272,512]{1,0:T(8,128)(2,1)S(1)} %get-tuple-element.65), channel_id=1, source_target_pairs={{0,16},{4,20},{8,24},{12,28},{1,17},{5,21},{9,25},{13,29},{2,18},{... | collective-permute-start | bytes 835592 | tf_op jit(solution)/shard_map/ppermute | solution.py:266
  29.7 3.5 %collective-permute-done.3.got = bf16[272,512]{1,0:T(8,128)(2,1)S(1)} collective-permute-done((bf16[272,512]{1,0:T(8,128)(2,1)S(1)}, bf16[272,512]{1,0:T(8,128)(2,1)S(1)}, u32[]{:S(2)}, u32[]{:S(2)}) %collective-permute-start.3) | collective-permute-done | bytes 278560 | tf_op jit(solution)/shard_map/ppermute | solution.py:266
  33.2 1.0 copy-done.12
  34.2 1.0 copy-done.14
  35.3 1.5 %collective-permute-done.4.refs_9_.refs_7_ = bf16[512,512]{1,0:T(8,128)(2,1)S(1)} collective-permute-done((bf16[512,512]{1,0:T(8,128)(2,1)S(1)}, bf16[512,512]{1,0:T(8,128)(2,1)S(1)}, u32[]{:S(2)}, u32[]{:S(2)}) %collective-permute-start.4) | collective-permute-done | bytes 524320 | tf_op jit(solution)/shard_map/ppermute | solution.py:258
  36.8 8.4 %collective-permute-done.6.refs_10_.refs_8_ = bf16[384,512]{1,0:T(8,128)(2,1)S(1)} collective-permute-done((bf16[384,512]{1,0:T(8,128)(2,1)S(1)}, bf16[384,512]{1,0:T(8,128)(2,1)S(1)}, u32[]{:S(2)}, u32[]{:S(2)}) %collective-permute-start.6) | collective-permute-done | bytes 393248 | tf_op jit(solution)/shard_map/ppermute | solution.py:258
  45.9 1.1 collective-permute-start.7
  47.1 2.9 %shard_map.78 = (f32[256,1024]{1,0:T(8,128)S(1)}, f32[256,1024]{1,0:T(8,128)S(1)}, f32[256,1024]{1,0:T(8,128)S(1)}) custom-call(s32[1]{0:T(128)} %bitcast.1.me, bf16[256,1024]{1,0:T(8,128)(2,1)S(1)} %copy-done.10, bf16[256,1024]{1,0:T(8,128)(2,1)S(1)} %copy-done.17, bf16[256,256]{1,0:T(8,128)(2,1)S(1)} %bitcast.11, bf16[256,256]{1,0:T(8,128)(2,1)S(1)} %bitcast.8, ...), custom_call_target="tpu_custom_call" | custom-call | flops 1 | bytes 1 | tf_op jit(solution)/shard_map/pallas_call | solution.py:21
  50.4 2.1 %collective-permute-done.7.refs_1_ = bf16[256,512]{1,0:T(8,128)(2,1)S(1)} collective-permute-done((bf16[256,512]{1,0:T(8,128)(2,1)S(1)}, bf16[256,512]{1,0:T(8,128)(2,1)S(1)}, u32[]{:S(2)}, u32[]{:S(2)}) %collective-permute-start.7) | collective-permute-done | bytes 262176 | tf_op jit(solution)/shard_map/ppermute | solution.py:258
  52.5 1.2 shard_map.79
  53.7 0.9 collective-permute-start.13
  54.7 1.3 collective-permute-start.14
  55.9 4.4 %collective-permute-start.8 = (bf16[128,1024]{1,0:T(8,128)(2,1)S(1)}, bf16[128,1024]{1,0:T(8,128)(2,1)S(1)}, u32[]{:S(2)}, u32[]{:S(2)}) collective-permute-start(bf16[128,1024]{1,0:T(8,128)(2,1)S(1)} %get-tuple-element.75.refs_0_), channel_id=1, source_target_pairs={{0,1},{1,0},{2,3},{3,2},{4,5},{5,4},{6,7},{7,6},{8,9},{9,8},{10,11... | collective-permute-start | bytes 786440 | tf_op jit(solution)/shard_map/ppermute | solution.py:269
  61.0 1.3 collective-permute-start.19
  62.3 3.2 %collective-permute-done.14.refs_1_ = bf16[128,1024]{1,0:T(8,128)(2,1)} collective-permute-done((bf16[128,1024]{1,0:T(8,128)(2,1)}, bf16[128,1024]{1,0:T(8,128)(2,1)}, u32[]{:S(2)}, u32[]{:S(2)}) %collective-permute-start.14) | collective-permute-done | bytes 262176 | tf_op jit(solution)/shard_map/ppermute | solution.py:262
  65.5 7.3 %collective-permute-start.15 = (bf16[128,1024]{1,0:T(8,128)(2,1)}, bf16[128,1024]{1,0:T(8,128)(2,1)}, u32[]{:S(2)}, u32[]{:S(2)}) collective-permute-start(bf16[128,1024]{1,0:T(8,128)(2,1)} %collective-permute-done.13.refs_0_), channel_id=1, source_target_pairs={{0,1},{1,0},{2,3},{3,2},{4,5},{5,4},{6,7},{7,6},{8,9},{9,8},{10,11... | collective-permute-start | bytes 786440 | tf_op jit(solution)/shard_map/ppermute | solution.py:269
  73.5 1.0 copy-done.1
  74.5 1.0 copy-done.4
  75.5 0.9 copy-done.24
  76.5 0.9 copy-done.26
  77.4 2.7 %shard_map.80 = (f32[2,2,64,512]{3,2,1,0:T(8,128)S(1)}, bf16[2,2,64,512]{3,2,1,0:T(8,128)(2,1)S(1)}) custom-call(s32[1]{0:T(128)} %bitcast.3.me, bf16[128,1024]{1,0:T(8,128)(2,1)S(1)} %copy-done.24, bf16[128,1024]{1,0:T(8,128)(2,1)} %get-tuple-element.76.refs_1_, bf16[128,1024]{1,0:T(8,128)(2,1)S(1)} %copy-done.26, ...), custom_call_target="tpu_custom_call" | custom-call | flops 1 | bytes 1 | tf_op jit(solution)/shard_map/pallas_call | solution.py:21
  80.1 1.0 collective-permute-start.12
  81.1 1.0 collective-permute-start.25
  82.1 0.8 collective-permute-start.21
  84.3 2.8 %shard_map.82 = (f32[2,2,64,512]{3,2,1,0:T(8,128)S(1)}, bf16[2,2,64,512]{3,2,1,0:T(8,128)(2,1)S(1)}) custom-call(s32[1]{0:T(128)} %bitcast.3.me, bf16[128,1024]{1,0:T(8,128)(2,1)} %collective-permute-done.13.refs_0_, bf16[128,1024]{1,0:T(8,128)(2,1)} %collective-permute-done.14.refs_1_, bf16[128,1024]{1,0:T(8,128)(2,1)} %collective-permute-done.15.refs_2_, ...), custom_call_target="tpu_custom_call" | custom-call | flops 1 | bytes 1 | tf_op jit(solution)/shard_map/pallas_call | solution.py:21
  87.1 1.0 collective-permute-start.17
  89.3 1.5 %collective-permute-done.25.refs_0_ = bf16[128,1024]{1,0:T(8,128)(2,1)S(1)} collective-permute-done((bf16[128,1024]{1,0:T(8,128)(2,1)}, bf16[128,1024]{1,0:T(8,128)(2,1)S(1)}, u32[]{:S(2)}, u32[]{:S(2)}) %collective-permute-start.25) | collective-permute-done | bytes 262176 | tf_op jit(solution)/shard_map/ppermute | solution.py:262
  90.8 1.4 collective-permute-start.26
  92.1 2.6 %shard_map.84 = (f32[2,2,64,512]{3,2,1,0:T(8,128)S(1)}, bf16[2,2,64,512]{3,2,1,0:T(8,128)(2,1)S(1)}) custom-call(s32[1]{0:T(128)} %bitcast.3.me, bf16[128,1024]{1,0:T(8,128)(2,1)} %collective-permute-done.19.refs_0_, bf16[128,1024]{1,0:T(8,128)(2,1)} %collective-permute-done.20.refs_1_, bf16[128,1024]{1,0:T(8,128)(2,1)S(1)} %collective-permute-done.21.refs_2_, ...), custom_call_target="tpu_custom_call" | custom-call | flops 1 | bytes 1 | tf_op jit(solution)/shard_map/pallas_call | solution.py:21
  95.4 2.4 %collective-permute-start.18 = (bf16[2,2,64,512]{3,2,1,0:T(8,128)(2,1)S(1)}, bf16[2,2,64,512]{3,2,1,0:T(8,128)(2,1)S(1)}, u32[]{:S(2)}, u32[]{:S(2)}) collective-permute-start(bf16[2,2,64,512]{3,2,1,0:T(8,128)(2,1)S(1)} %shard_map.83), channel_id=1, source_target_pairs={{0,24},{4,28},{8,0},{12,4},{16,8},{20,12},{24,16},{28,20},{1,25},{... | collective-permute-start | bytes 786440 | tf_op jit(solution)/shard_map/ppermute | solution.py:262
  97.8 1.1 collective-permute-start.33
  98.9 1.0 shard_map.86
  99.8 1.0 collective-permute-start.27
  100.9 1.9 %collective-permute-done.23.refs_0_ = bf16[2,2,64,512]{3,2,1,0:T(8,128)(2,1)S(1)} collective-permute-done((bf16[2,2,64,512]{3,2,1,0:T(8,128)(2,1)S(1)}, bf16[2,2,64,512]{3,2,1,0:T(8,128)(2,1)S(1)}, u32[]{:S(2)}, u32[]{:S(2)}) %collective-permute-start.23) | collective-permute-done | bytes 262176 | tf_op jit(solution)/shard_map/ppermute | solution.py:273
  103.5 2.3 %collective-permute-start.24 = (bf16[2,2,64,512]{3,2,1,0:T(8,128)(2,1)}, bf16[2,2,64,512]{3,2,1,0:T(8,128)(2,1)}, u32[]{:S(2)}, u32[]{:S(2)}) collective-permute-start(bf16[2,2,64,512]{3,2,1,0:T(8,128)(2,1)} %shard_map.85), channel_id=1, source_target_pairs={{0,16},{4,20},{8,24},{12,28},{16,0},{20,4},{24,8},{28,12},{1,17},{... | collective-permute-start | bytes 786440 | tf_op jit(solution)/shard_map/ppermute | solution.py:262
  105.8 1.0 shard_map.89
  107.5 1.0 collective-permute-start.34
  108.6 2.7 %collective-permute-done.34.refs_0_ = bf16[1,2,64,512]{3,2,1,0:T(8,128)(2,1)S(1)} collective-permute-done((bf16[1,2,64,512]{3,2,1,0:T(8,128)(2,1)S(1)}, bf16[1,2,64,512]{3,2,1,0:T(8,128)(2,1)S(1)}, u32[]{:S(2)}, u32[]{:S(2)}) %collective-permute-start.34) | collective-permute-done | bytes 131104 | tf_op jit(solution)/shard_map/ppermute | solution.py:273
  111.3 0.9 copy-done.22
  112.5 11.2 %collective-permute-done.24.refs_2_ = bf16[2,2,64,512]{3,2,1,0:T(8,128)(2,1)} collective-permute-done((bf16[2,2,64,512]{3,2,1,0:T(8,128)(2,1)}, bf16[2,2,64,512]{3,2,1,0:T(8,128)(2,1)}, u32[]{:S(2)}, u32[]{:S(2)}) %collective-permute-start.24) | collective-permute-done | bytes 262176 | tf_op jit(solution)/shard_map/ppermute | solution.py:262
  123.7 0.9 copy-done.7
  124.6 0.9 copy-done.16
  125.6 1.0 shard_map.88
  126.6 1.7 %collective-permute-start.29 = (bf16[2,64,512]{2,1,0:T(8,128)(2,1)S(1)}, bf16[2,64,512]{2,1,0:T(8,128)(2,1)S(1)}, u32[]{:S(2)}, u32[]{:S(2)}) collective-permute-start(bf16[2,64,512]{2,1,0:T(8,128)(2,1)S(1)} %get-tuple-element.90), channel_id=1, source_target_pairs={{0,1},{1,2},{2,3},{3,0},{4,5},{5,6},{6,7},{7,4},{8,9},{9,10},{10,1... | collective-permute-start | bytes 393224 | tf_op jit(solution)/shard_map/ppermute | solution.py:276
  128.8 1.0 shard_map.91
  129.8 1.5 %collective-permute-start.36 = (bf16[2,64,512]{2,1,0:T(8,128)(2,1)S(1)}, bf16[2,64,512]{2,1,0:T(8,128)(2,1)S(1)}, u32[]{:S(2)}, u32[]{:S(2)}) collective-permute-start(bf16[2,64,512]{2,1,0:T(8,128)(2,1)S(1)} %get-tuple-element.98), channel_id=1, source_target_pairs={{0,1},{1,2},{2,3},{3,0},{4,5},{5,6},{6,7},{7,4},{8,9},{9,10},{10,1... | collective-permute-start | bytes 393224 | tf_op jit(solution)/shard_map/ppermute | solution.py:276
  131.3 1.3 collective-permute-start.37
  132.6 1.8 %collective-permute-done.30.refs_2_ = bf16[2,64,512]{2,1,0:T(8,128)(2,1)S(1)} collective-permute-done((bf16[2,64,512]{2,1,0:T(8,128)(2,1)S(1)}, bf16[2,64,512]{2,1,0:T(8,128)(2,1)S(1)}, u32[]{:S(2)}, u32[]{:S(2)}) %collective-permute-start.30) | collective-permute-done | bytes 131104 | tf_op jit(solution)/shard_map/ppermute | solution.py:276
  134.4 1.5 %collective-permute-done.31.refs_3_ = bf16[2,64,512]{2,1,0:T(8,128)(2,1)S(1)} collective-permute-done((bf16[2,64,512]{2,1,0:T(8,128)(2,1)S(1)}, bf16[2,64,512]{2,1,0:T(8,128)(2,1)S(1)}, u32[]{:S(2)}, u32[]{:S(2)}) %collective-permute-start.31) | collective-permute-done | bytes 131104 | tf_op jit(solution)/shard_map/ppermute | solution.py:276
  136.6 3.5 %collective-permute-done.37.refs_6_ = bf16[2,64,512]{2,1,0:T(8,128)(2,1)S(1)} collective-permute-done((bf16[2,64,512]{2,1,0:T(8,128)(2,1)S(1)}, bf16[2,64,512]{2,1,0:T(8,128)(2,1)S(1)}, u32[]{:S(2)}, u32[]{:S(2)}) %collective-permute-start.37) | collective-permute-done | bytes 131104 | tf_op jit(solution)/shard_map/ppermute | solution.py:276
  140.7 1.6 %shard_map.92 = bf16[256,2048]{1,0:T(8,128)(2,1)} custom-call(s32[2]{0:T(128)S(1)} %pad_add_fusion.me, bf16[2,64,512]{2,1,0:T(8,128)(2,1)S(1)} %get-tuple-element.89.refs_0_, bf16[2,64,512]{2,1,0:T(8,128)(2,1)S(1)} %collective-permute-done.29.refs_1_, bf16[2,64,512]{2,1,0:T(8,128)(2,1)S(1)} %collective-permute-done.30.refs_2_, ...), custom_call_target="tpu_custom_call" | custom-call | flops 1 | bytes 1 | tf_op jit(solution)/shard_map/pallas_call | solution.py:21
  (92 shorter events, 11.0 us)
Async XLA Ops:
  0.8 1.0 copy-start.9
  1.9 0.9 copy-start.19
  5.7 8.7 %copy-start.11 = (bf16[272,512]{1,0:T(8,128)(2,1)}, bf16[272,512]{1,0:T(8,128)(2,1)S(1)}, u32[]{:S(2)}) copy-start(bf16[272,512]{1,0:T(8,128)(2,1)S(1)} %get-tuple-element.53.refs_0_) | copy-start | bytes 835588
  5.7 8.6 %collective-permute-start = (bf16[272,512]{1,0:T(8,128)(2,1)}, bf16[272,512]{1,0:T(8,128)(2,1)S(1)}, u32[]{:S(2)}, u32[]{:S(2)}) collective-permute-start(bf16[272,512]{1,0:T(8,128)(2,1)} %get-tuple-element.54), channel_id=1, source_target_pairs={{0,4},{4,0},{8,12},{12,8},{16,20},{20,16},{24,28},{28,24},{1,5},{5... | collective-permute-start | bytes 835592 | tf_op jit(solution)/shard_map/ppermute | solution.py:258
  7.7 1.6 %copy-start.8 = (bf16[1024,1024]{1,0:T(8,128)(2,1)S(1)}, bf16[1024,1024]{1,0:T(8,128)(2,1)}, u32[]{:S(2)}) copy-start(bf16[1024,1024]{1,0:T(8,128)(2,1)} %w_out) | copy-start | bytes 6291460
  9.4 37.6 %copy-start.10 = (bf16[256,1024]{1,0:T(8,128)(2,1)S(1)}, bf16[256,1024]{1,0:T(8,128)(2,1)}, u32[]{:S(2)}) copy-start(bf16[256,1024]{1,0:T(8,128)(2,1)} %x.3) | copy-start | bytes 1572868
  9.5 37.6 %copy-start.17 = (bf16[256,1024]{1,0:T(8,128)(2,1)S(1)}, bf16[256,1024]{1,0:T(8,128)(2,1)}, u32[]{:S(2)}) copy-start(bf16[256,1024]{1,0:T(8,128)(2,1)} %z) | copy-start | bytes 1572868
  9.5 37.6 %copy-start.18 = (bf16[256,1,256]{2,0,1:T(8,128)(2,1)S(1)}, bf16[256,1,256]{2,0,1:T(8,128)(2,1)}, u32[]{:S(2)}) copy-start(bf16[256,1,256]{2,0,1:T(8,128)(2,1)} %param.10) | copy-start | bytes 393220
  9.5 37.6 %copy-start.20 = (bf16[256,1,256]{2,0,1:T(8,128)(2,1)S(1)}, bf16[256,1,256]{2,0,1:T(8,128)(2,1)}, u32[]{:S(2)}) copy-start(bf16[256,1,256]{2,0,1:T(8,128)(2,1)} %param.9) | copy-start | bytes 393220
  9.5 16.0 %collective-permute-start.2 = (bf16[512,512]{1,0:T(8,128)(2,1)S(1)}, bf16[512,512]{1,0:T(8,128)(2,1)S(1)}, u32[]{:S(2)}, u32[]{:S(2)}) collective-permute-start(bf16[512,512]{1,0:T(8,128)(2,1)S(1)} %get-tuple-element.57.refs_4_.refs_2_), channel_id=1, source_target_pairs={{0,4},{4,0},{8,12},{12,8},{16,20},{20,16},{24,28},{28,24},{1,5},{5... | collective-permute-start | bytes 1572872 | tf_op jit(solution)/shard_map/ppermute | solution.py:258
  9.7 9.8 %collective-permute-start.5 = (bf16[384,512]{1,0:T(8,128)(2,1)S(1)}, bf16[384,512]{1,0:T(8,128)(2,1)S(1)}, u32[]{:S(2)}, u32[]{:S(2)}) collective-permute-start(bf16[384,512]{1,0:T(8,128)(2,1)S(1)} %get-tuple-element.59), channel_id=1, source_target_pairs={{0,1},{1,0},{2,3},{3,2},{4,5},{5,4},{6,7},{7,6},{8,9},{9,8},{10,11... | collective-permute-start | bytes 1179656 | tf_op jit(solution)/shard_map/ppermute | solution.py:269
  10.6 39.4 %collective-permute-start.10 = (bf16[640,512]{1,0:T(8,128)(2,1)S(1)}, bf16[640,512]{1,0:T(8,128)(2,1)S(1)}, u32[]{:S(2)}, u32[]{:S(2)}) collective-permute-start(bf16[640,512]{1,0:T(8,128)(2,1)S(1)} %get-tuple-element.60), channel_id=1, source_target_pairs={{0,1},{1,0},{2,3},{3,2},{4,5},{5,4},{6,7},{7,6},{8,9},{9,8},{10,11... | collective-permute-start | bytes 1966088 | tf_op jit(solution)/shard_map/ppermute | solution.py:269
  14.3 0.7 copy-start.13
  15.0 6.6 %collective-permute-start.1 = (bf16[272,512]{1,0:T(8,128)(2,1)S(1)}, bf16[272,512]{1,0:T(8,128)(2,1)S(1)}, u32[]{:S(2)}, u32[]{:S(2)}) collective-permute-start(bf16[272,512]{1,0:T(8,128)(2,1)S(1)} %get-tuple-element.61), channel_id=1, source_target_pairs={{0,8},{4,12},{8,16},{12,20},{16,24},{20,28},{1,9},{5,13},{9,17},{1... | collective-permute-start | bytes 835592 | tf_op jit(solution)/shard_map/ppermute | solution.py:266
  18.2 18.6 %collective-permute-start.4 = (bf16[512,512]{1,0:T(8,128)(2,1)S(1)}, bf16[512,512]{1,0:T(8,128)(2,1)S(1)}, u32[]{:S(2)}, u32[]{:S(2)}) collective-permute-start(bf16[512,512]{1,0:T(8,128)(2,1)S(1)} %get-tuple-element.58.refs_5_.refs_3_), channel_id=1, source_target_pairs={{0,4},{4,0},{8,12},{12,8},{16,20},{20,16},{24,28},{28,24},{1,5},{5... | collective-permute-start | bytes 1572872 | tf_op jit(solution)/shard_map/ppermute | solution.py:258
  19.5 30.5 %copy-start = (bf16[384,512]{1,0:T(8,128)(2,1)}, bf16[384,512]{1,0:T(8,128)(2,1)S(1)}, u32[]{:S(2)}) copy-start(bf16[384,512]{1,0:T(8,128)(2,1)S(1)} %collective-permute-done.5.refs_6_.refs_4_) | copy-start | bytes 1179652
  19.5 25.7 %collective-permute-start.6 = (bf16[384,512]{1,0:T(8,128)(2,1)S(1)}, bf16[384,512]{1,0:T(8,128)(2,1)S(1)}, u32[]{:S(2)}, u32[]{:S(2)}) collective-permute-start(bf16[384,512]{1,0:T(8,128)(2,1)S(1)} %collective-permute-done.5.refs_6_.refs_4_), channel_id=1, source_target_pairs={{0,4},{4,0},{8,12},{12,8},{16,20},{20,16},{24,28},{28,24},{1,5},{5... | collective-permute-start | bytes 1179656 | tf_op jit(solution)/shard_map/ppermute | solution.py:258
  21.6 30.9 %copy-start.27 = (f32[1024]{0:T(1024)S(1)}, f32[1024]{0:T(1024)}, u32[]{:S(2)}) copy-start(f32[1024]{0:T(1024)} %param.12) | copy-start | bytes 12292
  25.5 7.7 %collective-permute-start.3 = (bf16[272,512]{1,0:T(8,128)(2,1)S(1)}, bf16[272,512]{1,0:T(8,128)(2,1)S(1)}, u32[]{:S(2)}, u32[]{:S(2)}) collective-permute-start(bf16[272,512]{1,0:T(8,128)(2,1)S(1)} %get-tuple-element.65), channel_id=1, source_target_pairs={{0,16},{4,20},{8,24},{12,28},{1,17},{5,21},{9,25},{13,29},{2,18},{... | collective-permute-start | bytes 835592 | tf_op jit(solution)/shard_map/ppermute | solution.py:266
  33.2 1.0 copy-start.12
  34.1 1.0 copy-start.14
  45.2 0.7 copy-start.3
  45.9 6.6 %collective-permute-start.7 = (bf16[256,512]{1,0:T(8,128)(2,1)S(1)}, bf16[256,512]{1,0:T(8,128)(2,1)S(1)}, u32[]{:S(2)}, u32[]{:S(2)}) collective-permute-start(bf16[256,512]{1,0:T(8,128)(2,1)S(1)} %get-tuple-element.74), channel_id=1, source_target_pairs={{0,4},{4,0},{8,12},{12,8},{16,20},{20,16},{24,28},{28,24},{1,5},{5... | collective-permute-start | bytes 786440 | tf_op jit(solution)/shard_map/ppermute | solution.py:258
  50.0 23.5 %collective-permute-start.11 = (bf16[640,512]{1,0:T(8,128)(2,1)S(1)}, bf16[640,512]{1,0:T(8,128)(2,1)S(1)}, u32[]{:S(2)}, u32[]{:S(2)}) collective-permute-start(bf16[640,512]{1,0:T(8,128)(2,1)S(1)} %collective-permute-done.10.refs_7_.refs_5_), channel_id=1, source_target_pairs={{0,4},{4,0},{8,12},{12,8},{16,20},{20,16},{24,28},{28,24},{1,5},{5... | collective-permute-start | bytes 1966088 | tf_op jit(solution)/shard_map/ppermute | solution.py:258
  53.7 7.3 %collective-permute-start.13 = (bf16[128,1024]{1,0:T(8,128)(2,1)S(1)}, bf16[128,1024]{1,0:T(8,128)(2,1)}, u32[]{:S(2)}, u32[]{:S(2)}) collective-permute-start(bf16[128,1024]{1,0:T(8,128)(2,1)S(1)} %get-tuple-element.75.refs_0_), channel_id=1, source_target_pairs={{0,8},{4,12},{8,16},{12,20},{16,24},{20,28},{24,0},{28,4},{1,9},{5... | collective-permute-start | bytes 786440 | tf_op jit(solution)/shard_map/ppermute | solution.py:262
  54.7 10.8 %collective-permute-start.14 = (bf16[128,1024]{1,0:T(8,128)(2,1)}, bf16[128,1024]{1,0:T(8,128)(2,1)}, u32[]{:S(2)}, u32[]{:S(2)}) collective-permute-start(bf16[128,1024]{1,0:T(8,128)(2,1)} %get-tuple-element.76.refs_1_), channel_id=1, source_target_pairs={{0,8},{4,12},{8,16},{12,20},{16,24},{20,28},{24,0},{28,4},{1,9},{5... | collective-permute-start | bytes 786440 | tf_op jit(solution)/shard_map/ppermute | solution.py:262
  55.9 16.8 %collective-permute-start.8 = (bf16[128,1024]{1,0:T(8,128)(2,1)S(1)}, bf16[128,1024]{1,0:T(8,128)(2,1)S(1)}, u32[]{:S(2)}, u32[]{:S(2)}) collective-permute-start(bf16[128,1024]{1,0:T(8,128)(2,1)S(1)} %get-tuple-element.75.refs_0_), channel_id=1, source_target_pairs={{0,1},{1,0},{2,3},{3,2},{4,5},{5,4},{6,7},{7,6},{8,9},{9,8},{10,11... | collective-permute-start | bytes 786440 | tf_op jit(solution)/shard_map/ppermute | solution.py:269
  61.0 12.5 %collective-permute-start.9 = (bf16[128,1024]{1,0:T(8,128)(2,1)}, bf16[128,1024]{1,0:T(8,128)(2,1)}, u32[]{:S(2)}, u32[]{:S(2)}) collective-permute-start(bf16[128,1024]{1,0:T(8,128)(2,1)} %get-tuple-element.76.refs_1_), channel_id=1, source_target_pairs={{0,1},{1,0},{2,3},{3,2},{4,5},{5,4},{6,7},{7,6},{8,9},{9,8},{10,11... | collective-permute-start | bytes 786440 | tf_op jit(solution)/shard_map/ppermute | solution.py:269
  61.0 20.1 %collective-permute-start.19 = (bf16[128,1024]{1,0:T(8,128)(2,1)}, bf16[128,1024]{1,0:T(8,128)(2,1)}, u32[]{:S(2)}, u32[]{:S(2)}) collective-permute-start(bf16[128,1024]{1,0:T(8,128)(2,1)} %collective-permute-done.13.refs_0_), channel_id=1, source_target_pairs={{0,8},{4,12},{8,16},{12,20},{16,24},{20,28},{24,0},{28,4},{1,9},{5... | collective-permute-start | bytes 786440 | tf_op jit(solution)/shard_map/ppermute | solution.py:262
  65.5 16.6 %collective-permute-start.15 = (bf16[128,1024]{1,0:T(8,128)(2,1)}, bf16[128,1024]{1,0:T(8,128)(2,1)}, u32[]{:S(2)}, u32[]{:S(2)}) collective-permute-start(bf16[128,1024]{1,0:T(8,128)(2,1)} %collective-permute-done.13.refs_0_), channel_id=1, source_target_pairs={{0,1},{1,0},{2,3},{3,2},{4,5},{5,4},{6,7},{7,6},{8,9},{9,8},{10,11... | collective-permute-start | bytes 786440 | tf_op jit(solution)/shard_map/ppermute | solution.py:269
  73.5 10.1 %collective-permute-start.20 = (bf16[128,1024]{1,0:T(8,128)(2,1)}, bf16[128,1024]{1,0:T(8,128)(2,1)}, u32[]{:S(2)}, u32[]{:S(2)}) collective-permute-start(bf16[128,1024]{1,0:T(8,128)(2,1)} %collective-permute-done.14.refs_1_), channel_id=1, source_target_pairs={{0,8},{4,12},{8,16},{12,20},{16,24},{20,28},{24,0},{28,4},{1,9},{5... | collective-permute-start | bytes 786440 | tf_op jit(solution)/shard_map/ppermute | solution.py:262
  73.5 10.8 %collective-permute-start.16 = (bf16[128,1024]{1,0:T(8,128)(2,1)}, bf16[128,1024]{1,0:T(8,128)(2,1)}, u32[]{:S(2)}, u32[]{:S(2)}) collective-permute-start(bf16[128,1024]{1,0:T(8,128)(2,1)} %collective-permute-done.14.refs_1_), channel_id=1, source_target_pairs={{0,1},{1,0},{2,3},{3,2},{4,5},{5,4},{6,7},{7,6},{8,9},{9,8},{10,11... | collective-permute-start | bytes 786440 | tf_op jit(solution)/shard_map/ppermute | solution.py:269
  73.5 1.0 copy-start.1
  74.5 1.0 copy-start.4
  75.5 0.9 copy-start.24
  76.5 0.9 copy-start.26
  77.4 6.9 %copy-start.2 = (bf16[384,512]{1,0:T(8,128)(2,1)S(1)}, bf16[384,512]{1,0:T(8,128)(2,1)}, u32[]{:S(2)}) copy-start(bf16[384,512]{1,0:T(8,128)(2,1)} %copy-done) | copy-start | bytes 1179652
  77.4 6.9 %copy-start.5 = (bf16[384,512]{1,0:T(8,128)(2,1)S(1)}, bf16[384,512]{1,0:T(8,128)(2,1)}, u32[]{:S(2)}) copy-start(bf16[384,512]{1,0:T(8,128)(2,1)} %copy-done.3) | copy-start | bytes 1179652
  80.1 8.0 %collective-permute-start.12 = (bf16[2,2,64,512]{3,2,1,0:T(8,128)(2,1)S(1)}, bf16[2,2,64,512]{3,2,1,0:T(8,128)(2,1)S(1)}, u32[]{:S(2)}, u32[]{:S(2)}) collective-permute-start(bf16[2,2,64,512]{3,2,1,0:T(8,128)(2,1)S(1)} %get-tuple-element.79), channel_id=1, source_target_pairs={{0,2},{1,3},{2,0},{3,1},{4,6},{5,7},{6,4},{7,5},{8,10},{9,11},{10,... | collective-permute-start | bytes 786440 | tf_op jit(solution)/shard_map/ppermute | solution.py:273
  81.1 9.6 %collective-permute-start.25 = (bf16[128,1024]{1,0:T(8,128)(2,1)}, bf16[128,1024]{1,0:T(8,128)(2,1)S(1)}, u32[]{:S(2)}, u32[]{:S(2)}) collective-permute-start(bf16[128,1024]{1,0:T(8,128)(2,1)} %collective-permute-done.19.refs_0_), channel_id=1, source_target_pairs={{0,8},{4,12},{8,16},{12,20},{16,24},{20,28},{24,0},{28,4},{1,9},{5... | collective-permute-start | bytes 786440 | tf_op jit(solution)/shard_map/ppermute | solution.py:262
  82.1 10.0 %collective-permute-start.21 = (bf16[128,1024]{1,0:T(8,128)(2,1)}, bf16[128,1024]{1,0:T(8,128)(2,1)S(1)}, u32[]{:S(2)}, u32[]{:S(2)}) collective-permute-start(bf16[128,1024]{1,0:T(8,128)(2,1)} %collective-permute-done.19.refs_0_), channel_id=1, source_target_pairs={{0,1},{1,0},{2,3},{3,2},{4,5},{5,4},{6,7},{7,6},{8,9},{9,8},{10,11... | collective-permute-start | bytes 786440 | tf_op jit(solution)/shard_map/ppermute | solution.py:269
  83.5 8.6 %collective-permute-start.22 = (bf16[128,1024]{1,0:T(8,128)(2,1)}, bf16[128,1024]{1,0:T(8,128)(2,1)S(1)}, u32[]{:S(2)}, u32[]{:S(2)}) collective-permute-start(bf16[128,1024]{1,0:T(8,128)(2,1)} %collective-permute-done.20.refs_1_), channel_id=1, source_target_pairs={{0,1},{1,0},{2,3},{3,2},{4,5},{5,4},{6,7},{7,6},{8,9},{9,8},{10,11... | collective-permute-start | bytes 786440 | tf_op jit(solution)/shard_map/ppermute | solution.py:269
  87.1 8.2 %collective-permute-start.17 = (bf16[2,2,64,512]{3,2,1,0:T(8,128)(2,1)S(1)}, bf16[2,2,64,512]{3,2,1,0:T(8,128)(2,1)S(1)}, u32[]{:S(2)}, u32[]{:S(2)}) collective-permute-start(bf16[2,2,64,512]{3,2,1,0:T(8,128)(2,1)S(1)} %get-tuple-element.81), channel_id=1, source_target_pairs={{0,2},{1,3},{2,0},{3,1},{4,6},{5,7},{6,4},{7,5},{8,10},{9,11},{10,... | collective-permute-start | bytes 786440 | tf_op jit(solution)/shard_map/ppermute | solution.py:273
  88.1 9.7 %collective-permute-start.32 = (bf16[128,1024]{1,0:T(8,128)(2,1)}, bf16[128,1024]{1,0:T(8,128)(2,1)S(1)}, u32[]{:S(2)}, u32[]{:S(2)}) collective-permute-start(bf16[128,1024]{1,0:T(8,128)(2,1)} %collective-permute-done.20.refs_1_), channel_id=1, source_target_pairs={{0,8},{4,12},{8,16},{12,20},{16,24},{20,28},{24,0},{28,4},{1,9},{5... | collective-permute-start | bytes 786440 | tf_op jit(solution)/shard_map/ppermute | solution.py:262
  90.8 8.1 %collective-permute-start.26 = (bf16[128,1024]{1,0:T(8,128)(2,1)S(1)}, bf16[128,1024]{1,0:T(8,128)(2,1)S(1)}, u32[]{:S(2)}, u32[]{:S(2)}) collective-permute-start(bf16[128,1024]{1,0:T(8,128)(2,1)S(1)} %collective-permute-done.25.refs_0_), channel_id=1, source_target_pairs={{0,1},{1,0},{2,3},{3,2},{4,5},{5,4},{6,7},{7,6},{8,9},{9,8},{10,11... | collective-permute-start | bytes 786440 | tf_op jit(solution)/shard_map/ppermute | solution.py:269
  94.7 8.0 %collective-permute-start.23 = (bf16[2,2,64,512]{3,2,1,0:T(8,128)(2,1)S(1)}, bf16[2,2,64,512]{3,2,1,0:T(8,128)(2,1)S(1)}, u32[]{:S(2)}, u32[]{:S(2)}) collective-permute-start(bf16[2,2,64,512]{3,2,1,0:T(8,128)(2,1)S(1)} %get-tuple-element.84), channel_id=1, source_target_pairs={{0,2},{1,3},{2,0},{3,1},{4,6},{5,7},{6,4},{7,5},{8,10},{9,11},{10,... | collective-permute-start | bytes 786440 | tf_op jit(solution)/shard_map/ppermute | solution.py:273
  95.4 10.3 %collective-permute-start.18 = (bf16[2,2,64,512]{3,2,1,0:T(8,128)(2,1)S(1)}, bf16[2,2,64,512]{3,2,1,0:T(8,128)(2,1)S(1)}, u32[]{:S(2)}, u32[]{:S(2)}) collective-permute-start(bf16[2,2,64,512]{3,2,1,0:T(8,128)(2,1)S(1)} %shard_map.83), channel_id=1, source_target_pairs={{0,24},{4,28},{8,0},{12,4},{16,8},{20,12},{24,16},{28,20},{1,25},{... | collective-permute-start | bytes 786440 | tf_op jit(solution)/shard_map/ppermute | solution.py:262
  97.8 8.0 %collective-permute-start.33 = (bf16[128,1024]{1,0:T(8,128)(2,1)S(1)}, bf16[128,1024]{1,0:T(8,128)(2,1)S(1)}, u32[]{:S(2)}, u32[]{:S(2)}) collective-permute-start(bf16[128,1024]{1,0:T(8,128)(2,1)S(1)} %collective-permute-done.32.refs_0_), channel_id=1, source_target_pairs={{0,1},{1,0},{2,3},{3,2},{4,5},{5,4},{6,7},{7,6},{8,9},{9,8},{10,11... | collective-permute-start | bytes 786440 | tf_op jit(solution)/shard_map/ppermute | solution.py:269
  99.8 8.6 %collective-permute-start.27 = (bf16[1,2,64,512]{3,2,1,0:T(8,128)(2,1)S(1)}, bf16[1,2,64,512]{3,2,1,0:T(8,128)(2,1)S(1)}, u32[]{:S(2)}, u32[]{:S(2)}) collective-permute-start(bf16[1,2,64,512]{3,2,1,0:T(8,128)(2,1)S(1)} %get-tuple-element.88), channel_id=1, source_target_pairs={{0,2},{1,3},{2,0},{3,1},{4,6},{5,7},{6,4},{7,5},{8,10},{9,11},{10,... | collective-permute-start | bytes 393224 | tf_op jit(solution)/shard_map/ppermute | solution.py:273
  103.5 20.2 %collective-permute-start.24 = (bf16[2,2,64,512]{3,2,1,0:T(8,128)(2,1)}, bf16[2,2,64,512]{3,2,1,0:T(8,128)(2,1)}, u32[]{:S(2)}, u32[]{:S(2)}) collective-permute-start(bf16[2,2,64,512]{3,2,1,0:T(8,128)(2,1)} %shard_map.85), channel_id=1, source_target_pairs={{0,16},{4,20},{8,24},{12,28},{16,0},{20,4},{24,8},{28,12},{1,17},{... | collective-permute-start | bytes 786440 | tf_op jit(solution)/shard_map/ppermute | solution.py:262
  105.8 1.0 copy-start.15
  106.8 0.7 copy-start.21
  107.5 3.8 %collective-permute-start.34 = (bf16[1,2,64,512]{3,2,1,0:T(8,128)(2,1)S(1)}, bf16[1,2,64,512]{3,2,1,0:T(8,128)(2,1)S(1)}, u32[]{:S(2)}, u32[]{:S(2)}) collective-permute-start(bf16[1,2,64,512]{3,2,1,0:T(8,128)(2,1)S(1)} %get-tuple-element.96), channel_id=1, source_target_pairs={{0,2},{1,3},{2,0},{3,1},{4,6},{5,7},{6,4},{7,5},{8,10},{9,11},{10,... | collective-permute-start | bytes 393224 | tf_op jit(solution)/shard_map/ppermute | solution.py:273
  108.5 15.2 %collective-permute-start.28 = (bf16[1,2,64,512]{3,2,1,0:T(8,128)(2,1)S(1)}, bf16[1,2,64,512]{3,2,1,0:T(8,128)(2,1)S(1)}, u32[]{:S(2)}, u32[]{:S(2)}) collective-permute-start(bf16[1,2,64,512]{3,2,1,0:T(8,128)(2,1)S(1)} %shard_map.87), channel_id=1, source_target_pairs={{0,8},{4,12},{8,16},{12,20},{16,24},{20,28},{24,0},{28,4},{1,9},{5... | collective-permute-start | bytes 393224 | tf_op jit(solution)/shard_map/ppermute | solution.py:262
  111.3 1.0 copy-start.22
  112.3 16.5 %collective-permute-start.35 = (bf16[1,2,64,512]{3,2,1,0:T(8,128)(2,1)S(1)}, bf16[1,2,64,512]{3,2,1,0:T(8,128)(2,1)S(1)}, u32[]{:S(2)}, u32[]{:S(2)}) collective-permute-start(bf16[1,2,64,512]{3,2,1,0:T(8,128)(2,1)S(1)} %shard_map.90), channel_id=1, source_target_pairs={{0,8},{4,12},{8,16},{12,20},{16,24},{20,28},{24,0},{28,4},{1,9},{5... | collective-permute-start | bytes 393224 | tf_op jit(solution)/shard_map/ppermute | solution.py:262
  123.7 1.0 copy-start.7
  124.6 0.9 copy-start.16
  126.6 6.0 %collective-permute-start.29 = (bf16[2,64,512]{2,1,0:T(8,128)(2,1)S(1)}, bf16[2,64,512]{2,1,0:T(8,128)(2,1)S(1)}, u32[]{:S(2)}, u32[]{:S(2)}) collective-permute-start(bf16[2,64,512]{2,1,0:T(8,128)(2,1)S(1)} %get-tuple-element.90), channel_id=1, source_target_pairs={{0,1},{1,2},{2,3},{3,0},{4,5},{5,6},{6,7},{7,4},{8,9},{9,10},{10,1... | collective-permute-start | bytes 393224 | tf_op jit(solution)/shard_map/ppermute | solution.py:276
  128.3 6.2 %collective-permute-start.30 = (bf16[2,64,512]{2,1,0:T(8,128)(2,1)S(1)}, bf16[2,64,512]{2,1,0:T(8,128)(2,1)S(1)}, u32[]{:S(2)}, u32[]{:S(2)}) collective-permute-start(bf16[2,64,512]{2,1,0:T(8,128)(2,1)S(1)} %get-tuple-element.91), channel_id=1, source_target_pairs={{0,2},{1,3},{2,0},{3,1},{4,6},{5,7},{6,4},{7,5},{8,10},{9,11},{10,... | collective-permute-start | bytes 393224 | tf_op jit(solution)/shard_map/ppermute | solution.py:276
  128.5 7.5 %collective-permute-start.31 = (bf16[2,64,512]{2,1,0:T(8,128)(2,1)S(1)}, bf16[2,64,512]{2,1,0:T(8,128)(2,1)S(1)}, u32[]{:S(2)}, u32[]{:S(2)}) collective-permute-start(bf16[2,64,512]{2,1,0:T(8,128)(2,1)S(1)} %get-tuple-element.92), channel_id=1, source_target_pairs={{0,3},{1,0},{2,1},{3,2},{4,7},{5,4},{6,5},{7,6},{8,11},{9,8},{10,9... | collective-permute-start | bytes 393224 | tf_op jit(solution)/shard_map/ppermute | solution.py:276
  129.8 6.8 %collective-permute-start.36 = (bf16[2,64,512]{2,1,0:T(8,128)(2,1)S(1)}, bf16[2,64,512]{2,1,0:T(8,128)(2,1)S(1)}, u32[]{:S(2)}, u32[]{:S(2)}) collective-permute-start(bf16[2,64,512]{2,1,0:T(8,128)(2,1)S(1)} %get-tuple-element.98), channel_id=1, source_target_pairs={{0,1},{1,2},{2,3},{3,0},{4,5},{5,6},{6,7},{7,4},{8,9},{9,10},{10,1... | collective-permute-start | bytes 393224 | tf_op jit(solution)/shard_map/ppermute | solution.py:276
  131.3 8.8 %collective-permute-start.37 = (bf16[2,64,512]{2,1,0:T(8,128)(2,1)S(1)}, bf16[2,64,512]{2,1,0:T(8,128)(2,1)S(1)}, u32[]{:S(2)}, u32[]{:S(2)}) collective-permute-start(bf16[2,64,512]{2,1,0:T(8,128)(2,1)S(1)} %get-tuple-element.99), channel_id=1, source_target_pairs={{0,2},{1,3},{2,0},{3,1},{4,6},{5,7},{6,4},{7,5},{8,10},{9,11},{10,... | collective-permute-start | bytes 393224 | tf_op jit(solution)/shard_map/ppermute | solution.py:276
  132.6 8.1 %collective-permute-start.38 = (bf16[2,64,512]{2,1,0:T(8,128)(2,1)S(1)}, bf16[2,64,512]{2,1,0:T(8,128)(2,1)S(1)}, u32[]{:S(2)}, u32[]{:S(2)}) collective-permute-start(bf16[2,64,512]{2,1,0:T(8,128)(2,1)S(1)} %get-tuple-element.100), channel_id=1, source_target_pairs={{0,3},{1,0},{2,1},{3,2},{4,7},{5,4},{6,5},{7,6},{8,11},{9,8},{10,9... | collective-permute-start | bytes 393224 | tf_op jit(solution)/shard_map/ppermute | solution.py:276
  (3 other events, 2.1 us)

commit v3 on v2

--- a/solution.py
+++ b/solution.py
@@ -93,7 +93,8 @@
             run_decay[...] = jnp.broadcast_to(decay, run_decay.shape)
 
 
-def step_kernel(first, me, got, before, before_decay, run, run_decay, message, o_before, o_before_decay, o_run, o_run_decay):
+def step_kernel(first, me, got, before, before_decay, run, run_decay, *refs):
+    message, o_before, o_before_decay, o_run, o_run_decay = refs[-5:]
     s, d = read_message(got)
     if first:
         o_before[...], o_before_decay[...] = s, jnp.broadcast_to(d, o_before_decay.shape)
@@ -149,7 +150,7 @@
 
 
 def hidden_kernel(r, me, c, y, silu, grow, gain, *refs):
-    parts, outs, entering = refs[:r], refs[r:-1], refs[-1]
+    parts, outs, entering = refs[:r], refs[-1 - CHUNKS : -1], refs[-1]
     w = entering.shape[1] // r
     for g in range(r):
 
@@ -308,7 +309,7 @@
         out, before, before_decay, run, run_decay = call(
             functools.partial(step_kernel, k == 1),
             [message, full, row, full, row],
-            (me, shift_h(out, k), before, before_decay, run, run_decay),
+            (me, shift_h(out, k), before, before_decay, run, run_decay, *got),
         )
         k *= 2
         out = after(out, *[group[0] for group in w_parts[1:]])
@@ -327,7 +328,7 @@
     hidden = call(
         functools.partial(hidden_kernel, r),
         [((part_rows, channels), BF)] * CHUNKS,
-        (me, c_local, y, silu, grow, norm_gain.reshape(1, channels), *parts),
+        (me, c_local, y, silu, grow, norm_gain.reshape(1, channels), *parts, *early),
         scratch=[pltpu.VMEM((n, channels), BF)],
     )
 
@@ -346,8 +347,8 @@
         if k + 1 < n_head:
             hidden = [rot_h(after(v, *outs[: max(t - 1, 0)]), 1) for v in hidden]
         other = [swap_core(v) for v in now]
-        if t > 1:
-            other[0] = after(other[0], sums[t - 2], *back[: max(t - 3, 0)])
+        if t > 2:
+            other[0] = after(other[0], sums[t - 3])
         shape = (len(chunks), r, piece, width)
         mine, *send = call(
             functools.partial(product_kernel, r, n_y, len(chunks)),

time: 143 us -> 141 us (0.986)
  starting transfers between devices: 48.6 us -> 53.2 us
  local copies, waits for them, and re-layouts: 17.2 us -> 13.1 us
  waiting for transfers between devices: 53.2 us -> 50.2 us
    unnamed x57 -> x47, local copies, waits for them, and re-layouts: 17.2 us -> 13.1 us
    ppermute x10, starting transfers between devices: 16.7 us -> 19.2 us  [swap_core(): return lax.ppermute(v, 'head', [(i, i ^ 1) for i in range(n_head)])]
    ppermute x2, waiting for transfers between devices: 5.42 us -> 3.5 us  [shift_h(): return lax.ppermute(v, 'seq', pairs)]
    ppermute x5, waiting for transfers between devices: 4.59 us -> 2.76 us  [rot_y(): return lax.ppermute(v, 'head', pairs)]
    ppermute x10, starting transfers between devices: 9.79 us -> 11.5 us  [rot_h(): return lax.ppermute(v, 'seq', pairs)]
  transfers between devices with their start and end apart: 39 -> 39, of which waited for: 18 -> 17; matrix products, arithmetic and copies ran while one was open for 0% -> 0% of each run, Pallas kernels for 13% -> 14%
where the time goes in v3:
time: 141 us; the launch traced here: 140 us
  starting transfers between devices  53.2 us (38%)
  waiting for transfers between devices  50.2 us (36%)
  Pallas kernels  23.5 us (17%)
  local copies, waits for them, and re-layouts  13.1 us (9%)
    pallas_call x20, Pallas kernels, call(): pl.pallas_call(kernel, out_shape=[jax.ShapeDtypeStruct(s, d) for s, d in...  23.5 us
    ppermute x10, starting transfers between devices, swap_core(): return lax.ppermute(v, 'head', [(i, i ^ 1) for i in range(n_head)])  19.2 us
    ppermute x6, waiting for transfers between devices, rot_b(): return lax.ppermute(v, 'seq', pairs)  18 us
    ppermute x10, waiting for transfers between devices, rot_h(): return lax.ppermute(v, 'seq', pairs)  17.6 us
    unnamed x47, local copies, waits for them, and re-layouts  13.1 us
    ppermute x10, starting transfers between devices, rot_h(): return lax.ppermute(v, 'seq', pairs)  11.5 us
    ppermute x6, waiting for transfers between devices, rot_head(): lax.ppermute(v, 'head', [(i, (i + j) % n_head) for i in range(n_head)])  8.27 us
    ppermute x2, starting transfers between devices, shift_h(): return lax.ppermute(v, 'seq', pairs)  7.29 us
  transfers between devices with their start and end apart: 39, of which 17 were waited for; matrix products, arithmetic and copies ran while one was open for 0% of the time, Pallas kernels for 14%

profile of v3, /device:TPU:1, one launch (start us, length us, event | category | flops | bytes accessed | tf_op | source)
XLA Modules:
  0.0 140.4 jit_solution(6352027782603012712)
XLA Ops:
  0.0 0.8 copy.8.logs
  0.8 1.1 copy-done.8
  1.9 0.9 copy-done.14
  2.8 2.2 %shard_map.73 = (bf16[272,512]{1,0:T(8,128)(2,1)S(1)}, bf16[272,512]{1,0:T(8,128)(2,1)S(1)}) custom-call(s32[1]{0:T(128)} %bitcast.1.me, bf16[256,1024]{1,0:T(8,128)(2,1)S(1)} %copy-done.8, bf16[256,256]{1,0:T(8,128)(2,1)S(1)} %bitcast.10, f32[256,16]{1,0:T(8,128)S(1)} %copy.8.logs), custom_call_target="tpu_custom_call" | custom-call | flops 1 | bytes 1 | tf_op jit(solution)/shard_map/pallas_call | solution.py:21
  5.0 2.1 %collective-permute-start = (bf16[272,512]{1,0:T(8,128)(2,1)S(1)}, bf16[272,512]{1,0:T(8,128)(2,1)S(1)}, u32[]{:S(2)}, u32[]{:S(2)}) collective-permute-start(bf16[272,512]{1,0:T(8,128)(2,1)S(1)} %get-tuple-element.53), channel_id=1, source_target_pairs={{0,4},{4,0},{8,12},{12,8},{16,20},{20,16},{24,28},{28,24},{1,5},{5... | collective-permute-start | bytes 835592 | tf_op jit(solution)/shard_map/ppermute | solution.py:259
  7.1 1.6 %copy-done.7 = bf16[1024,1024]{1,0:T(8,128)(2,1)S(1)} copy-done((bf16[1024,1024]{1,0:T(8,128)(2,1)S(1)}, bf16[1024,1024]{1,0:T(8,128)(2,1)}, u32[]{:S(2)}) %copy-start.7) | copy-done | bytes 2097176
  9.0 1.0 collective-permute-start.5
  10.0 3.5 %collective-permute-done.refs_1_ = bf16[272,512]{1,0:T(8,128)(2,1)S(1)} collective-permute-done((bf16[272,512]{1,0:T(8,128)(2,1)S(1)}, bf16[272,512]{1,0:T(8,128)(2,1)S(1)}, u32[]{:S(2)}, u32[]{:S(2)}) %collective-permute-start) | collective-permute-done | bytes 278560 | tf_op jit(solution)/shard_map/ppermute | solution.py:259
  14.3 3.1 %collective-permute-start.1 = (bf16[272,512]{1,0:T(8,128)(2,1)S(1)}, bf16[272,512]{1,0:T(8,128)(2,1)S(1)}, u32[]{:S(2)}, u32[]{:S(2)}) collective-permute-start(bf16[272,512]{1,0:T(8,128)(2,1)S(1)} %get-tuple-element.60), channel_id=1, source_target_pairs={{0,8},{4,12},{8,16},{12,20},{16,24},{20,28},{1,9},{5,13},{9,17},{1... | collective-permute-start | bytes 835592 | tf_op jit(solution)/shard_map/ppermute | solution.py:267
  17.5 1.3 collective-permute-start.4
  18.7 3.3 %collective-permute-start.10 = (bf16[640,512]{1,0:T(8,128)(2,1)S(1)}, bf16[640,512]{1,0:T(8,128)(2,1)S(1)}, u32[]{:S(2)}, u32[]{:S(2)}) collective-permute-start(bf16[640,512]{1,0:T(8,128)(2,1)S(1)} %get-tuple-element.59), channel_id=1, source_target_pairs={{0,1},{1,0},{2,3},{3,2},{4,5},{5,4},{6,7},{7,6},{8,9},{9,8},{10,11... | collective-permute-start | bytes 1966088 | tf_op jit(solution)/shard_map/ppermute | solution.py:270
  22.3 1.0 copy-done.6
  23.2 0.9 shard_map.76
  24.7 4.2 %collective-permute-start.3 = (bf16[272,512]{1,0:T(8,128)(2,1)S(1)}, bf16[272,512]{1,0:T(8,128)(2,1)S(1)}, u32[]{:S(2)}, u32[]{:S(2)}) collective-permute-start(bf16[272,512]{1,0:T(8,128)(2,1)S(1)} %get-tuple-element.64), channel_id=1, source_target_pairs={{0,16},{4,20},{8,24},{12,28},{1,17},{5,21},{9,25},{13,29},{2,18},{... | collective-permute-start | bytes 835592 | tf_op jit(solution)/shard_map/ppermute | solution.py:267
  28.9 3.5 %collective-permute-done.3.got = bf16[272,512]{1,0:T(8,128)(2,1)S(1)} collective-permute-done((bf16[272,512]{1,0:T(8,128)(2,1)S(1)}, bf16[272,512]{1,0:T(8,128)(2,1)S(1)}, u32[]{:S(2)}, u32[]{:S(2)}) %collective-permute-start.3) | collective-permute-done | bytes 278560 | tf_op jit(solution)/shard_map/ppermute | solution.py:267
  32.6 3.4 %collective-permute-done.4.refs_3_.refs_9_.refs_7_ = bf16[512,512]{1,0:T(8,128)(2,1)S(1)} collective-permute-done((bf16[512,512]{1,0:T(8,128)(2,1)S(1)}, bf16[512,512]{1,0:T(8,128)(2,1)S(1)}, u32[]{:S(2)}, u32[]{:S(2)}) %collective-permute-start.4) | collective-permute-done | bytes 524320 | tf_op jit(solution)/shard_map/ppermute | solution.py:259
  36.0 8.4 %collective-permute-done.6.refs_4_.refs_10_.refs_8_ = bf16[384,512]{1,0:T(8,128)(2,1)S(1)} collective-permute-done((bf16[384,512]{1,0:T(8,128)(2,1)S(1)}, bf16[384,512]{1,0:T(8,128)(2,1)S(1)}, u32[]{:S(2)}, u32[]{:S(2)}) %collective-permute-start.6) | collective-permute-done | bytes 393248 | tf_op jit(solution)/shard_map/ppermute | solution.py:259
  44.4 1.1 collective-permute-start.7
  45.6 2.9 %shard_map.78 = (f32[256,1024]{1,0:T(8,128)S(1)}, f32[256,1024]{1,0:T(8,128)S(1)}, f32[256,1024]{1,0:T(8,128)S(1)}) custom-call(s32[1]{0:T(128)} %bitcast.1.me, bf16[256,1024]{1,0:T(8,128)(2,1)S(1)} %copy-done.9, bf16[256,1024]{1,0:T(8,128)(2,1)S(1)} %copy-done.12, bf16[256,256]{1,0:T(8,128)(2,1)S(1)} %bitcast.11, bf16[256,256]{1,0:T(8,128)(2,1)S(1)} %bitcast.8, ...), custom_call_target="tpu_custom_call" | custom-call | flops 1 | bytes 1 | tf_op jit(solution)/shard_map/pallas_call | solution.py:21
  48.9 2.1 %collective-permute-done.7.refs_1_ = bf16[256,512]{1,0:T(8,128)(2,1)S(1)} collective-permute-done((bf16[256,512]{1,0:T(8,128)(2,1)S(1)}, bf16[256,512]{1,0:T(8,128)(2,1)S(1)}, u32[]{:S(2)}, u32[]{:S(2)}) %collective-permute-start.7) | collective-permute-done | bytes 262176 | tf_op jit(solution)/shard_map/ppermute | solution.py:259
  51.0 1.3 shard_map.79
  52.3 0.9 collective-permute-start.13
  53.2 1.3 collective-permute-start.14
  54.5 4.4 %collective-permute-start.8 = (bf16[128,1024]{1,0:T(8,128)(2,1)S(1)}, bf16[128,1024]{1,0:T(8,128)(2,1)S(1)}, u32[]{:S(2)}, u32[]{:S(2)}) collective-permute-start(bf16[128,1024]{1,0:T(8,128)(2,1)S(1)} %get-tuple-element.74.refs_0_), channel_id=1, source_target_pairs={{0,1},{1,0},{2,3},{3,2},{4,5},{5,4},{6,7},{7,6},{8,9},{9,8},{10,11... | collective-permute-start | bytes 786440 | tf_op jit(solution)/shard_map/ppermute | solution.py:270
  59.5 1.3 collective-permute-start.19
  60.8 3.2 %collective-permute-done.14.refs_1_ = bf16[128,1024]{1,0:T(8,128)(2,1)} collective-permute-done((bf16[128,1024]{1,0:T(8,128)(2,1)}, bf16[128,1024]{1,0:T(8,128)(2,1)}, u32[]{:S(2)}, u32[]{:S(2)}) %collective-permute-start.14) | collective-permute-done | bytes 262176 | tf_op jit(solution)/shard_map/ppermute | solution.py:263
  64.8 8.1 %collective-permute-start.15 = (bf16[128,1024]{1,0:T(8,128)(2,1)}, bf16[128,1024]{1,0:T(8,128)(2,1)}, u32[]{:S(2)}, u32[]{:S(2)}) collective-permute-start(bf16[128,1024]{1,0:T(8,128)(2,1)} %collective-permute-done.13.refs_0_), channel_id=1, source_target_pairs={{0,1},{1,0},{2,3},{3,2},{4,5},{5,4},{6,7},{7,6},{8,9},{9,8},{10,11... | collective-permute-start | bytes 786440 | tf_op jit(solution)/shard_map/ppermute | solution.py:270
  72.9 1.0 copy-done.1
  74.0 1.0 copy-done.4
  75.0 0.9 copy-done.19
  75.9 0.9 copy-done.21
  76.9 2.7 %shard_map.80 = (f32[2,2,64,512]{3,2,1,0:T(8,128)S(1)}, bf16[2,2,64,512]{3,2,1,0:T(8,128)(2,1)S(1)}) custom-call(s32[1]{0:T(128)} %bitcast.3.me, bf16[128,1024]{1,0:T(8,128)(2,1)S(1)} %copy-done.19, bf16[128,1024]{1,0:T(8,128)(2,1)} %get-tuple-element.75.refs_1_, bf16[128,1024]{1,0:T(8,128)(2,1)S(1)} %copy-done.21, ...), custom_call_target="tpu_custom_call" | custom-call | flops 1 | bytes 1 | tf_op jit(solution)/shard_map/pallas_call | solution.py:21
  80.1 1.3 collective-permute-start.25
  81.8 1.3 collective-permute-start.32
  83.1 1.3 collective-permute-start.12
  84.4 2.7 %shard_map.82 = (f32[2,2,64,512]{3,2,1,0:T(8,128)S(1)}, bf16[2,2,64,512]{3,2,1,0:T(8,128)(2,1)S(1)}) custom-call(s32[1]{0:T(128)} %bitcast.3.me, bf16[128,1024]{1,0:T(8,128)(2,1)} %collective-permute-done.13.refs_0_, bf16[128,1024]{1,0:T(8,128)(2,1)} %collective-permute-done.14.refs_1_, bf16[128,1024]{1,0:T(8,128)(2,1)} %collective-permute-done.15.refs_2_, ...), custom_call_target="tpu_custom_call" | custom-call | flops 1 | bytes 1 | tf_op jit(solution)/shard_map/pallas_call | solution.py:21
  87.4 2.9 %collective-permute-done.25.refs_0_ = bf16[128,1024]{1,0:T(8,128)(2,1)S(1)} collective-permute-done((bf16[128,1024]{1,0:T(8,128)(2,1)S(1)}, bf16[128,1024]{1,0:T(8,128)(2,1)S(1)}, u32[]{:S(2)}, u32[]{:S(2)}) %collective-permute-start.25) | collective-permute-done | bytes 262176 | tf_op jit(solution)/shard_map/ppermute | solution.py:263
  90.3 0.9 collective-permute-start.26
  91.2 2.5 %shard_map.84 = (f32[2,2,64,512]{3,2,1,0:T(8,128)S(1)}, bf16[2,2,64,512]{3,2,1,0:T(8,128)(2,1)S(1)}) custom-call(s32[1]{0:T(128)} %bitcast.3.me, bf16[128,1024]{1,0:T(8,128)(2,1)S(1)} %collective-permute-done.19.refs_0_, bf16[128,1024]{1,0:T(8,128)(2,1)} %collective-permute-done.20.refs_1_, bf16[128,1024]{1,0:T(8,128)(2,1)S(1)} %collective-permute-done.21.refs_2_, ...), custom_call_target="tpu_custom_call" | custom-call | flops 1 | bytes 1 | tf_op jit(solution)/shard_map/pallas_call | solution.py:21
  93.7 0.7 collective-permute-start.23
  94.4 1.5 %collective-permute-done.32.refs_0_ = bf16[128,1024]{1,0:T(8,128)(2,1)S(1)} collective-permute-done((bf16[128,1024]{1,0:T(8,128)(2,1)}, bf16[128,1024]{1,0:T(8,128)(2,1)S(1)}, u32[]{:S(2)}, u32[]{:S(2)}) %collective-permute-start.32) | collective-permute-done | bytes 262176 | tf_op jit(solution)/shard_map/ppermute | solution.py:263
  96.6 0.7 shard_map.83
  97.3 1.5 %collective-permute-start.18 = (bf16[2,2,64,512]{3,2,1,0:T(8,128)(2,1)}, bf16[2,2,64,512]{3,2,1,0:T(8,128)(2,1)}, u32[]{:S(2)}, u32[]{:S(2)}) collective-permute-start(bf16[2,2,64,512]{3,2,1,0:T(8,128)(2,1)} %shard_map.83), channel_id=1, source_target_pairs={{0,24},{4,28},{8,0},{12,4},{16,8},{20,12},{24,16},{28,20},{1,25},{... | collective-permute-start | bytes 786440 | tf_op jit(solution)/shard_map/ppermute | solution.py:263
  98.9 1.0 shard_map.86
  99.8 1.3 collective-permute-start.27
  101.2 1.0 collective-permute-done.23.refs_0_
  102.2 0.7 shard_map.85
  102.9 1.0 collective-permute-start.24
  103.9 1.6 %shard_map.89 = (f32[1,2,64,512]{3,2,1,0:T(8,128)S(1)}, bf16[1,2,64,512]{3,2,1,0:T(8,128)(2,1)}) custom-call(s32[1]{0:T(128)} %bitcast.3.me, bf16[128,1024]{1,0:T(8,128)(2,1)S(1)} %collective-permute-done.32.refs_0_, bf16[128,1024]{1,0:T(8,128)(2,1)S(1)} %collective-permute-done.33.refs_1_, bf16[512,512]{1,0:T(8,128)(2,1)S(1)} %get-tuple-element.56.refs_4_.refs_2_, ...), custom_call_target="tpu_custom_call" | custom-call | flops 1 | bytes 1 | tf_op jit(solution)/shard_map/pallas_call | solution.py:21
  106.2 0.8 collective-permute-start.34
  107.0 1.4 %collective-permute-start.28 = (bf16[1,2,64,512]{3,2,1,0:T(8,128)(2,1)S(1)}, bf16[1,2,64,512]{3,2,1,0:T(8,128)(2,1)S(1)}, u32[]{:S(2)}, u32[]{:S(2)}) collective-permute-start(bf16[1,2,64,512]{3,2,1,0:T(8,128)(2,1)S(1)} %shard_map.87), channel_id=1, source_target_pairs={{0,8},{4,12},{8,16},{12,20},{16,24},{20,28},{24,0},{28,4},{1,9},{5... | collective-permute-start | bytes 393224 | tf_op jit(solution)/shard_map/ppermute | solution.py:263
  108.5 1.8 %collective-permute-done.34.refs_0_ = bf16[1,2,64,512]{3,2,1,0:T(8,128)(2,1)S(1)} collective-permute-done((bf16[1,2,64,512]{3,2,1,0:T(8,128)(2,1)}, bf16[1,2,64,512]{3,2,1,0:T(8,128)(2,1)S(1)}, u32[]{:S(2)}, u32[]{:S(2)}) %collective-permute-start.34) | collective-permute-done | bytes 131104 | tf_op jit(solution)/shard_map/ppermute | solution.py:274
  110.2 0.9 copy-done.17
  111.2 1.4 %collective-permute-start.35 = (bf16[1,2,64,512]{3,2,1,0:T(8,128)(2,1)S(1)}, bf16[1,2,64,512]{3,2,1,0:T(8,128)(2,1)S(1)}, u32[]{:S(2)}, u32[]{:S(2)}) collective-permute-start(bf16[1,2,64,512]{3,2,1,0:T(8,128)(2,1)S(1)} %shard_map.90), channel_id=1, source_target_pairs={{0,8},{4,12},{8,16},{12,20},{16,24},{20,28},{24,0},{28,4},{1,9},{5... | collective-permute-start | bytes 393224 | tf_op jit(solution)/shard_map/ppermute | solution.py:263
  112.7 10.0 %collective-permute-done.24.refs_2_ = bf16[2,2,64,512]{3,2,1,0:T(8,128)(2,1)} collective-permute-done((bf16[2,2,64,512]{3,2,1,0:T(8,128)(2,1)}, bf16[2,2,64,512]{3,2,1,0:T(8,128)(2,1)}, u32[]{:S(2)}, u32[]{:S(2)}) %collective-permute-start.24) | collective-permute-done | bytes 262176 | tf_op jit(solution)/shard_map/ppermute | solution.py:263
  122.7 1.1 shard_map.88
  123.8 2.2 %collective-permute-start.29 = (bf16[2,64,512]{2,1,0:T(8,128)(2,1)S(1)}, bf16[2,64,512]{2,1,0:T(8,128)(2,1)S(1)}, u32[]{:S(2)}, u32[]{:S(2)}) collective-permute-start(bf16[2,64,512]{2,1,0:T(8,128)(2,1)S(1)} %get-tuple-element.88), channel_id=1, source_target_pairs={{0,1},{1,2},{2,3},{3,0},{4,5},{5,6},{6,7},{7,4},{8,9},{9,10},{10,1... | collective-permute-start | bytes 393224 | tf_op jit(solution)/shard_map/ppermute | solution.py:277
  126.6 1.1 shard_map.91
  127.7 1.8 %collective-permute-start.36 = (bf16[2,64,512]{2,1,0:T(8,128)(2,1)S(1)}, bf16[2,64,512]{2,1,0:T(8,128)(2,1)S(1)}, u32[]{:S(2)}, u32[]{:S(2)}) collective-permute-start(bf16[2,64,512]{2,1,0:T(8,128)(2,1)S(1)} %get-tuple-element.96), channel_id=1, source_target_pairs={{0,1},{1,2},{2,3},{3,0},{4,5},{5,6},{6,7},{7,4},{8,9},{9,10},{10,1... | collective-permute-start | bytes 393224 | tf_op jit(solution)/shard_map/ppermute | solution.py:277
  129.5 0.9 collective-permute-start.37
  130.5 2.0 %collective-permute-done.30.refs_2_ = bf16[2,64,512]{2,1,0:T(8,128)(2,1)S(1)} collective-permute-done((bf16[2,64,512]{2,1,0:T(8,128)(2,1)S(1)}, bf16[2,64,512]{2,1,0:T(8,128)(2,1)S(1)}, u32[]{:S(2)}, u32[]{:S(2)}) %collective-permute-start.30) | collective-permute-done | bytes 131104 | tf_op jit(solution)/shard_map/ppermute | solution.py:277
  132.5 1.5 %collective-permute-done.31.refs_3_ = bf16[2,64,512]{2,1,0:T(8,128)(2,1)S(1)} collective-permute-done((bf16[2,64,512]{2,1,0:T(8,128)(2,1)S(1)}, bf16[2,64,512]{2,1,0:T(8,128)(2,1)S(1)}, u32[]{:S(2)}, u32[]{:S(2)}) %collective-permute-start.31) | collective-permute-done | bytes 131104 | tf_op jit(solution)/shard_map/ppermute | solution.py:277
  134.3 3.9 %collective-permute-done.37.refs_6_ = bf16[2,64,512]{2,1,0:T(8,128)(2,1)S(1)} collective-permute-done((bf16[2,64,512]{2,1,0:T(8,128)(2,1)S(1)}, bf16[2,64,512]{2,1,0:T(8,128)(2,1)S(1)}, u32[]{:S(2)}, u32[]{:S(2)}) %collective-permute-start.37) | collective-permute-done | bytes 131104 | tf_op jit(solution)/shard_map/ppermute | solution.py:277
  138.8 1.6 %shard_map.92 = bf16[256,2048]{1,0:T(8,128)(2,1)} custom-call(s32[2]{0:T(128)S(1)} %pad_add_fusion.me, bf16[2,64,512]{2,1,0:T(8,128)(2,1)S(1)} %get-tuple-element.87.refs_0_, bf16[2,64,512]{2,1,0:T(8,128)(2,1)S(1)} %collective-permute-done.29.refs_1_, bf16[2,64,512]{2,1,0:T(8,128)(2,1)S(1)} %collective-permute-done.30.refs_2_, ...), custom_call_target="tpu_custom_call" | custom-call | flops 1 | bytes 1 | tf_op jit(solution)/shard_map/pallas_call | solution.py:21
  (82 shorter events, 8.3 us)
Async XLA Ops:
  0.8 8.1 %copy-start.10 = (f32[256,16]{1,0:T(8,128)}, f32[256,16]{1,0:T(8,128)S(1)}, u32[]{:S(2)}) copy-start(f32[256,16]{1,0:T(8,128)S(1)} %copy.8.logs) | copy-start | bytes 49156
  0.8 1.1 copy-start.8
  1.9 0.9 copy-start.14
  5.0 8.5 %collective-permute-start = (bf16[272,512]{1,0:T(8,128)(2,1)S(1)}, bf16[272,512]{1,0:T(8,128)(2,1)S(1)}, u32[]{:S(2)}, u32[]{:S(2)}) collective-permute-start(bf16[272,512]{1,0:T(8,128)(2,1)S(1)} %get-tuple-element.53), channel_id=1, source_target_pairs={{0,4},{4,0},{8,12},{12,8},{16,20},{20,16},{24,28},{28,24},{1,5},{5... | collective-permute-start | bytes 835592 | tf_op jit(solution)/shard_map/ppermute | solution.py:259
  7.1 1.6 %copy-start.7 = (bf16[1024,1024]{1,0:T(8,128)(2,1)S(1)}, bf16[1024,1024]{1,0:T(8,128)(2,1)}, u32[]{:S(2)}) copy-start(bf16[1024,1024]{1,0:T(8,128)(2,1)} %w_out) | copy-start | bytes 6291460
  8.7 36.8 %copy-start.12 = (bf16[256,1024]{1,0:T(8,128)(2,1)S(1)}, bf16[256,1024]{1,0:T(8,128)(2,1)}, u32[]{:S(2)}) copy-start(bf16[256,1024]{1,0:T(8,128)(2,1)} %z) | copy-start | bytes 1572868
  8.7 36.8 %copy-start.13 = (bf16[256,1,256]{2,0,1:T(8,128)(2,1)S(1)}, bf16[256,1,256]{2,0,1:T(8,128)(2,1)}, u32[]{:S(2)}) copy-start(bf16[256,1,256]{2,0,1:T(8,128)(2,1)} %param.10) | copy-start | bytes 393220
  8.7 36.8 %copy-start.15 = (bf16[256,1,256]{2,0,1:T(8,128)(2,1)S(1)}, bf16[256,1,256]{2,0,1:T(8,128)(2,1)}, u32[]{:S(2)}) copy-start(bf16[256,1,256]{2,0,1:T(8,128)(2,1)} %param.9) | copy-start | bytes 393220
  8.9 39.6 %copy-start = (bf16[512,512]{1,0:T(8,128)(2,1)}, bf16[512,512]{1,0:T(8,128)(2,1)S(1)}, u32[]{:S(2)}) copy-start(bf16[512,512]{1,0:T(8,128)(2,1)S(1)} %get-tuple-element.57.refs_5_.refs_3_) | copy-start | bytes 1572868
  8.9 36.7 %copy-start.9 = (bf16[256,1024]{1,0:T(8,128)(2,1)S(1)}, bf16[256,1024]{1,0:T(8,128)(2,1)}, u32[]{:S(2)}) copy-start(bf16[256,1024]{1,0:T(8,128)(2,1)} %x.3) | copy-start | bytes 1572868
  8.9 15.8 %collective-permute-start.2 = (bf16[512,512]{1,0:T(8,128)(2,1)S(1)}, bf16[512,512]{1,0:T(8,128)(2,1)S(1)}, u32[]{:S(2)}, u32[]{:S(2)}) collective-permute-start(bf16[512,512]{1,0:T(8,128)(2,1)S(1)} %get-tuple-element.56.refs_4_.refs_2_), channel_id=1, source_target_pairs={{0,4},{4,0},{8,12},{12,8},{16,20},{20,16},{24,28},{28,24},{1,5},{5... | collective-permute-start | bytes 1572872 | tf_op jit(solution)/shard_map/ppermute | solution.py:259
  9.0 13.0 %collective-permute-start.5 = (bf16[384,512]{1,0:T(8,128)(2,1)S(1)}, bf16[384,512]{1,0:T(8,128)(2,1)S(1)}, u32[]{:S(2)}, u32[]{:S(2)}) collective-permute-start(bf16[384,512]{1,0:T(8,128)(2,1)S(1)} %get-tuple-element.58), channel_id=1, source_target_pairs={{0,1},{1,0},{2,3},{3,2},{4,5},{5,4},{6,7},{7,6},{8,9},{9,8},{10,11... | collective-permute-start | bytes 1179656 | tf_op jit(solution)/shard_map/ppermute | solution.py:270
  13.6 0.7 copy-start.5
  14.3 7.9 %collective-permute-start.1 = (bf16[272,512]{1,0:T(8,128)(2,1)S(1)}, bf16[272,512]{1,0:T(8,128)(2,1)S(1)}, u32[]{:S(2)}, u32[]{:S(2)}) collective-permute-start(bf16[272,512]{1,0:T(8,128)(2,1)S(1)} %get-tuple-element.60), channel_id=1, source_target_pairs={{0,8},{4,12},{8,16},{12,20},{16,24},{20,28},{1,9},{5,13},{9,17},{1... | collective-permute-start | bytes 835592 | tf_op jit(solution)/shard_map/ppermute | solution.py:267
  17.5 18.5 %collective-permute-start.4 = (bf16[512,512]{1,0:T(8,128)(2,1)S(1)}, bf16[512,512]{1,0:T(8,128)(2,1)S(1)}, u32[]{:S(2)}, u32[]{:S(2)}) collective-permute-start(bf16[512,512]{1,0:T(8,128)(2,1)S(1)} %get-tuple-element.57.refs_5_.refs_3_), channel_id=1, source_target_pairs={{0,4},{4,0},{8,12},{12,8},{16,20},{20,16},{24,28},{28,24},{1,5},{5... | collective-permute-start | bytes 1572872 | tf_op jit(solution)/shard_map/ppermute | solution.py:259
  18.7 29.8 %collective-permute-start.10 = (bf16[640,512]{1,0:T(8,128)(2,1)S(1)}, bf16[640,512]{1,0:T(8,128)(2,1)S(1)}, u32[]{:S(2)}, u32[]{:S(2)}) collective-permute-start(bf16[640,512]{1,0:T(8,128)(2,1)S(1)} %get-tuple-element.59), channel_id=1, source_target_pairs={{0,1},{1,0},{2,3},{3,2},{4,5},{5,4},{6,7},{7,6},{8,9},{9,8},{10,11... | collective-permute-start | bytes 1966088 | tf_op jit(solution)/shard_map/ppermute | solution.py:270
  22.0 22.4 %copy-start.3 = (bf16[384,512]{1,0:T(8,128)(2,1)}, bf16[384,512]{1,0:T(8,128)(2,1)S(1)}, u32[]{:S(2)}) copy-start(bf16[384,512]{1,0:T(8,128)(2,1)S(1)} %collective-permute-done.5.refs_6_.refs_4_) | copy-start | bytes 1179652
  22.0 22.4 %collective-permute-start.6 = (bf16[384,512]{1,0:T(8,128)(2,1)S(1)}, bf16[384,512]{1,0:T(8,128)(2,1)S(1)}, u32[]{:S(2)}, u32[]{:S(2)}) collective-permute-start(bf16[384,512]{1,0:T(8,128)(2,1)S(1)} %collective-permute-done.5.refs_6_.refs_4_), channel_id=1, source_target_pairs={{0,4},{4,0},{8,12},{12,8},{16,20},{20,16},{24,28},{28,24},{1,5},{5... | collective-permute-start | bytes 1179656 | tf_op jit(solution)/shard_map/ppermute | solution.py:259
  22.3 1.0 copy-start.6
  23.2 22.3 %copy-start.11 = (f32[256,16]{1,0:T(8,128)S(1)}, f32[256,16]{1,0:T(8,128)}, u32[]{:S(2)}) copy-start(f32[256,16]{1,0:T(8,128)} %copy-done.10) | copy-start | bytes 49156
  23.2 27.8 %copy-start.22 = (f32[1024]{0:T(1024)S(1)}, f32[1024]{0:T(1024)}, u32[]{:S(2)}) copy-start(f32[1024]{0:T(1024)} %param.12) | copy-start | bytes 12292
  24.7 7.7 %collective-permute-start.3 = (bf16[272,512]{1,0:T(8,128)(2,1)S(1)}, bf16[272,512]{1,0:T(8,128)(2,1)S(1)}, u32[]{:S(2)}, u32[]{:S(2)}) collective-permute-start(bf16[272,512]{1,0:T(8,128)(2,1)S(1)} %get-tuple-element.64), channel_id=1, source_target_pairs={{0,16},{4,20},{8,24},{12,28},{1,17},{5,21},{9,25},{13,29},{2,18},{... | collective-permute-start | bytes 835592 | tf_op jit(solution)/shard_map/ppermute | solution.py:267
  44.4 6.6 %collective-permute-start.7 = (bf16[256,512]{1,0:T(8,128)(2,1)S(1)}, bf16[256,512]{1,0:T(8,128)(2,1)S(1)}, u32[]{:S(2)}, u32[]{:S(2)}) collective-permute-start(bf16[256,512]{1,0:T(8,128)(2,1)S(1)} %get-tuple-element.73), channel_id=1, source_target_pairs={{0,4},{4,0},{8,12},{12,8},{16,20},{20,16},{24,28},{28,24},{1,5},{5... | collective-permute-start | bytes 786440 | tf_op jit(solution)/shard_map/ppermute | solution.py:259
  48.5 24.4 %collective-permute-start.11 = (bf16[640,512]{1,0:T(8,128)(2,1)S(1)}, bf16[640,512]{1,0:T(8,128)(2,1)S(1)}, u32[]{:S(2)}, u32[]{:S(2)}) collective-permute-start(bf16[640,512]{1,0:T(8,128)(2,1)S(1)} %collective-permute-done.10.refs_7_.refs_5_), channel_id=1, source_target_pairs={{0,4},{4,0},{8,12},{12,8},{16,20},{20,16},{24,28},{28,24},{1,5},{5... | collective-permute-start | bytes 1966088 | tf_op jit(solution)/shard_map/ppermute | solution.py:259
  52.3 7.3 %collective-permute-start.13 = (bf16[128,1024]{1,0:T(8,128)(2,1)S(1)}, bf16[128,1024]{1,0:T(8,128)(2,1)}, u32[]{:S(2)}, u32[]{:S(2)}) collective-permute-start(bf16[128,1024]{1,0:T(8,128)(2,1)S(1)} %get-tuple-element.74.refs_0_), channel_id=1, source_target_pairs={{0,8},{4,12},{8,16},{12,20},{16,24},{20,28},{24,0},{28,4},{1,9},{5... | collective-permute-start | bytes 786440 | tf_op jit(solution)/shard_map/ppermute | solution.py:263
  53.2 10.9 %collective-permute-start.14 = (bf16[128,1024]{1,0:T(8,128)(2,1)}, bf16[128,1024]{1,0:T(8,128)(2,1)}, u32[]{:S(2)}, u32[]{:S(2)}) collective-permute-start(bf16[128,1024]{1,0:T(8,128)(2,1)} %get-tuple-element.75.refs_1_), channel_id=1, source_target_pairs={{0,8},{4,12},{8,16},{12,20},{16,24},{20,28},{24,0},{28,4},{1,9},{5... | collective-permute-start | bytes 786440 | tf_op jit(solution)/shard_map/ppermute | solution.py:263
  54.5 9.6 %collective-permute-start.8 = (bf16[128,1024]{1,0:T(8,128)(2,1)S(1)}, bf16[128,1024]{1,0:T(8,128)(2,1)S(1)}, u32[]{:S(2)}, u32[]{:S(2)}) collective-permute-start(bf16[128,1024]{1,0:T(8,128)(2,1)S(1)} %get-tuple-element.74.refs_0_), channel_id=1, source_target_pairs={{0,1},{1,0},{2,3},{3,2},{4,5},{5,4},{6,7},{7,6},{8,9},{9,8},{10,11... | collective-permute-start | bytes 786440 | tf_op jit(solution)/shard_map/ppermute | solution.py:270
  58.8 0.7 copy-start.18
  59.5 13.4 %collective-permute-start.9 = (bf16[128,1024]{1,0:T(8,128)(2,1)}, bf16[128,1024]{1,0:T(8,128)(2,1)}, u32[]{:S(2)}, u32[]{:S(2)}) collective-permute-start(bf16[128,1024]{1,0:T(8,128)(2,1)} %get-tuple-element.75.refs_1_), channel_id=1, source_target_pairs={{0,1},{1,0},{2,3},{3,2},{4,5},{5,4},{6,7},{7,6},{8,9},{9,8},{10,11... | collective-permute-start | bytes 786440 | tf_op jit(solution)/shard_map/ppermute | solution.py:270
  59.5 20.0 %collective-permute-start.19 = (bf16[128,1024]{1,0:T(8,128)(2,1)}, bf16[128,1024]{1,0:T(8,128)(2,1)S(1)}, u32[]{:S(2)}, u32[]{:S(2)}) collective-permute-start(bf16[128,1024]{1,0:T(8,128)(2,1)} %collective-permute-done.13.refs_0_), channel_id=1, source_target_pairs={{0,8},{4,12},{8,16},{12,20},{16,24},{20,28},{24,0},{28,4},{1,9},{5... | collective-permute-start | bytes 786440 | tf_op jit(solution)/shard_map/ppermute | solution.py:263
  64.1 17.4 %collective-permute-start.20 = (bf16[128,1024]{1,0:T(8,128)(2,1)}, bf16[128,1024]{1,0:T(8,128)(2,1)}, u32[]{:S(2)}, u32[]{:S(2)}) collective-permute-start(bf16[128,1024]{1,0:T(8,128)(2,1)} %collective-permute-done.14.refs_1_), channel_id=1, source_target_pairs={{0,8},{4,12},{8,16},{12,20},{16,24},{20,28},{24,0},{28,4},{1,9},{5... | collective-permute-start | bytes 786440 | tf_op jit(solution)/shard_map/ppermute | solution.py:263
  64.1 0.7 copy-start.20
  64.8 17.0 %collective-permute-start.15 = (bf16[128,1024]{1,0:T(8,128)(2,1)}, bf16[128,1024]{1,0:T(8,128)(2,1)}, u32[]{:S(2)}, u32[]{:S(2)}) collective-permute-start(bf16[128,1024]{1,0:T(8,128)(2,1)} %collective-permute-done.13.refs_0_), channel_id=1, source_target_pairs={{0,1},{1,0},{2,3},{3,2},{4,5},{5,4},{6,7},{7,6},{8,9},{9,8},{10,11... | collective-permute-start | bytes 786440 | tf_op jit(solution)/shard_map/ppermute | solution.py:270
  72.9 10.2 %collective-permute-start.16 = (bf16[128,1024]{1,0:T(8,128)(2,1)}, bf16[128,1024]{1,0:T(8,128)(2,1)S(1)}, u32[]{:S(2)}, u32[]{:S(2)}) collective-permute-start(bf16[128,1024]{1,0:T(8,128)(2,1)} %collective-permute-done.14.refs_1_), channel_id=1, source_target_pairs={{0,1},{1,0},{2,3},{3,2},{4,5},{5,4},{6,7},{7,6},{8,9},{9,8},{10,11... | collective-permute-start | bytes 786440 | tf_op jit(solution)/shard_map/ppermute | solution.py:270
  72.9 1.0 copy-start.1
  74.0 1.0 copy-start.4
  75.0 0.9 copy-start.19
  75.9 0.9 copy-start.21
  76.9 7.5 %copy-start.2 = (bf16[512,512]{1,0:T(8,128)(2,1)S(1)}, bf16[512,512]{1,0:T(8,128)(2,1)}, u32[]{:S(2)}) copy-start(bf16[512,512]{1,0:T(8,128)(2,1)} %copy-done) | copy-start | bytes 1572868
  79.5 7.5 %collective-permute-start.21 = (bf16[128,1024]{1,0:T(8,128)(2,1)S(1)}, bf16[128,1024]{1,0:T(8,128)(2,1)S(1)}, u32[]{:S(2)}, u32[]{:S(2)}) collective-permute-start(bf16[128,1024]{1,0:T(8,128)(2,1)S(1)} %collective-permute-done.19.refs_0_), channel_id=1, source_target_pairs={{0,1},{1,0},{2,3},{3,2},{4,5},{5,4},{6,7},{7,6},{8,9},{9,8},{10,11... | collective-permute-start | bytes 786440 | tf_op jit(solution)/shard_map/ppermute | solution.py:270
  80.1 10.2 %collective-permute-start.25 = (bf16[128,1024]{1,0:T(8,128)(2,1)S(1)}, bf16[128,1024]{1,0:T(8,128)(2,1)S(1)}, u32[]{:S(2)}, u32[]{:S(2)}) collective-permute-start(bf16[128,1024]{1,0:T(8,128)(2,1)S(1)} %collective-permute-done.19.refs_0_), channel_id=1, source_target_pairs={{0,8},{4,12},{8,16},{12,20},{16,24},{20,28},{24,0},{28,4},{1,9},{5... | collective-permute-start | bytes 786440 | tf_op jit(solution)/shard_map/ppermute | solution.py:263
  81.4 9.7 %collective-permute-start.22 = (bf16[128,1024]{1,0:T(8,128)(2,1)}, bf16[128,1024]{1,0:T(8,128)(2,1)S(1)}, u32[]{:S(2)}, u32[]{:S(2)}) collective-permute-start(bf16[128,1024]{1,0:T(8,128)(2,1)} %collective-permute-done.20.refs_1_), channel_id=1, source_target_pairs={{0,1},{1,0},{2,3},{3,2},{4,5},{5,4},{6,7},{7,6},{8,9},{9,8},{10,11... | collective-permute-start | bytes 786440 | tf_op jit(solution)/shard_map/ppermute | solution.py:270
  81.8 14.1 %collective-permute-start.32 = (bf16[128,1024]{1,0:T(8,128)(2,1)}, bf16[128,1024]{1,0:T(8,128)(2,1)S(1)}, u32[]{:S(2)}, u32[]{:S(2)}) collective-permute-start(bf16[128,1024]{1,0:T(8,128)(2,1)} %collective-permute-done.20.refs_1_), channel_id=1, source_target_pairs={{0,8},{4,12},{8,16},{12,20},{16,24},{20,28},{24,0},{28,4},{1,9},{5... | collective-permute-start | bytes 786440 | tf_op jit(solution)/shard_map/ppermute | solution.py:263
  83.1 13.4 %collective-permute-start.12 = (bf16[2,2,64,512]{3,2,1,0:T(8,128)(2,1)S(1)}, bf16[2,2,64,512]{3,2,1,0:T(8,128)(2,1)S(1)}, u32[]{:S(2)}, u32[]{:S(2)}) collective-permute-start(bf16[2,2,64,512]{3,2,1,0:T(8,128)(2,1)S(1)} %get-tuple-element.78), channel_id=1, source_target_pairs={{0,2},{1,3},{2,0},{3,1},{4,6},{5,7},{6,4},{7,5},{8,10},{9,11},{10,... | collective-permute-start | bytes 786440 | tf_op jit(solution)/shard_map/ppermute | solution.py:274
  87.1 9.5 %collective-permute-start.17 = (bf16[2,2,64,512]{3,2,1,0:T(8,128)(2,1)S(1)}, bf16[2,2,64,512]{3,2,1,0:T(8,128)(2,1)S(1)}, u32[]{:S(2)}, u32[]{:S(2)}) collective-permute-start(bf16[2,2,64,512]{3,2,1,0:T(8,128)(2,1)S(1)} %get-tuple-element.80), channel_id=1, source_target_pairs={{0,2},{1,3},{2,0},{3,1},{4,6},{5,7},{6,4},{7,5},{8,10},{9,11},{10,... | collective-permute-start | bytes 786440 | tf_op jit(solution)/shard_map/ppermute | solution.py:274
  90.3 8.6 %collective-permute-start.26 = (bf16[128,1024]{1,0:T(8,128)(2,1)S(1)}, bf16[128,1024]{1,0:T(8,128)(2,1)S(1)}, u32[]{:S(2)}, u32[]{:S(2)}) collective-permute-start(bf16[128,1024]{1,0:T(8,128)(2,1)S(1)} %collective-permute-done.25.refs_0_), channel_id=1, source_target_pairs={{0,1},{1,0},{2,3},{3,2},{4,5},{5,4},{6,7},{7,6},{8,9},{9,8},{10,11... | collective-permute-start | bytes 786440 | tf_op jit(solution)/shard_map/ppermute | solution.py:270
  93.7 8.5 %collective-permute-start.23 = (bf16[2,2,64,512]{3,2,1,0:T(8,128)(2,1)S(1)}, bf16[2,2,64,512]{3,2,1,0:T(8,128)(2,1)S(1)}, u32[]{:S(2)}, u32[]{:S(2)}) collective-permute-start(bf16[2,2,64,512]{3,2,1,0:T(8,128)(2,1)S(1)} %get-tuple-element.82), channel_id=1, source_target_pairs={{0,2},{1,3},{2,0},{3,1},{4,6},{5,7},{6,4},{7,5},{8,10},{9,11},{10,... | collective-permute-start | bytes 786440 | tf_op jit(solution)/shard_map/ppermute | solution.py:274
  95.9 8.0 %collective-permute-start.33 = (bf16[128,1024]{1,0:T(8,128)(2,1)S(1)}, bf16[128,1024]{1,0:T(8,128)(2,1)S(1)}, u32[]{:S(2)}, u32[]{:S(2)}) collective-permute-start(bf16[128,1024]{1,0:T(8,128)(2,1)S(1)} %collective-permute-done.32.refs_0_), channel_id=1, source_target_pairs={{0,1},{1,0},{2,3},{3,2},{4,5},{5,4},{6,7},{7,6},{8,9},{9,8},{10,11... | collective-permute-start | bytes 786440 | tf_op jit(solution)/shard_map/ppermute | solution.py:270
  97.3 15.3 %collective-permute-start.18 = (bf16[2,2,64,512]{3,2,1,0:T(8,128)(2,1)}, bf16[2,2,64,512]{3,2,1,0:T(8,128)(2,1)}, u32[]{:S(2)}, u32[]{:S(2)}) collective-permute-start(bf16[2,2,64,512]{3,2,1,0:T(8,128)(2,1)} %shard_map.83), channel_id=1, source_target_pairs={{0,24},{4,28},{8,0},{12,4},{16,8},{20,12},{24,16},{28,20},{1,25},{... | collective-permute-start | bytes 786440 | tf_op jit(solution)/shard_map/ppermute | solution.py:263
  99.8 7.2 %collective-permute-start.27 = (bf16[1,2,64,512]{3,2,1,0:T(8,128)(2,1)S(1)}, bf16[1,2,64,512]{3,2,1,0:T(8,128)(2,1)S(1)}, u32[]{:S(2)}, u32[]{:S(2)}) collective-permute-start(bf16[1,2,64,512]{3,2,1,0:T(8,128)(2,1)S(1)} %get-tuple-element.86), channel_id=1, source_target_pairs={{0,2},{1,3},{2,0},{3,1},{4,6},{5,7},{6,4},{7,5},{8,10},{9,11},{10,... | collective-permute-start | bytes 393224 | tf_op jit(solution)/shard_map/ppermute | solution.py:274
  102.9 19.8 %collective-permute-start.24 = (bf16[2,2,64,512]{3,2,1,0:T(8,128)(2,1)}, bf16[2,2,64,512]{3,2,1,0:T(8,128)(2,1)}, u32[]{:S(2)}, u32[]{:S(2)}) collective-permute-start(bf16[2,2,64,512]{3,2,1,0:T(8,128)(2,1)} %shard_map.85), channel_id=1, source_target_pairs={{0,16},{4,20},{8,24},{12,28},{16,0},{20,4},{24,8},{28,12},{1,17},{... | collective-permute-start | bytes 786440 | tf_op jit(solution)/shard_map/ppermute | solution.py:263
  105.5 0.7 copy-start.16
  106.2 4.0 %collective-permute-start.34 = (bf16[1,2,64,512]{3,2,1,0:T(8,128)(2,1)}, bf16[1,2,64,512]{3,2,1,0:T(8,128)(2,1)S(1)}, u32[]{:S(2)}, u32[]{:S(2)}) collective-permute-start(bf16[1,2,64,512]{3,2,1,0:T(8,128)(2,1)} %get-tuple-element.94), channel_id=1, source_target_pairs={{0,2},{1,3},{2,0},{3,1},{4,6},{5,7},{6,4},{7,5},{8,10},{9,11},{10,... | collective-permute-start | bytes 393224 | tf_op jit(solution)/shard_map/ppermute | solution.py:274
  107.0 15.7 %collective-permute-start.28 = (bf16[1,2,64,512]{3,2,1,0:T(8,128)(2,1)S(1)}, bf16[1,2,64,512]{3,2,1,0:T(8,128)(2,1)S(1)}, u32[]{:S(2)}, u32[]{:S(2)}) collective-permute-start(bf16[1,2,64,512]{3,2,1,0:T(8,128)(2,1)S(1)} %shard_map.87), channel_id=1, source_target_pairs={{0,8},{4,12},{8,16},{12,20},{16,24},{20,28},{24,0},{28,4},{1,9},{5... | collective-permute-start | bytes 393224 | tf_op jit(solution)/shard_map/ppermute | solution.py:263
  110.2 1.0 copy-start.17
  111.2 15.4 %collective-permute-start.35 = (bf16[1,2,64,512]{3,2,1,0:T(8,128)(2,1)S(1)}, bf16[1,2,64,512]{3,2,1,0:T(8,128)(2,1)S(1)}, u32[]{:S(2)}, u32[]{:S(2)}) collective-permute-start(bf16[1,2,64,512]{3,2,1,0:T(8,128)(2,1)S(1)} %shard_map.90), channel_id=1, source_target_pairs={{0,8},{4,12},{8,16},{12,20},{16,24},{20,28},{24,0},{28,4},{1,9},{5... | collective-permute-start | bytes 393224 | tf_op jit(solution)/shard_map/ppermute | solution.py:263
  123.8 6.5 %collective-permute-start.29 = (bf16[2,64,512]{2,1,0:T(8,128)(2,1)S(1)}, bf16[2,64,512]{2,1,0:T(8,128)(2,1)S(1)}, u32[]{:S(2)}, u32[]{:S(2)}) collective-permute-start(bf16[2,64,512]{2,1,0:T(8,128)(2,1)S(1)} %get-tuple-element.88), channel_id=1, source_target_pairs={{0,1},{1,2},{2,3},{3,0},{4,5},{5,6},{6,7},{7,4},{8,9},{9,10},{10,1... | collective-permute-start | bytes 393224 | tf_op jit(solution)/shard_map/ppermute | solution.py:277
  126.0 6.6 %collective-permute-start.30 = (bf16[2,64,512]{2,1,0:T(8,128)(2,1)S(1)}, bf16[2,64,512]{2,1,0:T(8,128)(2,1)S(1)}, u32[]{:S(2)}, u32[]{:S(2)}) collective-permute-start(bf16[2,64,512]{2,1,0:T(8,128)(2,1)S(1)} %get-tuple-element.89), channel_id=1, source_target_pairs={{0,2},{1,3},{2,0},{3,1},{4,6},{5,7},{6,4},{7,5},{8,10},{9,11},{10,... | collective-permute-start | bytes 393224 | tf_op jit(solution)/shard_map/ppermute | solution.py:277
  126.6 7.5 %collective-permute-start.31 = (bf16[2,64,512]{2,1,0:T(8,128)(2,1)S(1)}, bf16[2,64,512]{2,1,0:T(8,128)(2,1)S(1)}, u32[]{:S(2)}, u32[]{:S(2)}) collective-permute-start(bf16[2,64,512]{2,1,0:T(8,128)(2,1)S(1)} %get-tuple-element.90), channel_id=1, source_target_pairs={{0,3},{1,0},{2,1},{3,2},{4,7},{5,4},{6,5},{7,6},{8,11},{9,8},{10,9... | collective-permute-start | bytes 393224 | tf_op jit(solution)/shard_map/ppermute | solution.py:277
  127.7 6.6 %collective-permute-start.36 = (bf16[2,64,512]{2,1,0:T(8,128)(2,1)S(1)}, bf16[2,64,512]{2,1,0:T(8,128)(2,1)S(1)}, u32[]{:S(2)}, u32[]{:S(2)}) collective-permute-start(bf16[2,64,512]{2,1,0:T(8,128)(2,1)S(1)} %get-tuple-element.96), channel_id=1, source_target_pairs={{0,1},{1,2},{2,3},{3,0},{4,5},{5,6},{6,7},{7,4},{8,9},{9,10},{10,1... | collective-permute-start | bytes 393224 | tf_op jit(solution)/shard_map/ppermute | solution.py:277
  129.5 8.7 %collective-permute-start.37 = (bf16[2,64,512]{2,1,0:T(8,128)(2,1)S(1)}, bf16[2,64,512]{2,1,0:T(8,128)(2,1)S(1)}, u32[]{:S(2)}, u32[]{:S(2)}) collective-permute-start(bf16[2,64,512]{2,1,0:T(8,128)(2,1)S(1)} %get-tuple-element.97), channel_id=1, source_target_pairs={{0,2},{1,3},{2,0},{3,1},{4,6},{5,7},{6,4},{7,5},{8,10},{9,11},{10,... | collective-permute-start | bytes 393224 | tf_op jit(solution)/shard_map/ppermute | solution.py:277
  130.3 8.4 %collective-permute-start.38 = (bf16[2,64,512]{2,1,0:T(8,128)(2,1)S(1)}, bf16[2,64,512]{2,1,0:T(8,128)(2,1)S(1)}, u32[]{:S(2)}, u32[]{:S(2)}) collective-permute-start(bf16[2,64,512]{2,1,0:T(8,128)(2,1)S(1)} %get-tuple-element.98), channel_id=1, source_target_pairs={{0,3},{1,0},{2,1},{3,2},{4,7},{5,4},{6,5},{7,6},{8,11},{9,8},{10,9... | collective-permute-start | bytes 393224 | tf_op jit(solution)/shard_map/ppermute | solution.py:277

commit v4 on v3

--- a/solution.py
+++ b/solution.py
@@ -11,7 +11,7 @@
 HIGH = lax.Precision.HIGHEST
 TAIL = 16
 CHUNKS = 2
-MINE, OTHER, EARLY = (4, 4), (3, 5), 3
+MINE, OTHER, EARLY = (4, 4), (3, 2, 3), 3
 
 
 def call(kernel, out_shapes, args, scratch=(), traffic=1, resident=0):
@@ -347,8 +347,8 @@
         if k + 1 < n_head:
             hidden = [rot_h(after(v, *outs[: max(t - 1, 0)]), 1) for v in hidden]
         other = [swap_core(v) for v in now]
-        if t > 2:
-            other[0] = after(other[0], sums[t - 3])
+        if t == 2:
+            other[0] = after(other[0], sums[0])
         shape = (len(chunks), r, piece, width)
         mine, *send = call(
             functools.partial(product_kernel, r, n_y, len(chunks)),

time: 141 us -> 142 us (level)
  local copies, waits for them, and re-layouts: 13.1 us -> 14.7 us
    ppermute x10, starting transfers between devices: 11.5 us -> 9.03 us  [rot_h(): return lax.ppermute(v, 'seq', pairs)]
    ppermute x10, waiting for transfers between devices: 17.6 us -> 15.3 us  [rot_h(): return lax.ppermute(v, 'seq', pairs)]
    ppermute x5, waiting for transfers between devices: 2.76 us -> 4.92 us  [rot_y(): return lax.ppermute(v, 'head', pairs)]
    ppermute x6 -> x7, waiting for transfers between devices: 18 us -> 19.8 us  [rot_b(): return lax.ppermute(v, 'seq', pairs)]
    unnamed x47 -> x51, local copies, waits for them, and re-layouts: 13.1 us -> 14.7 us
    ppermute x10 -> x11, starting transfers between devices: 19.2 us -> 20.4 us  [swap_core(): return lax.ppermute(v, 'head', [(i, i ^ 1) for i in range(n_head)])]
    ppermute x6 -> x7, starting transfers between devices: 5.25 us -> 6.15 us  [rot_b(): return lax.ppermute(v, 'seq', pairs)]
  transfers between devices with their start and end apart: 39 -> 41, of which waited for: 17 -> 19; matrix products, arithmetic and copies ran while one was open for 0% -> 0% of each run, Pallas kernels for 14% -> 14%
where the time goes in v4:
time: 142 us
  starting transfers between devices  52 us (37%)
  waiting for transfers between devices  50.7 us (36%)
  Pallas kernels  23.7 us (17%)
  local copies, waits for them, and re-layouts  14.7 us (10%)
    pallas_call x20, Pallas kernels, call(): pl.pallas_call(kernel, out_shape=[jax.ShapeDtypeStruct(s, d) for s, d in...  23.7 us
    ppermute x11, starting transfers between devices, swap_core(): return lax.ppermute(v, 'head', [(i, i ^ 1) for i in range(n_head)])  20.4 us
    ppermute x7, waiting for transfers between devices, rot_b(): return lax.ppermute(v, 'seq', pairs)  19.8 us
    ppermute x10, waiting for transfers between devices, rot_h(): return lax.ppermute(v, 'seq', pairs)  15.3 us
    unnamed x51, local copies, waits for them, and re-layouts  14.7 us
    ppermute x10, starting transfers between devices, rot_h(): return lax.ppermute(v, 'seq', pairs)  9.03 us
    ppermute x6, waiting for transfers between devices, rot_head(): lax.ppermute(v, 'head', [(i, (i + j) % n_head) for i in range(n_head)])  8.27 us
    ppermute x2, starting transfers between devices, shift_h(): return lax.ppermute(v, 'seq', pairs)  7.3 us
  transfers between devices with their start and end apart: 41, of which 19 were waited for; matrix products, arithmetic and copies ran while one was open for 0% of the time, Pallas kernels for 14%

profile of v4, /device:TPU:1, one launch (start us, length us, event | category | flops | bytes accessed | tf_op | source)
XLA Modules:
  0.0 141.5 jit_solution(10390046960983305175)
XLA Ops:
  0.0 0.8 copy.8.logs
  0.8 1.1 copy-done.10
  1.9 0.9 copy-done.16
  2.8 2.2 %shard_map.73 = (bf16[272,512]{1,0:T(8,128)(2,1)S(1)}, bf16[272,512]{1,0:T(8,128)(2,1)S(1)}) custom-call(s32[1]{0:T(128)} %bitcast.1.me, bf16[256,1024]{1,0:T(8,128)(2,1)S(1)} %copy-done.10, bf16[256,256]{1,0:T(8,128)(2,1)S(1)} %bitcast.10, f32[256,16]{1,0:T(8,128)S(1)} %copy.8.logs), custom_call_target="tpu_custom_call" | custom-call | flops 1 | bytes 1 | tf_op jit(solution)/shard_map/pallas_call | solution.py:21
  5.0 2.1 %collective-permute-start = (bf16[272,512]{1,0:T(8,128)(2,1)S(1)}, bf16[272,512]{1,0:T(8,128)(2,1)S(1)}, u32[]{:S(2)}, u32[]{:S(2)}) collective-permute-start(bf16[272,512]{1,0:T(8,128)(2,1)S(1)} %get-tuple-element.54), channel_id=1, source_target_pairs={{0,4},{4,0},{8,12},{12,8},{16,20},{20,16},{24,28},{28,24},{1,5},{5... | collective-permute-start | bytes 835592 | tf_op jit(solution)/shard_map/ppermute | solution.py:259
  7.1 1.6 %copy-done.9 = bf16[1024,1024]{1,0:T(8,128)(2,1)S(1)} copy-done((bf16[1024,1024]{1,0:T(8,128)(2,1)S(1)}, bf16[1024,1024]{1,0:T(8,128)(2,1)}, u32[]{:S(2)}) %copy-start.9) | copy-done | bytes 2097176
  9.0 1.0 collective-permute-start.5
  10.0 3.5 %collective-permute-done.refs_1_ = bf16[272,512]{1,0:T(8,128)(2,1)S(1)} collective-permute-done((bf16[272,512]{1,0:T(8,128)(2,1)S(1)}, bf16[272,512]{1,0:T(8,128)(2,1)S(1)}, u32[]{:S(2)}, u32[]{:S(2)}) %collective-permute-start) | collective-permute-done | bytes 278560 | tf_op jit(solution)/shard_map/ppermute | solution.py:259
  13.6 3.2 %collective-permute-start.1 = (bf16[272,512]{1,0:T(8,128)(2,1)S(1)}, bf16[272,512]{1,0:T(8,128)(2,1)S(1)}, u32[]{:S(2)}, u32[]{:S(2)}) collective-permute-start(bf16[272,512]{1,0:T(8,128)(2,1)S(1)} %get-tuple-element.62), channel_id=1, source_target_pairs={{0,8},{4,12},{8,16},{12,20},{16,24},{20,28},{1,9},{5,13},{9,17},{1... | collective-permute-start | bytes 835592 | tf_op jit(solution)/shard_map/ppermute | solution.py:267
  16.8 1.3 collective-permute-start.4
  18.3 1.9 %collective-permute-done.1.got = bf16[272,512]{1,0:T(8,128)(2,1)S(1)} collective-permute-done((bf16[272,512]{1,0:T(8,128)(2,1)S(1)}, bf16[272,512]{1,0:T(8,128)(2,1)S(1)}, u32[]{:S(2)}, u32[]{:S(2)}) %collective-permute-start.1) | collective-permute-done | bytes 278560 | tf_op jit(solution)/shard_map/ppermute | solution.py:267
  20.2 0.9 shard_map.76
  21.1 3.6 %collective-permute-done.2.refs_2_.refs_9_.refs_7_ = bf16[512,512]{1,0:T(8,128)(2,1)S(1)} collective-permute-done((bf16[512,512]{1,0:T(8,128)(2,1)S(1)}, bf16[512,512]{1,0:T(8,128)(2,1)S(1)}, u32[]{:S(2)}, u32[]{:S(2)}) %collective-permute-start.2) | collective-permute-done | bytes 524320 | tf_op jit(solution)/shard_map/ppermute | solution.py:259
  24.8 4.2 %collective-permute-start.3 = (bf16[272,512]{1,0:T(8,128)(2,1)S(1)}, bf16[272,512]{1,0:T(8,128)(2,1)S(1)}, u32[]{:S(2)}, u32[]{:S(2)}) collective-permute-start(bf16[272,512]{1,0:T(8,128)(2,1)S(1)} %get-tuple-element.66), channel_id=1, source_target_pairs={{0,16},{4,20},{8,24},{12,28},{1,17},{5,21},{9,25},{13,29},{2,18},{... | collective-permute-start | bytes 835592 | tf_op jit(solution)/shard_map/ppermute | solution.py:267
  28.9 3.0 %collective-permute-start.11 = (bf16[384,512]{1,0:T(8,128)(2,1)S(1)}, bf16[384,512]{1,0:T(8,128)(2,1)S(1)}, u32[]{:S(2)}, u32[]{:S(2)}) collective-permute-start(bf16[384,512]{1,0:T(8,128)(2,1)S(1)} %get-tuple-element.61), channel_id=1, source_target_pairs={{0,1},{1,0},{2,3},{3,2},{4,5},{5,4},{6,7},{7,6},{8,9},{9,8},{10,11... | collective-permute-start | bytes 1179656 | tf_op jit(solution)/shard_map/ppermute | solution.py:270
  32.4 1.0 copy-done.6
  33.6 2.4 %collective-permute-done.4.refs_3_.refs_10_.refs_8_ = bf16[512,512]{1,0:T(8,128)(2,1)S(1)} collective-permute-done((bf16[512,512]{1,0:T(8,128)(2,1)S(1)}, bf16[512,512]{1,0:T(8,128)(2,1)S(1)}, u32[]{:S(2)}, u32[]{:S(2)}) %collective-permute-start.4) | collective-permute-done | bytes 524320 | tf_op jit(solution)/shard_map/ppermute | solution.py:259
  36.0 8.4 %collective-permute-done.6.refs_4_.refs_11_.refs_9_ = bf16[384,512]{1,0:T(8,128)(2,1)S(1)} collective-permute-done((bf16[384,512]{1,0:T(8,128)(2,1)S(1)}, bf16[384,512]{1,0:T(8,128)(2,1)S(1)}, u32[]{:S(2)}, u32[]{:S(2)}) %collective-permute-start.6) | collective-permute-done | bytes 393248 | tf_op jit(solution)/shard_map/ppermute | solution.py:259
  44.4 1.1 collective-permute-start.7
  45.6 1.8 %collective-permute-start.10 = (bf16[256,512]{1,0:T(8,128)(2,1)S(1)}, bf16[256,512]{1,0:T(8,128)(2,1)S(1)}, u32[]{:S(2)}, u32[]{:S(2)}) collective-permute-start(bf16[256,512]{1,0:T(8,128)(2,1)S(1)} %get-tuple-element.60), channel_id=1, source_target_pairs={{0,1},{1,0},{2,3},{3,2},{4,5},{5,4},{6,7},{7,6},{8,9},{9,8},{10,11... | collective-permute-start | bytes 786440 | tf_op jit(solution)/shard_map/ppermute | solution.py:270
  47.4 2.9 %shard_map.78 = (f32[256,1024]{1,0:T(8,128)S(1)}, f32[256,1024]{1,0:T(8,128)S(1)}, f32[256,1024]{1,0:T(8,128)S(1)}) custom-call(s32[1]{0:T(128)} %bitcast.1.me, bf16[256,1024]{1,0:T(8,128)(2,1)S(1)} %copy-done.11, bf16[256,1024]{1,0:T(8,128)(2,1)S(1)} %copy-done.14, bf16[256,256]{1,0:T(8,128)(2,1)S(1)} %bitcast.11, bf16[256,256]{1,0:T(8,128)(2,1)S(1)} %bitcast.8, ...), custom_call_target="tpu_custom_call" | custom-call | flops 1 | bytes 1 | tf_op jit(solution)/shard_map/pallas_call | solution.py:21
  51.0 1.3 shard_map.79
  52.3 1.0 collective-permute-start.15
  53.2 1.2 collective-permute-start.12
  54.4 1.3 collective-permute-start.16
  55.7 3.7 %collective-permute-start.8 = (bf16[128,1024]{1,0:T(8,128)(2,1)S(1)}, bf16[128,1024]{1,0:T(8,128)(2,1)S(1)}, u32[]{:S(2)}, u32[]{:S(2)}) collective-permute-start(bf16[128,1024]{1,0:T(8,128)(2,1)S(1)} %get-tuple-element.76.refs_0_), channel_id=1, source_target_pairs={{0,1},{1,0},{2,3},{3,2},{4,5},{5,4},{6,7},{7,6},{8,9},{9,8},{10,11... | collective-permute-start | bytes 786440 | tf_op jit(solution)/shard_map/ppermute | solution.py:270
  60.2 5.4 %collective-permute-start.9 = (bf16[128,1024]{1,0:T(8,128)(2,1)}, bf16[128,1024]{1,0:T(8,128)(2,1)}, u32[]{:S(2)}, u32[]{:S(2)}) collective-permute-start(bf16[128,1024]{1,0:T(8,128)(2,1)} %get-tuple-element.77.refs_1_), channel_id=1, source_target_pairs={{0,1},{1,0},{2,3},{3,2},{4,5},{5,4},{6,7},{7,6},{8,9},{9,8},{10,11... | collective-permute-start | bytes 786440 | tf_op jit(solution)/shard_map/ppermute | solution.py:270
  65.6 1.3 collective-permute-done.12.refs_12_.refs_10_
  67.5 1.2 collective-permute-start.21
  68.7 1.1 collective-permute-start.17
  70.6 1.3 collective-permute-start.22
  72.9 1.0 copy-done.1
  73.9 0.9 copy-done.4
  74.8 0.9 copy-done.21
  75.8 0.9 copy-done.23
  76.7 2.7 %shard_map.80 = (f32[2,2,64,512]{3,2,1,0:T(8,128)S(1)}, bf16[2,2,64,512]{3,2,1,0:T(8,128)(2,1)S(1)}) custom-call(s32[1]{0:T(128)} %bitcast.3.me, bf16[128,1024]{1,0:T(8,128)(2,1)S(1)} %copy-done.21, bf16[128,1024]{1,0:T(8,128)(2,1)} %get-tuple-element.77.refs_1_, bf16[128,1024]{1,0:T(8,128)(2,1)S(1)} %copy-done.23, ...), custom_call_target="tpu_custom_call" | custom-call | flops 1 | bytes 1 | tf_op jit(solution)/shard_map/pallas_call | solution.py:21
  79.4 1.3 collective-permute-start.14
  81.2 1.3 collective-permute-start.27
  82.5 1.5 %collective-permute-start.24 = (bf16[128,1024]{1,0:T(8,128)(2,1)}, bf16[128,1024]{1,0:T(8,128)(2,1)S(1)}, u32[]{:S(2)}, u32[]{:S(2)}) collective-permute-start(bf16[128,1024]{1,0:T(8,128)(2,1)} %collective-permute-done.22.refs_1_), channel_id=1, source_target_pairs={{0,1},{1,0},{2,3},{3,2},{4,5},{5,4},{6,7},{7,6},{8,9},{9,8},{10,11... | collective-permute-start | bytes 786440 | tf_op jit(solution)/shard_map/ppermute | solution.py:270
  84.0 2.8 %shard_map.82 = (f32[2,2,64,512]{3,2,1,0:T(8,128)S(1)}, bf16[2,2,64,512]{3,2,1,0:T(8,128)(2,1)S(1)}) custom-call(s32[1]{0:T(128)} %bitcast.3.me, bf16[128,1024]{1,0:T(8,128)(2,1)} %collective-permute-done.15.refs_0_, bf16[128,1024]{1,0:T(8,128)(2,1)} %collective-permute-done.16.refs_1_, bf16[128,1024]{1,0:T(8,128)(2,1)} %collective-permute-done.17.refs_2_, ...), custom_call_target="tpu_custom_call" | custom-call | flops 1 | bytes 1 | tf_op jit(solution)/shard_map/pallas_call | solution.py:21
  87.1 1.3 collective-permute-start.19
  88.5 2.6 %collective-permute-done.27.refs_0_ = bf16[128,1024]{1,0:T(8,128)(2,1)S(1)} collective-permute-done((bf16[128,1024]{1,0:T(8,128)(2,1)}, bf16[128,1024]{1,0:T(8,128)(2,1)S(1)}, u32[]{:S(2)}, u32[]{:S(2)}) %collective-permute-start.27) | collective-permute-done | bytes 262176 | tf_op jit(solution)/shard_map/ppermute | solution.py:263
  91.1 1.3 collective-permute-start.28
  92.4 2.6 %shard_map.84 = (f32[2,2,64,512]{3,2,1,0:T(8,128)S(1)}, bf16[2,2,64,512]{3,2,1,0:T(8,128)(2,1)S(1)}) custom-call(s32[1]{0:T(128)} %bitcast.3.me, bf16[128,1024]{1,0:T(8,128)(2,1)} %collective-permute-done.21.refs_0_, bf16[128,1024]{1,0:T(8,128)(2,1)} %collective-permute-done.22.refs_1_, bf16[128,1024]{1,0:T(8,128)(2,1)S(1)} %collective-permute-done.23.refs_2_, ...), custom_call_target="tpu_custom_call" | custom-call | flops 1 | bytes 1 | tf_op jit(solution)/shard_map/pallas_call | solution.py:21
  95.3 1.4 collective-permute-done.34.refs_0_
  96.7 0.8 collective-permute-start.35
  98.5 1.0 shard_map.86
  99.5 1.3 collective-permute-start.29
  100.8 2.3 %collective-permute-done.25.refs_0_ = bf16[2,2,64,512]{3,2,1,0:T(8,128)(2,1)S(1)} collective-permute-done((bf16[2,2,64,512]{3,2,1,0:T(8,128)(2,1)S(1)}, bf16[2,2,64,512]{3,2,1,0:T(8,128)(2,1)S(1)}, u32[]{:S(2)}, u32[]{:S(2)}) %collective-permute-start.25) | collective-permute-done | bytes 262176 | tf_op jit(solution)/shard_map/ppermute | solution.py:274
  103.9 1.6 %shard_map.89 = (f32[1,2,64,512]{3,2,1,0:T(8,128)S(1)}, bf16[1,2,64,512]{3,2,1,0:T(8,128)(2,1)}) custom-call(s32[1]{0:T(128)} %bitcast.3.me, bf16[128,1024]{1,0:T(8,128)(2,1)S(1)} %collective-permute-done.34.refs_0_, bf16[128,1024]{1,0:T(8,128)(2,1)S(1)} %collective-permute-done.35.refs_1_, bf16[512,512]{1,0:T(8,128)(2,1)S(1)} %get-tuple-element.57.refs_4_.refs_2_, ...), custom_call_target="tpu_custom_call" | custom-call | flops 1 | bytes 1 | tf_op jit(solution)/shard_map/pallas_call | solution.py:21
  106.5 1.6 %collective-permute-start.30 = (bf16[1,2,64,512]{3,2,1,0:T(8,128)(2,1)S(1)}, bf16[1,2,64,512]{3,2,1,0:T(8,128)(2,1)S(1)}, u32[]{:S(2)}, u32[]{:S(2)}) collective-permute-start(bf16[1,2,64,512]{3,2,1,0:T(8,128)(2,1)S(1)} %shard_map.87), channel_id=1, source_target_pairs={{0,8},{4,12},{8,16},{12,20},{16,24},{20,28},{24,0},{28,4},{1,9},{5... | collective-permute-start | bytes 393224 | tf_op jit(solution)/shard_map/ppermute | solution.py:263
  108.1 2.2 %collective-permute-done.36.refs_0_ = bf16[1,2,64,512]{3,2,1,0:T(8,128)(2,1)S(1)} collective-permute-done((bf16[1,2,64,512]{3,2,1,0:T(8,128)(2,1)}, bf16[1,2,64,512]{3,2,1,0:T(8,128)(2,1)S(1)}, u32[]{:S(2)}, u32[]{:S(2)}) %collective-permute-start.36) | collective-permute-done | bytes 131104 | tf_op jit(solution)/shard_map/ppermute | solution.py:274
  110.3 0.9 copy-done.19
  111.3 1.3 collective-permute-start.37
  112.5 11.3 %collective-permute-done.26.refs_2_ = bf16[2,2,64,512]{3,2,1,0:T(8,128)(2,1)} collective-permute-done((bf16[2,2,64,512]{3,2,1,0:T(8,128)(2,1)}, bf16[2,2,64,512]{3,2,1,0:T(8,128)(2,1)}, u32[]{:S(2)}, u32[]{:S(2)}) %collective-permute-start.26) | collective-permute-done | bytes 262176 | tf_op jit(solution)/shard_map/ppermute | solution.py:263
  123.8 0.9 copy-done.8
  124.8 1.1 shard_map.88
  125.8 1.1 collective-permute-start.31
  127.8 1.1 shard_map.91
  128.8 1.8 %collective-permute-start.38 = (bf16[2,64,512]{2,1,0:T(8,128)(2,1)S(1)}, bf16[2,64,512]{2,1,0:T(8,128)(2,1)S(1)}, u32[]{:S(2)}, u32[]{:S(2)}) collective-permute-start(bf16[2,64,512]{2,1,0:T(8,128)(2,1)S(1)} %get-tuple-element.98), channel_id=1, source_target_pairs={{0,1},{1,2},{2,3},{3,0},{4,5},{5,6},{6,7},{7,4},{8,9},{9,10},{10,1... | collective-permute-start | bytes 393224 | tf_op jit(solution)/shard_map/ppermute | solution.py:277
  131.7 2.0 %collective-permute-done.32.refs_2_ = bf16[2,64,512]{2,1,0:T(8,128)(2,1)S(1)} collective-permute-done((bf16[2,64,512]{2,1,0:T(8,128)(2,1)S(1)}, bf16[2,64,512]{2,1,0:T(8,128)(2,1)S(1)}, u32[]{:S(2)}, u32[]{:S(2)}) %collective-permute-start.32) | collective-permute-done | bytes 131104 | tf_op jit(solution)/shard_map/ppermute | solution.py:277
  133.7 1.5 %collective-permute-done.33.refs_3_ = bf16[2,64,512]{2,1,0:T(8,128)(2,1)S(1)} collective-permute-done((bf16[2,64,512]{2,1,0:T(8,128)(2,1)S(1)}, bf16[2,64,512]{2,1,0:T(8,128)(2,1)S(1)}, u32[]{:S(2)}, u32[]{:S(2)}) %collective-permute-start.33) | collective-permute-done | bytes 131104 | tf_op jit(solution)/shard_map/ppermute | solution.py:277
  135.3 4.1 %collective-permute-done.39.refs_6_ = bf16[2,64,512]{2,1,0:T(8,128)(2,1)S(1)} collective-permute-done((bf16[2,64,512]{2,1,0:T(8,128)(2,1)S(1)}, bf16[2,64,512]{2,1,0:T(8,128)(2,1)S(1)}, u32[]{:S(2)}, u32[]{:S(2)}) %collective-permute-start.39) | collective-permute-done | bytes 131104 | tf_op jit(solution)/shard_map/ppermute | solution.py:277
  139.9 1.6 %shard_map.92 = bf16[256,2048]{1,0:T(8,128)(2,1)} custom-call(s32[2]{0:T(128)S(1)} %pad_add_fusion.me, bf16[2,64,512]{2,1,0:T(8,128)(2,1)S(1)} %get-tuple-element.90.refs_0_, bf16[2,64,512]{2,1,0:T(8,128)(2,1)S(1)} %collective-permute-done.31.refs_1_, bf16[2,64,512]{2,1,0:T(8,128)(2,1)S(1)} %collective-permute-done.32.refs_2_, ...), custom_call_target="tpu_custom_call" | custom-call | flops 1 | bytes 1 | tf_op jit(solution)/shard_map/pallas_call | solution.py:21
  (90 shorter events, 11.6 us)
Async XLA Ops:
  0.8 8.1 %copy-start.12 = (f32[256,16]{1,0:T(8,128)}, f32[256,16]{1,0:T(8,128)S(1)}, u32[]{:S(2)}) copy-start(f32[256,16]{1,0:T(8,128)S(1)} %copy.8.logs) | copy-start | bytes 49156
  0.8 1.1 copy-start.10
  1.9 0.9 copy-start.16
  5.0 8.5 %collective-permute-start = (bf16[272,512]{1,0:T(8,128)(2,1)S(1)}, bf16[272,512]{1,0:T(8,128)(2,1)S(1)}, u32[]{:S(2)}, u32[]{:S(2)}) collective-permute-start(bf16[272,512]{1,0:T(8,128)(2,1)S(1)} %get-tuple-element.54), channel_id=1, source_target_pairs={{0,4},{4,0},{8,12},{12,8},{16,20},{20,16},{24,28},{28,24},{1,5},{5... | collective-permute-start | bytes 835592 | tf_op jit(solution)/shard_map/ppermute | solution.py:259
  7.1 1.6 %copy-start.9 = (bf16[1024,1024]{1,0:T(8,128)(2,1)S(1)}, bf16[1024,1024]{1,0:T(8,128)(2,1)}, u32[]{:S(2)}) copy-start(bf16[1024,1024]{1,0:T(8,128)(2,1)} %w_out) | copy-start | bytes 6291460
  8.9 38.5 %copy-start.11 = (bf16[256,1024]{1,0:T(8,128)(2,1)S(1)}, bf16[256,1024]{1,0:T(8,128)(2,1)}, u32[]{:S(2)}) copy-start(bf16[256,1024]{1,0:T(8,128)(2,1)} %x.3) | copy-start | bytes 1572868
  8.9 38.5 %copy-start.14 = (bf16[256,1024]{1,0:T(8,128)(2,1)S(1)}, bf16[256,1024]{1,0:T(8,128)(2,1)}, u32[]{:S(2)}) copy-start(bf16[256,1024]{1,0:T(8,128)(2,1)} %z) | copy-start | bytes 1572868
  8.9 38.5 %copy-start.15 = (bf16[256,1,256]{2,0,1:T(8,128)(2,1)S(1)}, bf16[256,1,256]{2,0,1:T(8,128)(2,1)}, u32[]{:S(2)}) copy-start(bf16[256,1,256]{2,0,1:T(8,128)(2,1)} %param.10) | copy-start | bytes 393220
  8.9 38.5 %copy-start.17 = (bf16[256,1,256]{2,0,1:T(8,128)(2,1)S(1)}, bf16[256,1,256]{2,0,1:T(8,128)(2,1)}, u32[]{:S(2)}) copy-start(bf16[256,1,256]{2,0,1:T(8,128)(2,1)} %param.9) | copy-start | bytes 393220
  8.9 38.5 %copy-start.13 = (f32[256,16]{1,0:T(8,128)S(1)}, f32[256,16]{1,0:T(8,128)}, u32[]{:S(2)}) copy-start(f32[256,16]{1,0:T(8,128)} %copy-done.12) | copy-start | bytes 49156
  8.9 15.8 %collective-permute-start.2 = (bf16[512,512]{1,0:T(8,128)(2,1)S(1)}, bf16[512,512]{1,0:T(8,128)(2,1)S(1)}, u32[]{:S(2)}, u32[]{:S(2)}) collective-permute-start(bf16[512,512]{1,0:T(8,128)(2,1)S(1)} %get-tuple-element.57.refs_4_.refs_2_), channel_id=1, source_target_pairs={{0,4},{4,0},{8,12},{12,8},{16,20},{20,16},{24,28},{28,24},{1,5},{5... | collective-permute-start | bytes 1572872 | tf_op jit(solution)/shard_map/ppermute | solution.py:259
  9.0 9.0 %collective-permute-start.5 = (bf16[384,512]{1,0:T(8,128)(2,1)S(1)}, bf16[384,512]{1,0:T(8,128)(2,1)S(1)}, u32[]{:S(2)}, u32[]{:S(2)}) collective-permute-start(bf16[384,512]{1,0:T(8,128)(2,1)S(1)} %get-tuple-element.59), channel_id=1, source_target_pairs={{0,1},{1,0},{2,3},{3,2},{4,5},{5,4},{6,7},{7,6},{8,9},{9,8},{10,11... | collective-permute-start | bytes 1179656 | tf_op jit(solution)/shard_map/ppermute | solution.py:270
  13.5 11.2 %copy-start.5 = (bf16[272,512]{1,0:T(8,128)(2,1)}, bf16[272,512]{1,0:T(8,128)(2,1)S(1)}, u32[]{:S(2)}) copy-start(bf16[272,512]{1,0:T(8,128)(2,1)S(1)} %collective-permute-done.refs_1_) | copy-start | bytes 835588
  13.6 6.6 %collective-permute-start.1 = (bf16[272,512]{1,0:T(8,128)(2,1)S(1)}, bf16[272,512]{1,0:T(8,128)(2,1)S(1)}, u32[]{:S(2)}, u32[]{:S(2)}) collective-permute-start(bf16[272,512]{1,0:T(8,128)(2,1)S(1)} %get-tuple-element.62), channel_id=1, source_target_pairs={{0,8},{4,12},{8,16},{12,20},{16,24},{20,28},{1,9},{5,13},{9,17},{1... | collective-permute-start | bytes 835592 | tf_op jit(solution)/shard_map/ppermute | solution.py:267
  16.8 19.2 %collective-permute-start.4 = (bf16[512,512]{1,0:T(8,128)(2,1)S(1)}, bf16[512,512]{1,0:T(8,128)(2,1)S(1)}, u32[]{:S(2)}, u32[]{:S(2)}) collective-permute-start(bf16[512,512]{1,0:T(8,128)(2,1)S(1)} %get-tuple-element.58.refs_5_.refs_3_), channel_id=1, source_target_pairs={{0,4},{4,0},{8,12},{12,8},{16,20},{20,16},{24,28},{28,24},{1,5},{5... | collective-permute-start | bytes 1572872 | tf_op jit(solution)/shard_map/ppermute | solution.py:259
  18.0 26.4 %collective-permute-start.6 = (bf16[384,512]{1,0:T(8,128)(2,1)S(1)}, bf16[384,512]{1,0:T(8,128)(2,1)S(1)}, u32[]{:S(2)}, u32[]{:S(2)}) collective-permute-start(bf16[384,512]{1,0:T(8,128)(2,1)S(1)} %collective-permute-done.5.refs_6_.refs_4_), channel_id=1, source_target_pairs={{0,4},{4,0},{8,12},{12,8},{16,20},{20,16},{24,28},{28,24},{1,5},{5... | collective-permute-start | bytes 1179656 | tf_op jit(solution)/shard_map/ppermute | solution.py:259
  20.2 30.8 %copy-start.24 = (f32[1024]{0:T(1024)S(1)}, f32[1024]{0:T(1024)}, u32[]{:S(2)}) copy-start(f32[1024]{0:T(1024)} %param.12) | copy-start | bytes 12292
  24.8 7.7 %collective-permute-start.3 = (bf16[272,512]{1,0:T(8,128)(2,1)S(1)}, bf16[272,512]{1,0:T(8,128)(2,1)S(1)}, u32[]{:S(2)}, u32[]{:S(2)}) collective-permute-start(bf16[272,512]{1,0:T(8,128)(2,1)S(1)} %get-tuple-element.66), channel_id=1, source_target_pairs={{0,16},{4,20},{8,24},{12,28},{1,17},{5,21},{9,25},{13,29},{2,18},{... | collective-permute-start | bytes 835592 | tf_op jit(solution)/shard_map/ppermute | solution.py:267
  28.9 21.4 %collective-permute-start.11 = (bf16[384,512]{1,0:T(8,128)(2,1)S(1)}, bf16[384,512]{1,0:T(8,128)(2,1)S(1)}, u32[]{:S(2)}, u32[]{:S(2)}) collective-permute-start(bf16[384,512]{1,0:T(8,128)(2,1)S(1)} %get-tuple-element.61), channel_id=1, source_target_pairs={{0,1},{1,0},{2,3},{3,2},{4,5},{5,4},{6,7},{7,6},{8,9},{9,8},{10,11... | collective-permute-start | bytes 1179656 | tf_op jit(solution)/shard_map/ppermute | solution.py:270
  32.4 1.0 copy-start.6
  44.4 6.6 %collective-permute-start.7 = (bf16[256,512]{1,0:T(8,128)(2,1)S(1)}, bf16[256,512]{1,0:T(8,128)(2,1)S(1)}, u32[]{:S(2)}, u32[]{:S(2)}) collective-permute-start(bf16[256,512]{1,0:T(8,128)(2,1)S(1)} %get-tuple-element.75), channel_id=1, source_target_pairs={{0,4},{4,0},{8,12},{12,8},{16,20},{20,16},{24,28},{28,24},{1,5},{5... | collective-permute-start | bytes 786440 | tf_op jit(solution)/shard_map/ppermute | solution.py:259
  45.6 7.7 %collective-permute-start.10 = (bf16[256,512]{1,0:T(8,128)(2,1)S(1)}, bf16[256,512]{1,0:T(8,128)(2,1)S(1)}, u32[]{:S(2)}, u32[]{:S(2)}) collective-permute-start(bf16[256,512]{1,0:T(8,128)(2,1)S(1)} %get-tuple-element.60), channel_id=1, source_target_pairs={{0,1},{1,0},{2,3},{3,2},{4,5},{5,4},{6,7},{7,6},{8,9},{9,8},{10,11... | collective-permute-start | bytes 786440 | tf_op jit(solution)/shard_map/ppermute | solution.py:270
  50.3 19.5 %collective-permute-start.13 = (bf16[384,512]{1,0:T(8,128)(2,1)S(1)}, bf16[384,512]{1,0:T(8,128)(2,1)S(1)}, u32[]{:S(2)}, u32[]{:S(2)}) collective-permute-start(bf16[384,512]{1,0:T(8,128)(2,1)S(1)} %collective-permute-done.11.refs_8_.refs_6_), channel_id=1, source_target_pairs={{0,4},{4,0},{8,12},{12,8},{16,20},{20,16},{24,28},{28,24},{1,5},{5... | collective-permute-start | bytes 1179656 | tf_op jit(solution)/shard_map/ppermute | solution.py:259
  52.3 7.9 %collective-permute-start.15 = (bf16[128,1024]{1,0:T(8,128)(2,1)S(1)}, bf16[128,1024]{1,0:T(8,128)(2,1)}, u32[]{:S(2)}, u32[]{:S(2)}) collective-permute-start(bf16[128,1024]{1,0:T(8,128)(2,1)S(1)} %get-tuple-element.76.refs_0_), channel_id=1, source_target_pairs={{0,8},{4,12},{8,16},{12,20},{16,24},{20,28},{24,0},{28,4},{1,9},{5... | collective-permute-start | bytes 786440 | tf_op jit(solution)/shard_map/ppermute | solution.py:263
  53.2 13.6 %collective-permute-start.12 = (bf16[256,512]{1,0:T(8,128)(2,1)S(1)}, bf16[256,512]{1,0:T(8,128)(2,1)S(1)}, u32[]{:S(2)}, u32[]{:S(2)}) collective-permute-start(bf16[256,512]{1,0:T(8,128)(2,1)S(1)} %collective-permute-done.10.refs_7_.refs_5_), channel_id=1, source_target_pairs={{0,4},{4,0},{8,12},{12,8},{16,20},{20,16},{24,28},{28,24},{1,5},{5... | collective-permute-start | bytes 786440 | tf_op jit(solution)/shard_map/ppermute | solution.py:259
  54.4 14.3 %collective-permute-start.16 = (bf16[128,1024]{1,0:T(8,128)(2,1)}, bf16[128,1024]{1,0:T(8,128)(2,1)}, u32[]{:S(2)}, u32[]{:S(2)}) collective-permute-start(bf16[128,1024]{1,0:T(8,128)(2,1)} %get-tuple-element.77.refs_1_), channel_id=1, source_target_pairs={{0,8},{4,12},{8,16},{12,20},{16,24},{20,28},{24,0},{28,4},{1,9},{5... | collective-permute-start | bytes 786440 | tf_op jit(solution)/shard_map/ppermute | solution.py:263
  55.7 16.1 %collective-permute-start.8 = (bf16[128,1024]{1,0:T(8,128)(2,1)S(1)}, bf16[128,1024]{1,0:T(8,128)(2,1)S(1)}, u32[]{:S(2)}, u32[]{:S(2)}) collective-permute-start(bf16[128,1024]{1,0:T(8,128)(2,1)S(1)} %get-tuple-element.76.refs_0_), channel_id=1, source_target_pairs={{0,1},{1,0},{2,3},{3,2},{4,5},{5,4},{6,7},{7,6},{8,9},{9,8},{10,11... | collective-permute-start | bytes 786440 | tf_op jit(solution)/shard_map/ppermute | solution.py:270
  59.5 0.7 copy-start.20
  60.2 12.7 %collective-permute-start.9 = (bf16[128,1024]{1,0:T(8,128)(2,1)}, bf16[128,1024]{1,0:T(8,128)(2,1)}, u32[]{:S(2)}, u32[]{:S(2)}) collective-permute-start(bf16[128,1024]{1,0:T(8,128)(2,1)} %get-tuple-element.77.refs_1_), channel_id=1, source_target_pairs={{0,1},{1,0},{2,3},{3,2},{4,5},{5,4},{6,7},{7,6},{8,9},{9,8},{10,11... | collective-permute-start | bytes 786440 | tf_op jit(solution)/shard_map/ppermute | solution.py:270
  67.5 13.2 %collective-permute-start.21 = (bf16[128,1024]{1,0:T(8,128)(2,1)}, bf16[128,1024]{1,0:T(8,128)(2,1)}, u32[]{:S(2)}, u32[]{:S(2)}) collective-permute-start(bf16[128,1024]{1,0:T(8,128)(2,1)} %collective-permute-done.15.refs_0_), channel_id=1, source_target_pairs={{0,8},{4,12},{8,16},{12,20},{16,24},{20,28},{24,0},{28,4},{1,9},{5... | collective-permute-start | bytes 786440 | tf_op jit(solution)/shard_map/ppermute | solution.py:263
  68.7 12.5 %collective-permute-start.17 = (bf16[128,1024]{1,0:T(8,128)(2,1)}, bf16[128,1024]{1,0:T(8,128)(2,1)}, u32[]{:S(2)}, u32[]{:S(2)}) collective-permute-start(bf16[128,1024]{1,0:T(8,128)(2,1)} %collective-permute-done.15.refs_0_), channel_id=1, source_target_pairs={{0,1},{1,0},{2,3},{3,2},{4,5},{5,4},{6,7},{7,6},{8,9},{9,8},{10,11... | collective-permute-start | bytes 786440 | tf_op jit(solution)/shard_map/ppermute | solution.py:270
  69.8 0.7 copy-start
  70.6 12.0 %collective-permute-start.22 = (bf16[128,1024]{1,0:T(8,128)(2,1)}, bf16[128,1024]{1,0:T(8,128)(2,1)}, u32[]{:S(2)}, u32[]{:S(2)}) collective-permute-start(bf16[128,1024]{1,0:T(8,128)(2,1)} %collective-permute-done.16.refs_1_), channel_id=1, source_target_pairs={{0,8},{4,12},{8,16},{12,20},{16,24},{20,28},{24,0},{28,4},{1,9},{5... | collective-permute-start | bytes 786440 | tf_op jit(solution)/shard_map/ppermute | solution.py:263
  71.9 0.7 copy-start.22
  72.6 11.4 %collective-permute-start.18 = (bf16[128,1024]{1,0:T(8,128)(2,1)}, bf16[128,1024]{1,0:T(8,128)(2,1)}, u32[]{:S(2)}, u32[]{:S(2)}) collective-permute-start(bf16[128,1024]{1,0:T(8,128)(2,1)} %collective-permute-done.16.refs_1_), channel_id=1, source_target_pairs={{0,1},{1,0},{2,3},{3,2},{4,5},{5,4},{6,7},{7,6},{8,9},{9,8},{10,11... | collective-permute-start | bytes 786440 | tf_op jit(solution)/shard_map/ppermute | solution.py:270
  72.9 1.0 copy-start.1
  73.9 0.9 copy-start.4
  74.8 0.9 copy-start.21
  75.8 0.9 copy-start.23
  76.7 7.3 %copy-start.2 = (bf16[384,512]{1,0:T(8,128)(2,1)S(1)}, bf16[384,512]{1,0:T(8,128)(2,1)}, u32[]{:S(2)}) copy-start(bf16[384,512]{1,0:T(8,128)(2,1)} %copy-done) | copy-start | bytes 1179652
  79.4 7.8 %collective-permute-start.14 = (bf16[2,2,64,512]{3,2,1,0:T(8,128)(2,1)S(1)}, bf16[2,2,64,512]{3,2,1,0:T(8,128)(2,1)S(1)}, u32[]{:S(2)}, u32[]{:S(2)}) collective-permute-start(bf16[2,2,64,512]{3,2,1,0:T(8,128)(2,1)S(1)} %get-tuple-element.81), channel_id=1, source_target_pairs={{0,2},{1,3},{2,0},{3,1},{4,6},{5,7},{6,4},{7,5},{8,10},{9,11},{10,... | collective-permute-start | bytes 786440 | tf_op jit(solution)/shard_map/ppermute | solution.py:274
  80.7 7.8 %collective-permute-start.23 = (bf16[128,1024]{1,0:T(8,128)(2,1)}, bf16[128,1024]{1,0:T(8,128)(2,1)S(1)}, u32[]{:S(2)}, u32[]{:S(2)}) collective-permute-start(bf16[128,1024]{1,0:T(8,128)(2,1)} %collective-permute-done.21.refs_0_), channel_id=1, source_target_pairs={{0,1},{1,0},{2,3},{3,2},{4,5},{5,4},{6,7},{7,6},{8,9},{9,8},{10,11... | collective-permute-start | bytes 786440 | tf_op jit(solution)/shard_map/ppermute | solution.py:270
  81.2 9.9 %collective-permute-start.27 = (bf16[128,1024]{1,0:T(8,128)(2,1)}, bf16[128,1024]{1,0:T(8,128)(2,1)S(1)}, u32[]{:S(2)}, u32[]{:S(2)}) collective-permute-start(bf16[128,1024]{1,0:T(8,128)(2,1)} %collective-permute-done.21.refs_0_), channel_id=1, source_target_pairs={{0,8},{4,12},{8,16},{12,20},{16,24},{20,28},{24,0},{28,4},{1,9},{5... | collective-permute-start | bytes 786440 | tf_op jit(solution)/shard_map/ppermute | solution.py:263
  82.5 9.9 %collective-permute-start.24 = (bf16[128,1024]{1,0:T(8,128)(2,1)}, bf16[128,1024]{1,0:T(8,128)(2,1)S(1)}, u32[]{:S(2)}, u32[]{:S(2)}) collective-permute-start(bf16[128,1024]{1,0:T(8,128)(2,1)} %collective-permute-done.22.refs_1_), channel_id=1, source_target_pairs={{0,1},{1,0},{2,3},{3,2},{4,5},{5,4},{6,7},{7,6},{8,9},{9,8},{10,11... | collective-permute-start | bytes 786440 | tf_op jit(solution)/shard_map/ppermute | solution.py:270
  84.0 12.7 %collective-permute-start.34 = (bf16[128,1024]{1,0:T(8,128)(2,1)}, bf16[128,1024]{1,0:T(8,128)(2,1)S(1)}, u32[]{:S(2)}, u32[]{:S(2)}) collective-permute-start(bf16[128,1024]{1,0:T(8,128)(2,1)} %collective-permute-done.22.refs_1_), channel_id=1, source_target_pairs={{0,8},{4,12},{8,16},{12,20},{16,24},{20,28},{24,0},{28,4},{1,9},{5... | collective-permute-start | bytes 786440 | tf_op jit(solution)/shard_map/ppermute | solution.py:263
  87.1 10.4 %collective-permute-start.19 = (bf16[2,2,64,512]{3,2,1,0:T(8,128)(2,1)S(1)}, bf16[2,2,64,512]{3,2,1,0:T(8,128)(2,1)S(1)}, u32[]{:S(2)}, u32[]{:S(2)}) collective-permute-start(bf16[2,2,64,512]{3,2,1,0:T(8,128)(2,1)S(1)} %get-tuple-element.83), channel_id=1, source_target_pairs={{0,2},{1,3},{2,0},{3,1},{4,6},{5,7},{6,4},{7,5},{8,10},{9,11},{10,... | collective-permute-start | bytes 786440 | tf_op jit(solution)/shard_map/ppermute | solution.py:274
  88.5 6.6 %copy-start.7 = (bf16[2,2,64,512]{3,2,1,0:T(8,128)(2,1)}, bf16[2,2,64,512]{3,2,1,0:T(8,128)(2,1)S(1)}, u32[]{:S(2)}) copy-start(bf16[2,2,64,512]{3,2,1,0:T(8,128)(2,1)S(1)} %shard_map.81.refs_0_) | copy-start | bytes 786436
  91.1 7.4 %collective-permute-start.28 = (bf16[128,1024]{1,0:T(8,128)(2,1)S(1)}, bf16[128,1024]{1,0:T(8,128)(2,1)S(1)}, u32[]{:S(2)}, u32[]{:S(2)}) collective-permute-start(bf16[128,1024]{1,0:T(8,128)(2,1)S(1)} %collective-permute-done.27.refs_0_), channel_id=1, source_target_pairs={{0,1},{1,0},{2,3},{3,2},{4,5},{5,4},{6,7},{7,6},{8,9},{9,8},{10,11... | collective-permute-start | bytes 786440 | tf_op jit(solution)/shard_map/ppermute | solution.py:270
  95.0 8.1 %collective-permute-start.25 = (bf16[2,2,64,512]{3,2,1,0:T(8,128)(2,1)S(1)}, bf16[2,2,64,512]{3,2,1,0:T(8,128)(2,1)S(1)}, u32[]{:S(2)}, u32[]{:S(2)}) collective-permute-start(bf16[2,2,64,512]{3,2,1,0:T(8,128)(2,1)S(1)} %get-tuple-element.86), channel_id=1, source_target_pairs={{0,2},{1,3},{2,0},{3,1},{4,6},{5,7},{6,4},{7,5},{8,10},{9,11},{10,... | collective-permute-start | bytes 786440 | tf_op jit(solution)/shard_map/ppermute | solution.py:274
  96.7 7.2 %collective-permute-start.35 = (bf16[128,1024]{1,0:T(8,128)(2,1)S(1)}, bf16[128,1024]{1,0:T(8,128)(2,1)S(1)}, u32[]{:S(2)}, u32[]{:S(2)}) collective-permute-start(bf16[128,1024]{1,0:T(8,128)(2,1)S(1)} %collective-permute-done.34.refs_0_), channel_id=1, source_target_pairs={{0,1},{1,0},{2,3},{3,2},{4,5},{5,4},{6,7},{7,6},{8,9},{9,8},{10,11... | collective-permute-start | bytes 786440 | tf_op jit(solution)/shard_map/ppermute | solution.py:270
  98.3 14.2 %collective-permute-start.20 = (bf16[2,2,64,512]{3,2,1,0:T(8,128)(2,1)}, bf16[2,2,64,512]{3,2,1,0:T(8,128)(2,1)}, u32[]{:S(2)}, u32[]{:S(2)}) collective-permute-start(bf16[2,2,64,512]{3,2,1,0:T(8,128)(2,1)} %shard_map.83), channel_id=1, source_target_pairs={{0,24},{4,28},{8,0},{12,4},{16,8},{20,12},{24,16},{28,20},{1,25},{... | collective-permute-start | bytes 786440 | tf_op jit(solution)/shard_map/ppermute | solution.py:263
  99.5 7.0 %collective-permute-start.29 = (bf16[1,2,64,512]{3,2,1,0:T(8,128)(2,1)S(1)}, bf16[1,2,64,512]{3,2,1,0:T(8,128)(2,1)S(1)}, u32[]{:S(2)}, u32[]{:S(2)}) collective-permute-start(bf16[1,2,64,512]{3,2,1,0:T(8,128)(2,1)S(1)} %get-tuple-element.89), channel_id=1, source_target_pairs={{0,2},{1,3},{2,0},{3,1},{4,6},{5,7},{6,4},{7,5},{8,10},{9,11},{10,... | collective-permute-start | bytes 393224 | tf_op jit(solution)/shard_map/ppermute | solution.py:274
  103.9 19.9 %collective-permute-start.26 = (bf16[2,2,64,512]{3,2,1,0:T(8,128)(2,1)}, bf16[2,2,64,512]{3,2,1,0:T(8,128)(2,1)}, u32[]{:S(2)}, u32[]{:S(2)}) collective-permute-start(bf16[2,2,64,512]{3,2,1,0:T(8,128)(2,1)} %shard_map.85), channel_id=1, source_target_pairs={{0,16},{4,20},{8,24},{12,28},{16,0},{20,4},{24,8},{28,12},{1,17},{... | collective-permute-start | bytes 786440 | tf_op jit(solution)/shard_map/ppermute | solution.py:263
  106.2 4.0 %collective-permute-start.36 = (bf16[1,2,64,512]{3,2,1,0:T(8,128)(2,1)}, bf16[1,2,64,512]{3,2,1,0:T(8,128)(2,1)S(1)}, u32[]{:S(2)}, u32[]{:S(2)}) collective-permute-start(bf16[1,2,64,512]{3,2,1,0:T(8,128)(2,1)} %get-tuple-element.96), channel_id=1, source_target_pairs={{0,2},{1,3},{2,0},{3,1},{4,6},{5,7},{6,4},{7,5},{8,10},{9,11},{10,... | collective-permute-start | bytes 393224 | tf_op jit(solution)/shard_map/ppermute | solution.py:274
  106.5 17.3 %collective-permute-start.30 = (bf16[1,2,64,512]{3,2,1,0:T(8,128)(2,1)S(1)}, bf16[1,2,64,512]{3,2,1,0:T(8,128)(2,1)S(1)}, u32[]{:S(2)}, u32[]{:S(2)}) collective-permute-start(bf16[1,2,64,512]{3,2,1,0:T(8,128)(2,1)S(1)} %shard_map.87), channel_id=1, source_target_pairs={{0,8},{4,12},{8,16},{12,20},{16,24},{20,28},{24,0},{28,4},{1,9},{5... | collective-permute-start | bytes 393224 | tf_op jit(solution)/shard_map/ppermute | solution.py:263
  110.3 1.0 copy-start.19
  111.3 16.5 %collective-permute-start.37 = (bf16[1,2,64,512]{3,2,1,0:T(8,128)(2,1)S(1)}, bf16[1,2,64,512]{3,2,1,0:T(8,128)(2,1)S(1)}, u32[]{:S(2)}, u32[]{:S(2)}) collective-permute-start(bf16[1,2,64,512]{3,2,1,0:T(8,128)(2,1)S(1)} %shard_map.90), channel_id=1, source_target_pairs={{0,8},{4,12},{8,16},{12,20},{16,24},{20,28},{24,0},{28,4},{1,9},{5... | collective-permute-start | bytes 393224 | tf_op jit(solution)/shard_map/ppermute | solution.py:263
  123.8 1.0 copy-start.8
  125.8 5.5 %collective-permute-start.31 = (bf16[2,64,512]{2,1,0:T(8,128)(2,1)S(1)}, bf16[2,64,512]{2,1,0:T(8,128)(2,1)S(1)}, u32[]{:S(2)}, u32[]{:S(2)}) collective-permute-start(bf16[2,64,512]{2,1,0:T(8,128)(2,1)S(1)} %get-tuple-element.91), channel_id=1, source_target_pairs={{0,1},{1,2},{2,3},{3,0},{4,5},{5,6},{6,7},{7,4},{8,9},{9,10},{10,1... | collective-permute-start | bytes 393224 | tf_op jit(solution)/shard_map/ppermute | solution.py:277
  126.9 6.8 %collective-permute-start.32 = (bf16[2,64,512]{2,1,0:T(8,128)(2,1)S(1)}, bf16[2,64,512]{2,1,0:T(8,128)(2,1)S(1)}, u32[]{:S(2)}, u32[]{:S(2)}) collective-permute-start(bf16[2,64,512]{2,1,0:T(8,128)(2,1)S(1)} %get-tuple-element.92), channel_id=1, source_target_pairs={{0,2},{1,3},{2,0},{3,1},{4,6},{5,7},{6,4},{7,5},{8,10},{9,11},{10,... | collective-permute-start | bytes 393224 | tf_op jit(solution)/shard_map/ppermute | solution.py:277
  127.8 7.5 %collective-permute-start.33 = (bf16[2,64,512]{2,1,0:T(8,128)(2,1)S(1)}, bf16[2,64,512]{2,1,0:T(8,128)(2,1)S(1)}, u32[]{:S(2)}, u32[]{:S(2)}) collective-permute-start(bf16[2,64,512]{2,1,0:T(8,128)(2,1)S(1)} %get-tuple-element.93), channel_id=1, source_target_pairs={{0,3},{1,0},{2,1},{3,2},{4,7},{5,4},{6,5},{7,6},{8,11},{9,8},{10,9... | collective-permute-start | bytes 393224 | tf_op jit(solution)/shard_map/ppermute | solution.py:277
  128.8 6.4 %collective-permute-start.38 = (bf16[2,64,512]{2,1,0:T(8,128)(2,1)S(1)}, bf16[2,64,512]{2,1,0:T(8,128)(2,1)S(1)}, u32[]{:S(2)}, u32[]{:S(2)}) collective-permute-start(bf16[2,64,512]{2,1,0:T(8,128)(2,1)S(1)} %get-tuple-element.98), channel_id=1, source_target_pairs={{0,1},{1,2},{2,3},{3,0},{4,5},{5,6},{6,7},{7,4},{8,9},{9,10},{10,1... | collective-permute-start | bytes 393224 | tf_op jit(solution)/shard_map/ppermute | solution.py:277
  130.6 8.7 %collective-permute-start.39 = (bf16[2,64,512]{2,1,0:T(8,128)(2,1)S(1)}, bf16[2,64,512]{2,1,0:T(8,128)(2,1)S(1)}, u32[]{:S(2)}, u32[]{:S(2)}) collective-permute-start(bf16[2,64,512]{2,1,0:T(8,128)(2,1)S(1)} %get-tuple-element.99), channel_id=1, source_target_pairs={{0,2},{1,3},{2,0},{3,1},{4,6},{5,7},{6,4},{7,5},{8,10},{9,11},{10,... | collective-permute-start | bytes 393224 | tf_op jit(solution)/shard_map/ppermute | solution.py:277
  131.3 8.6 %collective-permute-start.40 = (bf16[2,64,512]{2,1,0:T(8,128)(2,1)S(1)}, bf16[2,64,512]{2,1,0:T(8,128)(2,1)S(1)}, u32[]{:S(2)}, u32[]{:S(2)}) collective-permute-start(bf16[2,64,512]{2,1,0:T(8,128)(2,1)S(1)} %get-tuple-element.100), channel_id=1, source_target_pairs={{0,3},{1,0},{2,1},{3,2},{4,7},{5,4},{6,5},{7,6},{8,11},{9,8},{10,9... | collective-permute-start | bytes 393224 | tf_op jit(solution)/shard_map/ppermute | solution.py:277
  (2 other events, 1.4 us)

commit v5 on v4

--- a/solution.py
+++ b/solution.py
@@ -347,8 +347,8 @@
         if k + 1 < n_head:
             hidden = [rot_h(after(v, *outs[: max(t - 1, 0)]), 1) for v in hidden]
         other = [swap_core(v) for v in now]
-        if t == 2:
-            other[0] = after(other[0], sums[0])
+        if t > 3:
+            other[0] = after(other[0], sums[t - 4])
         shape = (len(chunks), r, piece, width)
         mine, *send = call(
             functools.partial(product_kernel, r, n_y, len(chunks)),

time: 142 us -> 138 us (0.972)
  waiting for transfers between devices: 50.7 us -> 46 us
  starting transfers between devices: 52 us -> 55.7 us
  local copies, waits for them, and re-layouts: 14.7 us -> 11.4 us
    ppermute x10, waiting for transfers between devices: 15.3 us -> 7.81 us  [rot_h(): return lax.ppermute(v, 'seq', pairs)]
    ppermute x11, starting transfers between devices: 20.4 us -> 24.5 us  [swap_core(): return lax.ppermute(v, 'head', [(i, i ^ 1) for i in range(n_head)])]
    unnamed x51 -> x43, local copies, waits for them, and re-layouts: 14.7 us -> 11.4 us
    ppermute x5, waiting for transfers between devices: 4.92 us -> 7.95 us  [rot_y(): return lax.ppermute(v, 'head', pairs)]
  transfers between devices with their start and end apart: 41 -> 41, of which waited for: 19 -> 18; matrix products, arithmetic and copies ran while one was open for 0% -> 0% of each run, Pallas kernels for 14% -> 15%
where the time goes in v5:
time: 138 us; the launch traced here: 137 us
  starting transfers between devices  55.7 us (40%)
  waiting for transfers between devices  46 us (33%)
  Pallas kernels  23.8 us (17%)
  local copies, waits for them, and re-layouts  11.4 us (8%)
    ppermute x11, starting transfers between devices, swap_core(): return lax.ppermute(v, 'head', [(i, i ^ 1) for i in range(n_head)])  24.5 us
    pallas_call x20, Pallas kernels, call(): pl.pallas_call(kernel, out_shape=[jax.ShapeDtypeStruct(s, d) for s, d in...  23.8 us
    ppermute x7, waiting for transfers between devices, rot_b(): return lax.ppermute(v, 'seq', pairs)  19.6 us
    unnamed x43, local copies, waits for them, and re-layouts  11.4 us
    ppermute x6, waiting for transfers between devices, rot_head(): lax.ppermute(v, 'head', [(i, (i + j) % n_head) for i in range(n_head)])  8.25 us
    ppermute x10, starting transfers between devices, rot_h(): return lax.ppermute(v, 'seq', pairs)  7.96 us
    ppermute x5, waiting for transfers between devices, rot_y(): return lax.ppermute(v, 'head', pairs)  7.95 us
    ppermute x10, waiting for transfers between devices, rot_h(): return lax.ppermute(v, 'seq', pairs)  7.81 us
  transfers between devices with their start and end apart: 41, of which 18 were waited for; matrix products, arithmetic and copies ran while one was open for 0% of the time, Pallas kernels for 15%

profile of v5, /device:TPU:1, one launch (start us, length us, event | category | flops | bytes accessed | tf_op | source)
XLA Modules:
  0.0 137.3 jit_solution(8724143419474178583)
XLA Ops:
  0.0 0.8 copy.8.logs
  0.8 1.1 copy-done.10
  1.9 0.9 copy-done.16
  2.8 2.2 %shard_map.73 = (bf16[272,512]{1,0:T(8,128)(2,1)S(1)}, bf16[272,512]{1,0:T(8,128)(2,1)S(1)}) custom-call(s32[1]{0:T(128)} %bitcast.1.me, bf16[256,1024]{1,0:T(8,128)(2,1)S(1)} %copy-done.10, bf16[256,256]{1,0:T(8,128)(2,1)S(1)} %bitcast.10, f32[256,16]{1,0:T(8,128)S(1)} %copy.8.logs), custom_call_target="tpu_custom_call" | custom-call | flops 1 | bytes 1 | tf_op jit(solution)/shard_map/pallas_call | solution.py:21
  5.0 2.1 %collective-permute-start = (bf16[272,512]{1,0:T(8,128)(2,1)S(1)}, bf16[272,512]{1,0:T(8,128)(2,1)S(1)}, u32[]{:S(2)}, u32[]{:S(2)}) collective-permute-start(bf16[272,512]{1,0:T(8,128)(2,1)S(1)} %get-tuple-element.54), channel_id=1, source_target_pairs={{0,4},{4,0},{8,12},{12,8},{16,20},{20,16},{24,28},{28,24},{1,5},{5... | collective-permute-start | bytes 835592 | tf_op jit(solution)/shard_map/ppermute | solution.py:259
  7.1 1.6 %copy-done.9 = bf16[1024,1024]{1,0:T(8,128)(2,1)S(1)} copy-done((bf16[1024,1024]{1,0:T(8,128)(2,1)S(1)}, bf16[1024,1024]{1,0:T(8,128)(2,1)}, u32[]{:S(2)}) %copy-start.9) | copy-done | bytes 2097176
  9.0 1.0 collective-permute-start.5
  10.0 3.5 %collective-permute-done.refs_1_ = bf16[272,512]{1,0:T(8,128)(2,1)S(1)} collective-permute-done((bf16[272,512]{1,0:T(8,128)(2,1)S(1)}, bf16[272,512]{1,0:T(8,128)(2,1)S(1)}, u32[]{:S(2)}, u32[]{:S(2)}) %collective-permute-start) | collective-permute-done | bytes 278560 | tf_op jit(solution)/shard_map/ppermute | solution.py:259
  13.6 3.2 %collective-permute-start.1 = (bf16[272,512]{1,0:T(8,128)(2,1)S(1)}, bf16[272,512]{1,0:T(8,128)(2,1)S(1)}, u32[]{:S(2)}, u32[]{:S(2)}) collective-permute-start(bf16[272,512]{1,0:T(8,128)(2,1)S(1)} %get-tuple-element.62), channel_id=1, source_target_pairs={{0,8},{4,12},{8,16},{12,20},{16,24},{20,28},{1,9},{5,13},{9,17},{1... | collective-permute-start | bytes 835592 | tf_op jit(solution)/shard_map/ppermute | solution.py:267
  16.8 1.3 collective-permute-start.4
  18.3 1.9 %collective-permute-done.1.got = bf16[272,512]{1,0:T(8,128)(2,1)S(1)} collective-permute-done((bf16[272,512]{1,0:T(8,128)(2,1)S(1)}, bf16[272,512]{1,0:T(8,128)(2,1)S(1)}, u32[]{:S(2)}, u32[]{:S(2)}) %collective-permute-start.1) | collective-permute-done | bytes 278560 | tf_op jit(solution)/shard_map/ppermute | solution.py:267
  20.2 0.9 shard_map.76
  21.1 3.6 %collective-permute-done.2.refs_2_.refs_9_.refs_7_ = bf16[512,512]{1,0:T(8,128)(2,1)S(1)} collective-permute-done((bf16[512,512]{1,0:T(8,128)(2,1)S(1)}, bf16[512,512]{1,0:T(8,128)(2,1)S(1)}, u32[]{:S(2)}, u32[]{:S(2)}) %collective-permute-start.2) | collective-permute-done | bytes 524320 | tf_op jit(solution)/shard_map/ppermute | solution.py:259
  24.8 4.2 %collective-permute-start.3 = (bf16[272,512]{1,0:T(8,128)(2,1)S(1)}, bf16[272,512]{1,0:T(8,128)(2,1)S(1)}, u32[]{:S(2)}, u32[]{:S(2)}) collective-permute-start(bf16[272,512]{1,0:T(8,128)(2,1)S(1)} %get-tuple-element.66), channel_id=1, source_target_pairs={{0,16},{4,20},{8,24},{12,28},{1,17},{5,21},{9,25},{13,29},{2,18},{... | collective-permute-start | bytes 835592 | tf_op jit(solution)/shard_map/ppermute | solution.py:267
  28.9 3.0 %collective-permute-start.11 = (bf16[384,512]{1,0:T(8,128)(2,1)S(1)}, bf16[384,512]{1,0:T(8,128)(2,1)S(1)}, u32[]{:S(2)}, u32[]{:S(2)}) collective-permute-start(bf16[384,512]{1,0:T(8,128)(2,1)S(1)} %get-tuple-element.61), channel_id=1, source_target_pairs={{0,1},{1,0},{2,3},{3,2},{4,5},{5,4},{6,7},{7,6},{8,9},{9,8},{10,11... | collective-permute-start | bytes 1179656 | tf_op jit(solution)/shard_map/ppermute | solution.py:270
  32.4 1.0 copy-done.6
  33.6 2.4 %collective-permute-done.4.refs_3_.refs_10_.refs_8_ = bf16[512,512]{1,0:T(8,128)(2,1)S(1)} collective-permute-done((bf16[512,512]{1,0:T(8,128)(2,1)S(1)}, bf16[512,512]{1,0:T(8,128)(2,1)S(1)}, u32[]{:S(2)}, u32[]{:S(2)}) %collective-permute-start.4) | collective-permute-done | bytes 524320 | tf_op jit(solution)/shard_map/ppermute | solution.py:259
  36.0 8.4 %collective-permute-done.6.refs_4_.refs_11_.refs_9_ = bf16[384,512]{1,0:T(8,128)(2,1)S(1)} collective-permute-done((bf16[384,512]{1,0:T(8,128)(2,1)S(1)}, bf16[384,512]{1,0:T(8,128)(2,1)S(1)}, u32[]{:S(2)}, u32[]{:S(2)}) %collective-permute-start.6) | collective-permute-done | bytes 393248 | tf_op jit(solution)/shard_map/ppermute | solution.py:259
  44.4 1.1 collective-permute-start.7
  45.6 1.8 %collective-permute-start.10 = (bf16[256,512]{1,0:T(8,128)(2,1)S(1)}, bf16[256,512]{1,0:T(8,128)(2,1)S(1)}, u32[]{:S(2)}, u32[]{:S(2)}) collective-permute-start(bf16[256,512]{1,0:T(8,128)(2,1)S(1)} %get-tuple-element.60), channel_id=1, source_target_pairs={{0,1},{1,0},{2,3},{3,2},{4,5},{5,4},{6,7},{7,6},{8,9},{9,8},{10,11... | collective-permute-start | bytes 786440 | tf_op jit(solution)/shard_map/ppermute | solution.py:270
  47.4 2.9 %shard_map.78 = (f32[256,1024]{1,0:T(8,128)S(1)}, f32[256,1024]{1,0:T(8,128)S(1)}, f32[256,1024]{1,0:T(8,128)S(1)}) custom-call(s32[1]{0:T(128)} %bitcast.1.me, bf16[256,1024]{1,0:T(8,128)(2,1)S(1)} %copy-done.11, bf16[256,1024]{1,0:T(8,128)(2,1)S(1)} %copy-done.14, bf16[256,256]{1,0:T(8,128)(2,1)S(1)} %bitcast.11, bf16[256,256]{1,0:T(8,128)(2,1)S(1)} %bitcast.8, ...), custom_call_target="tpu_custom_call" | custom-call | flops 1 | bytes 1 | tf_op jit(solution)/shard_map/pallas_call | solution.py:21
  51.0 1.3 shard_map.79
  52.3 1.0 collective-permute-start.15
  53.2 1.3 collective-permute-start.16
  54.5 1.2 collective-permute-start.12
  55.7 3.7 %collective-permute-start.8 = (bf16[128,1024]{1,0:T(8,128)(2,1)}, bf16[128,1024]{1,0:T(8,128)(2,1)}, u32[]{:S(2)}, u32[]{:S(2)}) collective-permute-start(bf16[128,1024]{1,0:T(8,128)(2,1)} %get-tuple-element.76.refs_0_), channel_id=1, source_target_pairs={{0,1},{1,0},{2,3},{3,2},{4,5},{5,4},{6,7},{7,6},{8,9},{9,8},{10,11... | collective-permute-start | bytes 786440 | tf_op jit(solution)/shard_map/ppermute | solution.py:270
  60.0 5.7 %collective-permute-start.9 = (bf16[128,1024]{1,0:T(8,128)(2,1)}, bf16[128,1024]{1,0:T(8,128)(2,1)}, u32[]{:S(2)}, u32[]{:S(2)}) collective-permute-start(bf16[128,1024]{1,0:T(8,128)(2,1)} %get-tuple-element.77.refs_1_), channel_id=1, source_target_pairs={{0,1},{1,0},{2,3},{3,2},{4,5},{5,4},{6,7},{7,6},{8,9},{9,8},{10,11... | collective-permute-start | bytes 786440 | tf_op jit(solution)/shard_map/ppermute | solution.py:270
  65.8 1.0 collective-permute-done.12.refs_12_.refs_10_
  67.6 1.2 collective-permute-start.22
  68.8 0.7 copy-done
  69.5 1.7 %collective-permute-start.17 = (bf16[128,1024]{1,0:T(8,128)(2,1)}, bf16[128,1024]{1,0:T(8,128)(2,1)}, u32[]{:S(2)}, u32[]{:S(2)}) collective-permute-start(bf16[128,1024]{1,0:T(8,128)(2,1)} %collective-permute-done.15.refs_0_), channel_id=1, source_target_pairs={{0,1},{1,0},{2,3},{3,2},{4,5},{5,4},{6,7},{7,6},{8,9},{9,8},{10,11... | collective-permute-start | bytes 786440 | tf_op jit(solution)/shard_map/ppermute | solution.py:270
  71.2 1.0 copy-done.1
  72.2 0.9 copy-done.4
  73.2 2.8 %shard_map.80 = (f32[2,2,64,512]{3,2,1,0:T(8,128)S(1)}, bf16[2,2,64,512]{3,2,1,0:T(8,128)(2,1)S(1)}) custom-call(s32[1]{0:T(128)} %bitcast.3.me, bf16[128,1024]{1,0:T(8,128)(2,1)} %get-tuple-element.76.refs_0_, bf16[128,1024]{1,0:T(8,128)(2,1)} %get-tuple-element.77.refs_1_, bf16[128,1024]{1,0:T(8,128)(2,1)} %collective-permute-done.8.refs_2_, ...), custom_call_target="tpu_custom_call" | custom-call | flops 1 | bytes 1 | tf_op jit(solution)/shard_map/pallas_call | solution.py:21
  76.0 1.4 collective-permute-start.27
  77.4 2.1 %collective-permute-start.23 = (bf16[128,1024]{1,0:T(8,128)(2,1)}, bf16[128,1024]{1,0:T(8,128)(2,1)S(1)}, u32[]{:S(2)}, u32[]{:S(2)}) collective-permute-start(bf16[128,1024]{1,0:T(8,128)(2,1)} %collective-permute-done.21.refs_0_), channel_id=1, source_target_pairs={{0,1},{1,0},{2,3},{3,2},{4,5},{5,4},{6,7},{7,6},{8,9},{9,8},{10,11... | collective-permute-start | bytes 786440 | tf_op jit(solution)/shard_map/ppermute | solution.py:270
  79.4 3.7 %collective-permute-start.24 = (bf16[128,1024]{1,0:T(8,128)(2,1)}, bf16[128,1024]{1,0:T(8,128)(2,1)S(1)}, u32[]{:S(2)}, u32[]{:S(2)}) collective-permute-start(bf16[128,1024]{1,0:T(8,128)(2,1)} %collective-permute-done.22.refs_1_), channel_id=1, source_target_pairs={{0,1},{1,0},{2,3},{3,2},{4,5},{5,4},{6,7},{7,6},{8,9},{9,8},{10,11... | collective-permute-start | bytes 786440 | tf_op jit(solution)/shard_map/ppermute | solution.py:270
  83.1 2.7 %shard_map.82 = (f32[2,2,64,512]{3,2,1,0:T(8,128)S(1)}, bf16[2,2,64,512]{3,2,1,0:T(8,128)(2,1)S(1)}) custom-call(s32[1]{0:T(128)} %bitcast.3.me, bf16[128,1024]{1,0:T(8,128)(2,1)} %collective-permute-done.15.refs_0_, bf16[128,1024]{1,0:T(8,128)(2,1)} %collective-permute-done.16.refs_1_, bf16[128,1024]{1,0:T(8,128)(2,1)} %collective-permute-done.17.refs_2_, ...), custom_call_target="tpu_custom_call" | custom-call | flops 1 | bytes 1 | tf_op jit(solution)/shard_map/pallas_call | solution.py:21
  85.8 1.0 collective-permute-start.19
  86.9 0.9 collective-permute-start.28
  87.8 2.6 %shard_map.84 = (f32[2,2,64,512]{3,2,1,0:T(8,128)S(1)}, bf16[2,2,64,512]{3,2,1,0:T(8,128)(2,1)S(1)}) custom-call(s32[1]{0:T(128)} %bitcast.3.me, bf16[128,1024]{1,0:T(8,128)(2,1)} %collective-permute-done.21.refs_0_, bf16[128,1024]{1,0:T(8,128)(2,1)} %collective-permute-done.22.refs_1_, bf16[128,1024]{1,0:T(8,128)(2,1)S(1)} %collective-permute-done.23.refs_2_, ...), custom_call_target="tpu_custom_call" | custom-call | flops 1 | bytes 1 | tf_op jit(solution)/shard_map/pallas_call | solution.py:21
  90.4 1.2 collective-permute-start.25
  92.0 1.1 collective-permute-done.34.refs_0_
  93.1 0.8 collective-permute-start.35
  94.6 2.9 %collective-permute-start.20 = (bf16[2,2,64,512]{3,2,1,0:T(8,128)(2,1)}, bf16[2,2,64,512]{3,2,1,0:T(8,128)(2,1)}, u32[]{:S(2)}, u32[]{:S(2)}) collective-permute-start(bf16[2,2,64,512]{3,2,1,0:T(8,128)(2,1)} %shard_map.83), channel_id=1, source_target_pairs={{0,24},{4,28},{8,0},{12,4},{16,8},{20,12},{24,16},{28,20},{1,25},{... | collective-permute-start | bytes 786440 | tf_op jit(solution)/shard_map/ppermute | solution.py:263
  97.5 1.0 shard_map.86
  98.5 1.1 collective-permute-start.29
  99.6 0.8 shard_map.85
  100.4 4.6 %collective-permute-done.14.refs_0_ = bf16[2,2,64,512]{3,2,1,0:T(8,128)(2,1)S(1)} collective-permute-done((bf16[2,2,64,512]{3,2,1,0:T(8,128)(2,1)S(1)}, bf16[2,2,64,512]{3,2,1,0:T(8,128)(2,1)S(1)}, u32[]{:S(2)}, u32[]{:S(2)}) %collective-permute-start.14) | collective-permute-done | bytes 262176 | tf_op jit(solution)/shard_map/ppermute | solution.py:274
  105.1 1.6 %shard_map.89 = (f32[1,2,64,512]{3,2,1,0:T(8,128)S(1)}, bf16[1,2,64,512]{3,2,1,0:T(8,128)(2,1)}) custom-call(s32[1]{0:T(128)} %bitcast.3.me, bf16[128,1024]{1,0:T(8,128)(2,1)S(1)} %collective-permute-done.34.refs_0_, bf16[128,1024]{1,0:T(8,128)(2,1)S(1)} %collective-permute-done.35.refs_1_, bf16[512,512]{1,0:T(8,128)(2,1)S(1)} %get-tuple-element.57.refs_4_.refs_2_, ...), custom_call_target="tpu_custom_call" | custom-call | flops 1 | bytes 1 | tf_op jit(solution)/shard_map/pallas_call | solution.py:21
  107.5 1.0 collective-permute-start.36
  108.6 3.3 %collective-permute-done.36.refs_0_ = bf16[1,2,64,512]{3,2,1,0:T(8,128)(2,1)S(1)} collective-permute-done((bf16[1,2,64,512]{3,2,1,0:T(8,128)(2,1)}, bf16[1,2,64,512]{3,2,1,0:T(8,128)(2,1)S(1)}, u32[]{:S(2)}, u32[]{:S(2)}) %collective-permute-start.36) | collective-permute-done | bytes 131104 | tf_op jit(solution)/shard_map/ppermute | solution.py:274
  111.9 0.9 copy-done.19
  113.0 6.1 %collective-permute-done.26.refs_2_ = bf16[2,2,64,512]{3,2,1,0:T(8,128)(2,1)} collective-permute-done((bf16[2,2,64,512]{3,2,1,0:T(8,128)(2,1)}, bf16[2,2,64,512]{3,2,1,0:T(8,128)(2,1)}, u32[]{:S(2)}, u32[]{:S(2)}) %collective-permute-start.26) | collective-permute-done | bytes 262176 | tf_op jit(solution)/shard_map/ppermute | solution.py:263
  119.1 0.9 copy-done.8
  120.0 1.1 shard_map.88
  121.1 1.9 %collective-permute-start.31 = (bf16[2,64,512]{2,1,0:T(8,128)(2,1)S(1)}, bf16[2,64,512]{2,1,0:T(8,128)(2,1)S(1)}, u32[]{:S(2)}, u32[]{:S(2)}) collective-permute-start(bf16[2,64,512]{2,1,0:T(8,128)(2,1)S(1)} %get-tuple-element.90), channel_id=1, source_target_pairs={{0,1},{1,2},{2,3},{3,0},{4,5},{5,6},{6,7},{7,4},{8,9},{9,10},{10,1... | collective-permute-start | bytes 393224 | tf_op jit(solution)/shard_map/ppermute | solution.py:277
  123.5 1.1 shard_map.91
  124.6 1.8 %collective-permute-start.38 = (bf16[2,64,512]{2,1,0:T(8,128)(2,1)S(1)}, bf16[2,64,512]{2,1,0:T(8,128)(2,1)S(1)}, u32[]{:S(2)}, u32[]{:S(2)}) collective-permute-start(bf16[2,64,512]{2,1,0:T(8,128)(2,1)S(1)} %get-tuple-element.98), channel_id=1, source_target_pairs={{0,1},{1,2},{2,3},{3,0},{4,5},{5,6},{6,7},{7,4},{8,9},{9,10},{10,1... | collective-permute-start | bytes 393224 | tf_op jit(solution)/shard_map/ppermute | solution.py:277
  126.4 1.0 collective-permute-start.39
  127.5 2.0 %collective-permute-done.32.refs_2_ = bf16[2,64,512]{2,1,0:T(8,128)(2,1)S(1)} collective-permute-done((bf16[2,64,512]{2,1,0:T(8,128)(2,1)S(1)}, bf16[2,64,512]{2,1,0:T(8,128)(2,1)S(1)}, u32[]{:S(2)}, u32[]{:S(2)}) %collective-permute-start.32) | collective-permute-done | bytes 131104 | tf_op jit(solution)/shard_map/ppermute | solution.py:277
  129.5 1.5 %collective-permute-done.33.refs_3_ = bf16[2,64,512]{2,1,0:T(8,128)(2,1)S(1)} collective-permute-done((bf16[2,64,512]{2,1,0:T(8,128)(2,1)S(1)}, bf16[2,64,512]{2,1,0:T(8,128)(2,1)S(1)}, u32[]{:S(2)}, u32[]{:S(2)}) %collective-permute-start.33) | collective-permute-done | bytes 131104 | tf_op jit(solution)/shard_map/ppermute | solution.py:277
  131.4 3.8 %collective-permute-done.39.refs_6_ = bf16[2,64,512]{2,1,0:T(8,128)(2,1)S(1)} collective-permute-done((bf16[2,64,512]{2,1,0:T(8,128)(2,1)S(1)}, bf16[2,64,512]{2,1,0:T(8,128)(2,1)S(1)}, u32[]{:S(2)}, u32[]{:S(2)}) %collective-permute-start.39) | collective-permute-done | bytes 131104 | tf_op jit(solution)/shard_map/ppermute | solution.py:277
  135.7 1.6 %shard_map.92 = bf16[256,2048]{1,0:T(8,128)(2,1)} custom-call(s32[2]{0:T(128)S(1)} %pad_add_fusion.me, bf16[2,64,512]{2,1,0:T(8,128)(2,1)S(1)} %get-tuple-element.89.refs_0_, bf16[2,64,512]{2,1,0:T(8,128)(2,1)S(1)} %collective-permute-done.31.refs_1_, bf16[2,64,512]{2,1,0:T(8,128)(2,1)S(1)} %collective-permute-done.32.refs_2_, ...), custom_call_target="tpu_custom_call" | custom-call | flops 1 | bytes 1 | tf_op jit(solution)/shard_map/pallas_call | solution.py:21
  (82 shorter events, 7.0 us)
Async XLA Ops:
  0.8 8.1 %copy-start.12 = (f32[256,16]{1,0:T(8,128)}, f32[256,16]{1,0:T(8,128)S(1)}, u32[]{:S(2)}) copy-start(f32[256,16]{1,0:T(8,128)S(1)} %copy.8.logs) | copy-start | bytes 49156
  0.8 1.1 copy-start.10
  1.9 0.9 copy-start.16
  5.0 8.5 %collective-permute-start = (bf16[272,512]{1,0:T(8,128)(2,1)S(1)}, bf16[272,512]{1,0:T(8,128)(2,1)S(1)}, u32[]{:S(2)}, u32[]{:S(2)}) collective-permute-start(bf16[272,512]{1,0:T(8,128)(2,1)S(1)} %get-tuple-element.54), channel_id=1, source_target_pairs={{0,4},{4,0},{8,12},{12,8},{16,20},{20,16},{24,28},{28,24},{1,5},{5... | collective-permute-start | bytes 835592 | tf_op jit(solution)/shard_map/ppermute | solution.py:259
  7.1 1.6 %copy-start.9 = (bf16[1024,1024]{1,0:T(8,128)(2,1)S(1)}, bf16[1024,1024]{1,0:T(8,128)(2,1)}, u32[]{:S(2)}) copy-start(bf16[1024,1024]{1,0:T(8,128)(2,1)} %w_out) | copy-start | bytes 6291460
  8.9 38.5 %copy-start.11 = (bf16[256,1024]{1,0:T(8,128)(2,1)S(1)}, bf16[256,1024]{1,0:T(8,128)(2,1)}, u32[]{:S(2)}) copy-start(bf16[256,1024]{1,0:T(8,128)(2,1)} %x.3) | copy-start | bytes 1572868
  8.9 38.5 %copy-start.14 = (bf16[256,1024]{1,0:T(8,128)(2,1)S(1)}, bf16[256,1024]{1,0:T(8,128)(2,1)}, u32[]{:S(2)}) copy-start(bf16[256,1024]{1,0:T(8,128)(2,1)} %z) | copy-start | bytes 1572868
  8.9 38.5 %copy-start.15 = (bf16[256,1,256]{2,0,1:T(8,128)(2,1)S(1)}, bf16[256,1,256]{2,0,1:T(8,128)(2,1)}, u32[]{:S(2)}) copy-start(bf16[256,1,256]{2,0,1:T(8,128)(2,1)} %param.10) | copy-start | bytes 393220
  8.9 38.5 %copy-start.17 = (bf16[256,1,256]{2,0,1:T(8,128)(2,1)S(1)}, bf16[256,1,256]{2,0,1:T(8,128)(2,1)}, u32[]{:S(2)}) copy-start(bf16[256,1,256]{2,0,1:T(8,128)(2,1)} %param.9) | copy-start | bytes 393220
  8.9 38.5 %copy-start.13 = (f32[256,16]{1,0:T(8,128)S(1)}, f32[256,16]{1,0:T(8,128)}, u32[]{:S(2)}) copy-start(f32[256,16]{1,0:T(8,128)} %copy-done.12) | copy-start | bytes 49156
  8.9 15.8 %collective-permute-start.2 = (bf16[512,512]{1,0:T(8,128)(2,1)S(1)}, bf16[512,512]{1,0:T(8,128)(2,1)S(1)}, u32[]{:S(2)}, u32[]{:S(2)}) collective-permute-start(bf16[512,512]{1,0:T(8,128)(2,1)S(1)} %get-tuple-element.57.refs_4_.refs_2_), channel_id=1, source_target_pairs={{0,4},{4,0},{8,12},{12,8},{16,20},{20,16},{24,28},{28,24},{1,5},{5... | collective-permute-start | bytes 1572872 | tf_op jit(solution)/shard_map/ppermute | solution.py:259
  9.0 9.0 %collective-permute-start.5 = (bf16[384,512]{1,0:T(8,128)(2,1)S(1)}, bf16[384,512]{1,0:T(8,128)(2,1)S(1)}, u32[]{:S(2)}, u32[]{:S(2)}) collective-permute-start(bf16[384,512]{1,0:T(8,128)(2,1)S(1)} %get-tuple-element.59), channel_id=1, source_target_pairs={{0,1},{1,0},{2,3},{3,2},{4,5},{5,4},{6,7},{7,6},{8,9},{9,8},{10,11... | collective-permute-start | bytes 1179656 | tf_op jit(solution)/shard_map/ppermute | solution.py:270
  13.5 11.2 %copy-start.5 = (bf16[272,512]{1,0:T(8,128)(2,1)}, bf16[272,512]{1,0:T(8,128)(2,1)S(1)}, u32[]{:S(2)}) copy-start(bf16[272,512]{1,0:T(8,128)(2,1)S(1)} %collective-permute-done.refs_1_) | copy-start | bytes 835588
  13.6 6.6 %collective-permute-start.1 = (bf16[272,512]{1,0:T(8,128)(2,1)S(1)}, bf16[272,512]{1,0:T(8,128)(2,1)S(1)}, u32[]{:S(2)}, u32[]{:S(2)}) collective-permute-start(bf16[272,512]{1,0:T(8,128)(2,1)S(1)} %get-tuple-element.62), channel_id=1, source_target_pairs={{0,8},{4,12},{8,16},{12,20},{16,24},{20,28},{1,9},{5,13},{9,17},{1... | collective-permute-start | bytes 835592 | tf_op jit(solution)/shard_map/ppermute | solution.py:267
  16.8 19.2 %collective-permute-start.4 = (bf16[512,512]{1,0:T(8,128)(2,1)S(1)}, bf16[512,512]{1,0:T(8,128)(2,1)S(1)}, u32[]{:S(2)}, u32[]{:S(2)}) collective-permute-start(bf16[512,512]{1,0:T(8,128)(2,1)S(1)} %get-tuple-element.58.refs_5_.refs_3_), channel_id=1, source_target_pairs={{0,4},{4,0},{8,12},{12,8},{16,20},{20,16},{24,28},{28,24},{1,5},{5... | collective-permute-start | bytes 1572872 | tf_op jit(solution)/shard_map/ppermute | solution.py:259
  18.0 26.4 %collective-permute-start.6 = (bf16[384,512]{1,0:T(8,128)(2,1)S(1)}, bf16[384,512]{1,0:T(8,128)(2,1)S(1)}, u32[]{:S(2)}, u32[]{:S(2)}) collective-permute-start(bf16[384,512]{1,0:T(8,128)(2,1)S(1)} %collective-permute-done.5.refs_6_.refs_4_), channel_id=1, source_target_pairs={{0,4},{4,0},{8,12},{12,8},{16,20},{20,16},{24,28},{28,24},{1,5},{5... | collective-permute-start | bytes 1179656 | tf_op jit(solution)/shard_map/ppermute | solution.py:259
  20.2 30.8 %copy-start.20 = (f32[1024]{0:T(1024)S(1)}, f32[1024]{0:T(1024)}, u32[]{:S(2)}) copy-start(f32[1024]{0:T(1024)} %param.12) | copy-start | bytes 12292
  24.8 7.7 %collective-permute-start.3 = (bf16[272,512]{1,0:T(8,128)(2,1)S(1)}, bf16[272,512]{1,0:T(8,128)(2,1)S(1)}, u32[]{:S(2)}, u32[]{:S(2)}) collective-permute-start(bf16[272,512]{1,0:T(8,128)(2,1)S(1)} %get-tuple-element.66), channel_id=1, source_target_pairs={{0,16},{4,20},{8,24},{12,28},{1,17},{5,21},{9,25},{13,29},{2,18},{... | collective-permute-start | bytes 835592 | tf_op jit(solution)/shard_map/ppermute | solution.py:267
  28.9 21.4 %collective-permute-start.11 = (bf16[384,512]{1,0:T(8,128)(2,1)S(1)}, bf16[384,512]{1,0:T(8,128)(2,1)S(1)}, u32[]{:S(2)}, u32[]{:S(2)}) collective-permute-start(bf16[384,512]{1,0:T(8,128)(2,1)S(1)} %get-tuple-element.61), channel_id=1, source_target_pairs={{0,1},{1,0},{2,3},{3,2},{4,5},{5,4},{6,7},{7,6},{8,9},{9,8},{10,11... | collective-permute-start | bytes 1179656 | tf_op jit(solution)/shard_map/ppermute | solution.py:270
  32.4 1.0 copy-start.6
  44.4 6.6 %collective-permute-start.7 = (bf16[256,512]{1,0:T(8,128)(2,1)S(1)}, bf16[256,512]{1,0:T(8,128)(2,1)S(1)}, u32[]{:S(2)}, u32[]{:S(2)}) collective-permute-start(bf16[256,512]{1,0:T(8,128)(2,1)S(1)} %get-tuple-element.75), channel_id=1, source_target_pairs={{0,4},{4,0},{8,12},{12,8},{16,20},{20,16},{24,28},{28,24},{1,5},{5... | collective-permute-start | bytes 786440 | tf_op jit(solution)/shard_map/ppermute | solution.py:259
  45.6 9.0 %collective-permute-start.10 = (bf16[256,512]{1,0:T(8,128)(2,1)S(1)}, bf16[256,512]{1,0:T(8,128)(2,1)S(1)}, u32[]{:S(2)}, u32[]{:S(2)}) collective-permute-start(bf16[256,512]{1,0:T(8,128)(2,1)S(1)} %get-tuple-element.60), channel_id=1, source_target_pairs={{0,1},{1,0},{2,3},{3,2},{4,5},{5,4},{6,7},{7,6},{8,9},{9,8},{10,11... | collective-permute-start | bytes 786440 | tf_op jit(solution)/shard_map/ppermute | solution.py:270
  50.3 18.4 %collective-permute-start.13 = (bf16[384,512]{1,0:T(8,128)(2,1)S(1)}, bf16[384,512]{1,0:T(8,128)(2,1)S(1)}, u32[]{:S(2)}, u32[]{:S(2)}) collective-permute-start(bf16[384,512]{1,0:T(8,128)(2,1)S(1)} %collective-permute-done.11.refs_8_.refs_6_), channel_id=1, source_target_pairs={{0,4},{4,0},{8,12},{12,8},{16,20},{20,16},{24,28},{28,24},{1,5},{5... | collective-permute-start | bytes 1179656 | tf_op jit(solution)/shard_map/ppermute | solution.py:259
  52.3 7.8 %collective-permute-start.15 = (bf16[128,1024]{1,0:T(8,128)(2,1)}, bf16[128,1024]{1,0:T(8,128)(2,1)}, u32[]{:S(2)}, u32[]{:S(2)}) collective-permute-start(bf16[128,1024]{1,0:T(8,128)(2,1)} %get-tuple-element.76.refs_0_), channel_id=1, source_target_pairs={{0,8},{4,12},{8,16},{12,20},{16,24},{20,28},{24,0},{28,4},{1,9},{5... | collective-permute-start | bytes 786440 | tf_op jit(solution)/shard_map/ppermute | solution.py:263
  53.2 12.5 %collective-permute-start.16 = (bf16[128,1024]{1,0:T(8,128)(2,1)}, bf16[128,1024]{1,0:T(8,128)(2,1)}, u32[]{:S(2)}, u32[]{:S(2)}) collective-permute-start(bf16[128,1024]{1,0:T(8,128)(2,1)} %get-tuple-element.77.refs_1_), channel_id=1, source_target_pairs={{0,8},{4,12},{8,16},{12,20},{16,24},{20,28},{24,0},{28,4},{1,9},{5... | collective-permute-start | bytes 786440 | tf_op jit(solution)/shard_map/ppermute | solution.py:263
  54.5 12.3 %collective-permute-start.12 = (bf16[256,512]{1,0:T(8,128)(2,1)S(1)}, bf16[256,512]{1,0:T(8,128)(2,1)S(1)}, u32[]{:S(2)}, u32[]{:S(2)}) collective-permute-start(bf16[256,512]{1,0:T(8,128)(2,1)S(1)} %collective-permute-done.10.refs_7_.refs_5_), channel_id=1, source_target_pairs={{0,4},{4,0},{8,12},{12,8},{16,20},{20,16},{24,28},{28,24},{1,5},{5... | collective-permute-start | bytes 786440 | tf_op jit(solution)/shard_map/ppermute | solution.py:259
  55.7 15.5 %collective-permute-start.8 = (bf16[128,1024]{1,0:T(8,128)(2,1)}, bf16[128,1024]{1,0:T(8,128)(2,1)}, u32[]{:S(2)}, u32[]{:S(2)}) collective-permute-start(bf16[128,1024]{1,0:T(8,128)(2,1)} %get-tuple-element.76.refs_0_), channel_id=1, source_target_pairs={{0,1},{1,0},{2,3},{3,2},{4,5},{5,4},{6,7},{7,6},{8,9},{9,8},{10,11... | collective-permute-start | bytes 786440 | tf_op jit(solution)/shard_map/ppermute | solution.py:270
  60.0 11.2 %collective-permute-start.9 = (bf16[128,1024]{1,0:T(8,128)(2,1)}, bf16[128,1024]{1,0:T(8,128)(2,1)}, u32[]{:S(2)}, u32[]{:S(2)}) collective-permute-start(bf16[128,1024]{1,0:T(8,128)(2,1)} %get-tuple-element.77.refs_1_), channel_id=1, source_target_pairs={{0,1},{1,0},{2,3},{3,2},{4,5},{5,4},{6,7},{7,6},{8,9},{9,8},{10,11... | collective-permute-start | bytes 786440 | tf_op jit(solution)/shard_map/ppermute | solution.py:270
  65.8 10.2 %collective-permute-start.21 = (bf16[128,1024]{1,0:T(8,128)(2,1)}, bf16[128,1024]{1,0:T(8,128)(2,1)}, u32[]{:S(2)}, u32[]{:S(2)}) collective-permute-start(bf16[128,1024]{1,0:T(8,128)(2,1)} %collective-permute-done.15.refs_0_), channel_id=1, source_target_pairs={{0,8},{4,12},{8,16},{12,20},{16,24},{20,28},{24,0},{28,4},{1,9},{5... | collective-permute-start | bytes 786440 | tf_op jit(solution)/shard_map/ppermute | solution.py:263
  66.8 0.7 copy-start.3
  67.6 11.9 %collective-permute-start.22 = (bf16[128,1024]{1,0:T(8,128)(2,1)}, bf16[128,1024]{1,0:T(8,128)(2,1)}, u32[]{:S(2)}, u32[]{:S(2)}) collective-permute-start(bf16[128,1024]{1,0:T(8,128)(2,1)} %collective-permute-done.16.refs_1_), channel_id=1, source_target_pairs={{0,8},{4,12},{8,16},{12,20},{16,24},{20,28},{24,0},{28,4},{1,9},{5... | collective-permute-start | bytes 786440 | tf_op jit(solution)/shard_map/ppermute | solution.py:263
  68.8 0.7 copy-start
  69.5 13.6 %collective-permute-start.17 = (bf16[128,1024]{1,0:T(8,128)(2,1)}, bf16[128,1024]{1,0:T(8,128)(2,1)}, u32[]{:S(2)}, u32[]{:S(2)}) collective-permute-start(bf16[128,1024]{1,0:T(8,128)(2,1)} %collective-permute-done.15.refs_0_), channel_id=1, source_target_pairs={{0,1},{1,0},{2,3},{3,2},{4,5},{5,4},{6,7},{7,6},{8,9},{9,8},{10,11... | collective-permute-start | bytes 786440 | tf_op jit(solution)/shard_map/ppermute | solution.py:270
  71.2 11.9 %collective-permute-start.18 = (bf16[128,1024]{1,0:T(8,128)(2,1)}, bf16[128,1024]{1,0:T(8,128)(2,1)S(1)}, u32[]{:S(2)}, u32[]{:S(2)}) collective-permute-start(bf16[128,1024]{1,0:T(8,128)(2,1)} %collective-permute-done.16.refs_1_), channel_id=1, source_target_pairs={{0,1},{1,0},{2,3},{3,2},{4,5},{5,4},{6,7},{7,6},{8,9},{9,8},{10,11... | collective-permute-start | bytes 786440 | tf_op jit(solution)/shard_map/ppermute | solution.py:270
  71.2 1.0 copy-start.1
  72.2 0.9 copy-start.4
  73.2 9.9 %copy-start.2 = (bf16[384,512]{1,0:T(8,128)(2,1)S(1)}, bf16[384,512]{1,0:T(8,128)(2,1)}, u32[]{:S(2)}) copy-start(bf16[384,512]{1,0:T(8,128)(2,1)} %copy-done) | copy-start | bytes 1179652
  76.0 10.9 %collective-permute-start.27 = (bf16[128,1024]{1,0:T(8,128)(2,1)}, bf16[128,1024]{1,0:T(8,128)(2,1)S(1)}, u32[]{:S(2)}, u32[]{:S(2)}) collective-permute-start(bf16[128,1024]{1,0:T(8,128)(2,1)} %collective-permute-done.21.refs_0_), channel_id=1, source_target_pairs={{0,8},{4,12},{8,16},{12,20},{16,24},{20,28},{24,0},{28,4},{1,9},{5... | collective-permute-start | bytes 786440 | tf_op jit(solution)/shard_map/ppermute | solution.py:263
  77.4 10.4 %collective-permute-start.23 = (bf16[128,1024]{1,0:T(8,128)(2,1)}, bf16[128,1024]{1,0:T(8,128)(2,1)S(1)}, u32[]{:S(2)}, u32[]{:S(2)}) collective-permute-start(bf16[128,1024]{1,0:T(8,128)(2,1)} %collective-permute-done.21.refs_0_), channel_id=1, source_target_pairs={{0,1},{1,0},{2,3},{3,2},{4,5},{5,4},{6,7},{7,6},{8,9},{9,8},{10,11... | collective-permute-start | bytes 786440 | tf_op jit(solution)/shard_map/ppermute | solution.py:270
  79.4 8.4 %collective-permute-start.24 = (bf16[128,1024]{1,0:T(8,128)(2,1)}, bf16[128,1024]{1,0:T(8,128)(2,1)S(1)}, u32[]{:S(2)}, u32[]{:S(2)}) collective-permute-start(bf16[128,1024]{1,0:T(8,128)(2,1)} %collective-permute-done.22.refs_1_), channel_id=1, source_target_pairs={{0,1},{1,0},{2,3},{3,2},{4,5},{5,4},{6,7},{7,6},{8,9},{9,8},{10,11... | collective-permute-start | bytes 786440 | tf_op jit(solution)/shard_map/ppermute | solution.py:270
  83.1 9.9 %collective-permute-start.34 = (bf16[128,1024]{1,0:T(8,128)(2,1)}, bf16[128,1024]{1,0:T(8,128)(2,1)S(1)}, u32[]{:S(2)}, u32[]{:S(2)}) collective-permute-start(bf16[128,1024]{1,0:T(8,128)(2,1)} %collective-permute-done.22.refs_1_), channel_id=1, source_target_pairs={{0,8},{4,12},{8,16},{12,20},{16,24},{20,28},{24,0},{28,4},{1,9},{5... | collective-permute-start | bytes 786440 | tf_op jit(solution)/shard_map/ppermute | solution.py:263
  85.8 8.0 %collective-permute-start.19 = (bf16[2,2,64,512]{3,2,1,0:T(8,128)(2,1)S(1)}, bf16[2,2,64,512]{3,2,1,0:T(8,128)(2,1)S(1)}, u32[]{:S(2)}, u32[]{:S(2)}) collective-permute-start(bf16[2,2,64,512]{3,2,1,0:T(8,128)(2,1)S(1)} %get-tuple-element.83), channel_id=1, source_target_pairs={{0,2},{1,3},{2,0},{3,1},{4,6},{5,7},{6,4},{7,5},{8,10},{9,11},{10,... | collective-permute-start | bytes 786440 | tf_op jit(solution)/shard_map/ppermute | solution.py:274
  86.9 10.6 %collective-permute-start.28 = (bf16[128,1024]{1,0:T(8,128)(2,1)S(1)}, bf16[128,1024]{1,0:T(8,128)(2,1)S(1)}, u32[]{:S(2)}, u32[]{:S(2)}) collective-permute-start(bf16[128,1024]{1,0:T(8,128)(2,1)S(1)} %collective-permute-done.27.refs_0_), channel_id=1, source_target_pairs={{0,1},{1,0},{2,3},{3,2},{4,5},{5,4},{6,7},{7,6},{8,9},{9,8},{10,11... | collective-permute-start | bytes 786440 | tf_op jit(solution)/shard_map/ppermute | solution.py:270
  90.4 9.1 %collective-permute-start.25 = (bf16[2,2,64,512]{3,2,1,0:T(8,128)(2,1)S(1)}, bf16[2,2,64,512]{3,2,1,0:T(8,128)(2,1)S(1)}, u32[]{:S(2)}, u32[]{:S(2)}) collective-permute-start(bf16[2,2,64,512]{3,2,1,0:T(8,128)(2,1)S(1)} %get-tuple-element.85), channel_id=1, source_target_pairs={{0,2},{1,3},{2,0},{3,1},{4,6},{5,7},{6,4},{7,5},{8,10},{9,11},{10,... | collective-permute-start | bytes 786440 | tf_op jit(solution)/shard_map/ppermute | solution.py:274
  91.6 13.4 %collective-permute-start.14 = (bf16[2,2,64,512]{3,2,1,0:T(8,128)(2,1)S(1)}, bf16[2,2,64,512]{3,2,1,0:T(8,128)(2,1)S(1)}, u32[]{:S(2)}, u32[]{:S(2)}) collective-permute-start(bf16[2,2,64,512]{3,2,1,0:T(8,128)(2,1)S(1)} %get-tuple-element.81), channel_id=1, source_target_pairs={{0,2},{1,3},{2,0},{3,1},{4,6},{5,7},{6,4},{7,5},{8,10},{9,11},{10,... | collective-permute-start | bytes 786440 | tf_op jit(solution)/shard_map/ppermute | solution.py:274
  93.1 12.1 %collective-permute-start.35 = (bf16[128,1024]{1,0:T(8,128)(2,1)S(1)}, bf16[128,1024]{1,0:T(8,128)(2,1)S(1)}, u32[]{:S(2)}, u32[]{:S(2)}) collective-permute-start(bf16[128,1024]{1,0:T(8,128)(2,1)S(1)} %collective-permute-done.34.refs_0_), channel_id=1, source_target_pairs={{0,1},{1,0},{2,3},{3,2},{4,5},{5,4},{6,7},{7,6},{8,9},{9,8},{10,11... | collective-permute-start | bytes 786440 | tf_op jit(solution)/shard_map/ppermute | solution.py:270
  94.6 18.4 %collective-permute-start.20 = (bf16[2,2,64,512]{3,2,1,0:T(8,128)(2,1)}, bf16[2,2,64,512]{3,2,1,0:T(8,128)(2,1)}, u32[]{:S(2)}, u32[]{:S(2)}) collective-permute-start(bf16[2,2,64,512]{3,2,1,0:T(8,128)(2,1)} %shard_map.83), channel_id=1, source_target_pairs={{0,24},{4,28},{8,0},{12,4},{16,8},{20,12},{24,16},{28,20},{1,25},{... | collective-permute-start | bytes 786440 | tf_op jit(solution)/shard_map/ppermute | solution.py:263
  98.5 10.0 %collective-permute-start.29 = (bf16[1,2,64,512]{3,2,1,0:T(8,128)(2,1)S(1)}, bf16[1,2,64,512]{3,2,1,0:T(8,128)(2,1)S(1)}, u32[]{:S(2)}, u32[]{:S(2)}) collective-permute-start(bf16[1,2,64,512]{3,2,1,0:T(8,128)(2,1)S(1)} %get-tuple-element.88), channel_id=1, source_target_pairs={{0,2},{1,3},{2,0},{3,1},{4,6},{5,7},{6,4},{7,5},{8,10},{9,11},{10,... | collective-permute-start | bytes 393224 | tf_op jit(solution)/shard_map/ppermute | solution.py:274
  100.3 18.7 %collective-permute-start.26 = (bf16[2,2,64,512]{3,2,1,0:T(8,128)(2,1)}, bf16[2,2,64,512]{3,2,1,0:T(8,128)(2,1)}, u32[]{:S(2)}, u32[]{:S(2)}) collective-permute-start(bf16[2,2,64,512]{3,2,1,0:T(8,128)(2,1)} %shard_map.85), channel_id=1, source_target_pairs={{0,16},{4,20},{8,24},{12,28},{16,0},{20,4},{24,8},{28,12},{1,17},{... | collective-permute-start | bytes 786440 | tf_op jit(solution)/shard_map/ppermute | solution.py:263
  105.1 1.6 %copy-start.7 = (bf16[2,2,64,512]{3,2,1,0:T(8,128)(2,1)}, bf16[2,2,64,512]{3,2,1,0:T(8,128)(2,1)S(1)}, u32[]{:S(2)}) copy-start(bf16[2,2,64,512]{3,2,1,0:T(8,128)(2,1)S(1)} %shard_map.81.refs_0_) | copy-start | bytes 786436
  106.8 0.7 copy-start.18
  107.5 4.4 %collective-permute-start.36 = (bf16[1,2,64,512]{3,2,1,0:T(8,128)(2,1)}, bf16[1,2,64,512]{3,2,1,0:T(8,128)(2,1)S(1)}, u32[]{:S(2)}, u32[]{:S(2)}) collective-permute-start(bf16[1,2,64,512]{3,2,1,0:T(8,128)(2,1)} %get-tuple-element.96), channel_id=1, source_target_pairs={{0,2},{1,3},{2,0},{3,1},{4,6},{5,7},{6,4},{7,5},{8,10},{9,11},{10,... | collective-permute-start | bytes 393224 | tf_op jit(solution)/shard_map/ppermute | solution.py:274
  108.5 10.6 %collective-permute-start.30 = (bf16[1,2,64,512]{3,2,1,0:T(8,128)(2,1)S(1)}, bf16[1,2,64,512]{3,2,1,0:T(8,128)(2,1)S(1)}, u32[]{:S(2)}, u32[]{:S(2)}) collective-permute-start(bf16[1,2,64,512]{3,2,1,0:T(8,128)(2,1)S(1)} %shard_map.87), channel_id=1, source_target_pairs={{0,8},{4,12},{8,16},{12,20},{16,24},{20,28},{24,0},{28,4},{1,9},{5... | collective-permute-start | bytes 393224 | tf_op jit(solution)/shard_map/ppermute | solution.py:263
  111.9 1.0 copy-start.19
  112.9 10.7 %collective-permute-start.37 = (bf16[1,2,64,512]{3,2,1,0:T(8,128)(2,1)S(1)}, bf16[1,2,64,512]{3,2,1,0:T(8,128)(2,1)S(1)}, u32[]{:S(2)}, u32[]{:S(2)}) collective-permute-start(bf16[1,2,64,512]{3,2,1,0:T(8,128)(2,1)S(1)} %shard_map.90), channel_id=1, source_target_pairs={{0,8},{4,12},{8,16},{12,20},{16,24},{20,28},{24,0},{28,4},{1,9},{5... | collective-permute-start | bytes 393224 | tf_op jit(solution)/shard_map/ppermute | solution.py:263
  119.1 1.0 copy-start.8
  121.1 6.3 %collective-permute-start.31 = (bf16[2,64,512]{2,1,0:T(8,128)(2,1)S(1)}, bf16[2,64,512]{2,1,0:T(8,128)(2,1)S(1)}, u32[]{:S(2)}, u32[]{:S(2)}) collective-permute-start(bf16[2,64,512]{2,1,0:T(8,128)(2,1)S(1)} %get-tuple-element.90), channel_id=1, source_target_pairs={{0,1},{1,2},{2,3},{3,0},{4,5},{5,6},{6,7},{7,4},{8,9},{9,10},{10,1... | collective-permute-start | bytes 393224 | tf_op jit(solution)/shard_map/ppermute | solution.py:277
  123.0 6.5 %collective-permute-start.32 = (bf16[2,64,512]{2,1,0:T(8,128)(2,1)S(1)}, bf16[2,64,512]{2,1,0:T(8,128)(2,1)S(1)}, u32[]{:S(2)}, u32[]{:S(2)}) collective-permute-start(bf16[2,64,512]{2,1,0:T(8,128)(2,1)S(1)} %get-tuple-element.91), channel_id=1, source_target_pairs={{0,2},{1,3},{2,0},{3,1},{4,6},{5,7},{6,4},{7,5},{8,10},{9,11},{10,... | collective-permute-start | bytes 393224 | tf_op jit(solution)/shard_map/ppermute | solution.py:277
  123.5 7.5 %collective-permute-start.33 = (bf16[2,64,512]{2,1,0:T(8,128)(2,1)S(1)}, bf16[2,64,512]{2,1,0:T(8,128)(2,1)S(1)}, u32[]{:S(2)}, u32[]{:S(2)}) collective-permute-start(bf16[2,64,512]{2,1,0:T(8,128)(2,1)S(1)} %get-tuple-element.92), channel_id=1, source_target_pairs={{0,3},{1,0},{2,1},{3,2},{4,7},{5,4},{6,5},{7,6},{8,11},{9,8},{10,9... | collective-permute-start | bytes 393224 | tf_op jit(solution)/shard_map/ppermute | solution.py:277
  124.6 6.7 %collective-permute-start.38 = (bf16[2,64,512]{2,1,0:T(8,128)(2,1)S(1)}, bf16[2,64,512]{2,1,0:T(8,128)(2,1)S(1)}, u32[]{:S(2)}, u32[]{:S(2)}) collective-permute-start(bf16[2,64,512]{2,1,0:T(8,128)(2,1)S(1)} %get-tuple-element.98), channel_id=1, source_target_pairs={{0,1},{1,2},{2,3},{3,0},{4,5},{5,6},{6,7},{7,4},{8,9},{9,10},{10,1... | collective-permute-start | bytes 393224 | tf_op jit(solution)/shard_map/ppermute | solution.py:277
  126.4 8.7 %collective-permute-start.39 = (bf16[2,64,512]{2,1,0:T(8,128)(2,1)S(1)}, bf16[2,64,512]{2,1,0:T(8,128)(2,1)S(1)}, u32[]{:S(2)}, u32[]{:S(2)}) collective-permute-start(bf16[2,64,512]{2,1,0:T(8,128)(2,1)S(1)} %get-tuple-element.99), channel_id=1, source_target_pairs={{0,2},{1,3},{2,0},{3,1},{4,6},{5,7},{6,4},{7,5},{8,10},{9,11},{10,... | collective-permute-start | bytes 393224 | tf_op jit(solution)/shard_map/ppermute | solution.py:277
  127.4 8.3 %collective-permute-start.40 = (bf16[2,64,512]{2,1,0:T(8,128)(2,1)S(1)}, bf16[2,64,512]{2,1,0:T(8,128)(2,1)S(1)}, u32[]{:S(2)}, u32[]{:S(2)}) collective-permute-start(bf16[2,64,512]{2,1,0:T(8,128)(2,1)S(1)} %get-tuple-element.100), channel_id=1, source_target_pairs={{0,3},{1,0},{2,1},{3,2},{4,7},{5,4},{6,5},{7,6},{8,11},{9,8},{10,9... | collective-permute-start | bytes 393224 | tf_op jit(solution)/shard_map/ppermute | solution.py:277

commit v6 on v5

--- a/solution.py
+++ b/solution.py
@@ -347,14 +347,13 @@
         if k + 1 < n_head:
             hidden = [rot_h(after(v, *outs[: max(t - 1, 0)]), 1) for v in hidden]
         other = [swap_core(v) for v in now]
-        if t > 3:
-            other[0] = after(other[0], sums[t - 4])
+        if t > 2:
+            other[0] = after(other[0], sums[1 if t == 3 else 0])
         shape = (len(chunks), r, piece, width)
         mine, *send = call(
             functools.partial(product_kernel, r, n_y, len(chunks)),
             [(shape, F32)] + [(shape, BF)] * (n_y - 1),
             (me_y, *now, *other, *weights),
-            resident=len(weights),
         )
         outs.append(mine)
         gots = [rot_y(v, j + 1) for j, v in enumerate(send)]

time: 138 us -> 137 us (level)
  starting transfers between devices: 55.7 us -> 54.1 us
    ppermute x10, starting transfers between devices: 7.96 us -> 4.08 us  [rot_h(): return lax.ppermute(v, 'seq', pairs)]
    ppermute x5, waiting for transfers between devices: 7.95 us -> 10.5 us  [rot_y(): return lax.ppermute(v, 'head', pairs)]
    ppermute x10, waiting for transfers between devices: 7.81 us -> 5.33 us  [rot_h(): return lax.ppermute(v, 'seq', pairs)]
  transfers between devices with their start and end apart: 41 -> 41, of which waited for: 18 -> 19; matrix products, arithmetic and copies ran while one was open for 0% -> 0% of each run, Pallas kernels for 15% -> 15%
where the time goes in v6:
time: 137 us
  starting transfers between devices  54.1 us (39%)
  waiting for transfers between devices  47 us (34%)
  Pallas kernels  23.8 us (17%)
  local copies, waits for them, and re-layouts  11.4 us (8%)
    ppermute x11, starting transfers between devices, swap_core(): return lax.ppermute(v, 'head', [(i, i ^ 1) for i in range(n_head)])  24.7 us
    pallas_call x20, Pallas kernels, call(): pl.pallas_call(kernel, out_shape=[jax.ShapeDtypeStruct(s, d) for s, d in...  23.8 us
    ppermute x7, waiting for transfers between devices, rot_b(): return lax.ppermute(v, 'seq', pairs)  20.6 us
    unnamed x43, local copies, waits for them, and re-layouts  11.4 us
    ppermute x5, waiting for transfers between devices, rot_y(): return lax.ppermute(v, 'head', pairs)  10.5 us
    ppermute x6, waiting for transfers between devices, rot_head(): lax.ppermute(v, 'head', [(i, (i + j) % n_head) for i in range(n_head)])  8.21 us
    ppermute x2, starting transfers between devices, shift_h(): return lax.ppermute(v, 'seq', pairs)  7.3 us
    ppermute x7, starting transfers between devices, rot_b(): return lax.ppermute(v, 'seq', pairs)  6.34 us
  transfers between devices with their start and end apart: 41, of which 19 were waited for; matrix products, arithmetic and copies ran while one was open for 0% of the time, Pallas kernels for 15%

profile of v6, /device:TPU:1, one launch (start us, length us, event | category | flops | bytes accessed | tf_op | source)
XLA Modules:
  0.0 136.7 jit_solution(7087732909923774734)
XLA Ops:
  0.0 0.8 copy.8.logs
  0.8 1.1 copy-done.10
  1.9 0.9 copy-done.16
  2.8 2.2 %shard_map.73 = (bf16[272,512]{1,0:T(8,128)(2,1)S(1)}, bf16[272,512]{1,0:T(8,128)(2,1)S(1)}) custom-call(s32[1]{0:T(128)} %bitcast.1.me, bf16[256,1024]{1,0:T(8,128)(2,1)S(1)} %copy-done.10, bf16[256,256]{1,0:T(8,128)(2,1)S(1)} %bitcast.10, f32[256,16]{1,0:T(8,128)S(1)} %copy.8.logs), custom_call_target="tpu_custom_call" | custom-call | flops 1 | bytes 1 | tf_op jit(solution)/shard_map/pallas_call | solution.py:21
  5.0 2.1 %collective-permute-start = (bf16[272,512]{1,0:T(8,128)(2,1)S(1)}, bf16[272,512]{1,0:T(8,128)(2,1)S(1)}, u32[]{:S(2)}, u32[]{:S(2)}) collective-permute-start(bf16[272,512]{1,0:T(8,128)(2,1)S(1)} %get-tuple-element.55), channel_id=1, source_target_pairs={{0,4},{4,0},{8,12},{12,8},{16,20},{20,16},{24,28},{28,24},{1,5},{5... | collective-permute-start | bytes 835592 | tf_op jit(solution)/shard_map/ppermute | solution.py:259
  7.1 1.6 %copy-done.9 = bf16[1024,1024]{1,0:T(8,128)(2,1)S(1)} copy-done((bf16[1024,1024]{1,0:T(8,128)(2,1)S(1)}, bf16[1024,1024]{1,0:T(8,128)(2,1)}, u32[]{:S(2)}) %copy-start.9) | copy-done | bytes 2097176
  9.0 1.0 collective-permute-start.5
  10.0 3.5 %collective-permute-done.refs_1_ = bf16[272,512]{1,0:T(8,128)(2,1)S(1)} collective-permute-done((bf16[272,512]{1,0:T(8,128)(2,1)S(1)}, bf16[272,512]{1,0:T(8,128)(2,1)S(1)}, u32[]{:S(2)}, u32[]{:S(2)}) %collective-permute-start) | collective-permute-done | bytes 278560 | tf_op jit(solution)/shard_map/ppermute | solution.py:259
  13.6 3.2 %collective-permute-start.1 = (bf16[272,512]{1,0:T(8,128)(2,1)S(1)}, bf16[272,512]{1,0:T(8,128)(2,1)S(1)}, u32[]{:S(2)}, u32[]{:S(2)}) collective-permute-start(bf16[272,512]{1,0:T(8,128)(2,1)S(1)} %get-tuple-element.63), channel_id=1, source_target_pairs={{0,8},{4,12},{8,16},{12,20},{16,24},{20,28},{1,9},{5,13},{9,17},{1... | collective-permute-start | bytes 835592 | tf_op jit(solution)/shard_map/ppermute | solution.py:267
  16.8 1.3 collective-permute-start.4
  18.3 1.9 %collective-permute-done.1.got = bf16[272,512]{1,0:T(8,128)(2,1)S(1)} collective-permute-done((bf16[272,512]{1,0:T(8,128)(2,1)S(1)}, bf16[272,512]{1,0:T(8,128)(2,1)S(1)}, u32[]{:S(2)}, u32[]{:S(2)}) %collective-permute-start.1) | collective-permute-done | bytes 278560 | tf_op jit(solution)/shard_map/ppermute | solution.py:267
  20.2 0.9 shard_map.76
  21.1 3.6 %collective-permute-done.2.refs_2_.refs_9_.refs_7_ = bf16[512,512]{1,0:T(8,128)(2,1)S(1)} collective-permute-done((bf16[512,512]{1,0:T(8,128)(2,1)S(1)}, bf16[512,512]{1,0:T(8,128)(2,1)S(1)}, u32[]{:S(2)}, u32[]{:S(2)}) %collective-permute-start.2) | collective-permute-done | bytes 524320 | tf_op jit(solution)/shard_map/ppermute | solution.py:259
  24.8 4.2 %collective-permute-start.3 = (bf16[272,512]{1,0:T(8,128)(2,1)S(1)}, bf16[272,512]{1,0:T(8,128)(2,1)S(1)}, u32[]{:S(2)}, u32[]{:S(2)}) collective-permute-start(bf16[272,512]{1,0:T(8,128)(2,1)S(1)} %get-tuple-element.67), channel_id=1, source_target_pairs={{0,16},{4,20},{8,24},{12,28},{1,17},{5,21},{9,25},{13,29},{2,18},{... | collective-permute-start | bytes 835592 | tf_op jit(solution)/shard_map/ppermute | solution.py:267
  28.9 3.0 %collective-permute-start.11 = (bf16[384,512]{1,0:T(8,128)(2,1)S(1)}, bf16[384,512]{1,0:T(8,128)(2,1)S(1)}, u32[]{:S(2)}, u32[]{:S(2)}) collective-permute-start(bf16[384,512]{1,0:T(8,128)(2,1)S(1)} %get-tuple-element.62), channel_id=1, source_target_pairs={{0,1},{1,0},{2,3},{3,2},{4,5},{5,4},{6,7},{7,6},{8,9},{9,8},{10,11... | collective-permute-start | bytes 1179656 | tf_op jit(solution)/shard_map/ppermute | solution.py:270
  32.4 1.0 copy-done.6
  33.6 2.4 %collective-permute-done.4.refs_3_.refs_10_.refs_8_ = bf16[512,512]{1,0:T(8,128)(2,1)S(1)} collective-permute-done((bf16[512,512]{1,0:T(8,128)(2,1)S(1)}, bf16[512,512]{1,0:T(8,128)(2,1)S(1)}, u32[]{:S(2)}, u32[]{:S(2)}) %collective-permute-start.4) | collective-permute-done | bytes 524320 | tf_op jit(solution)/shard_map/ppermute | solution.py:259
  36.0 8.4 %collective-permute-done.6.refs_4_.refs_11_.refs_9_ = bf16[384,512]{1,0:T(8,128)(2,1)S(1)} collective-permute-done((bf16[384,512]{1,0:T(8,128)(2,1)S(1)}, bf16[384,512]{1,0:T(8,128)(2,1)S(1)}, u32[]{:S(2)}, u32[]{:S(2)}) %collective-permute-start.6) | collective-permute-done | bytes 393248 | tf_op jit(solution)/shard_map/ppermute | solution.py:259
  44.4 1.1 collective-permute-start.7
  45.6 1.8 %collective-permute-start.10 = (bf16[256,512]{1,0:T(8,128)(2,1)S(1)}, bf16[256,512]{1,0:T(8,128)(2,1)S(1)}, u32[]{:S(2)}, u32[]{:S(2)}) collective-permute-start(bf16[256,512]{1,0:T(8,128)(2,1)S(1)} %get-tuple-element.61), channel_id=1, source_target_pairs={{0,1},{1,0},{2,3},{3,2},{4,5},{5,4},{6,7},{7,6},{8,9},{9,8},{10,11... | collective-permute-start | bytes 786440 | tf_op jit(solution)/shard_map/ppermute | solution.py:270
  47.4 2.9 %shard_map.78 = (f32[256,1024]{1,0:T(8,128)S(1)}, f32[256,1024]{1,0:T(8,128)S(1)}, f32[256,1024]{1,0:T(8,128)S(1)}) custom-call(s32[1]{0:T(128)} %bitcast.1.me, bf16[256,1024]{1,0:T(8,128)(2,1)S(1)} %copy-done.11, bf16[256,1024]{1,0:T(8,128)(2,1)S(1)} %copy-done.14, bf16[256,256]{1,0:T(8,128)(2,1)S(1)} %bitcast.11, bf16[256,256]{1,0:T(8,128)(2,1)S(1)} %bitcast.8, ...), custom_call_target="tpu_custom_call" | custom-call | flops 1 | bytes 1 | tf_op jit(solution)/shard_map/pallas_call | solution.py:21
  51.0 1.3 shard_map.79
  52.3 0.9 collective-permute-start.15
  53.2 1.3 collective-permute-start.16
  54.5 1.2 collective-permute-start.13
  56.0 3.6 %collective-permute-start.8 = (bf16[128,1024]{1,0:T(8,128)(2,1)}, bf16[128,1024]{1,0:T(8,128)(2,1)}, u32[]{:S(2)}, u32[]{:S(2)}) collective-permute-start(bf16[128,1024]{1,0:T(8,128)(2,1)} %get-tuple-element.77.refs_0_), channel_id=1, source_target_pairs={{0,1},{1,0},{2,3},{3,2},{4,5},{5,4},{6,7},{7,6},{8,9},{9,8},{10,11... | collective-permute-start | bytes 786440 | tf_op jit(solution)/shard_map/ppermute | solution.py:270
  60.0 5.8 %collective-permute-start.9 = (bf16[128,1024]{1,0:T(8,128)(2,1)}, bf16[128,1024]{1,0:T(8,128)(2,1)}, u32[]{:S(2)}, u32[]{:S(2)}) collective-permute-start(bf16[128,1024]{1,0:T(8,128)(2,1)} %get-tuple-element.78.refs_1_), channel_id=1, source_target_pairs={{0,1},{1,0},{2,3},{3,2},{4,5},{5,4},{6,7},{7,6},{8,9},{9,8},{10,11... | collective-permute-start | bytes 786440 | tf_op jit(solution)/shard_map/ppermute | solution.py:270
  65.8 2.0 %collective-permute-done.12.refs_12_.refs_10_ = bf16[256,512]{1,0:T(8,128)(2,1)S(1)} collective-permute-done((bf16[256,512]{1,0:T(8,128)(2,1)S(1)}, bf16[256,512]{1,0:T(8,128)(2,1)S(1)}, u32[]{:S(2)}, u32[]{:S(2)}) %collective-permute-start.12) | collective-permute-done | bytes 262176 | tf_op jit(solution)/shard_map/ppermute | solution.py:259
  67.8 0.7 copy-done.3
  68.5 1.2 collective-permute-start.22
  69.7 0.7 copy-done
  70.4 4.2 %collective-permute-start.17 = (bf16[128,1024]{1,0:T(8,128)(2,1)}, bf16[128,1024]{1,0:T(8,128)(2,1)}, u32[]{:S(2)}, u32[]{:S(2)}) collective-permute-start(bf16[128,1024]{1,0:T(8,128)(2,1)} %collective-permute-done.15.refs_0_), channel_id=1, source_target_pairs={{0,1},{1,0},{2,3},{3,2},{4,5},{5,4},{6,7},{7,6},{8,9},{9,8},{10,11... | collective-permute-start | bytes 786440 | tf_op jit(solution)/shard_map/ppermute | solution.py:270
  74.7 1.0 copy-done.1
  75.7 0.9 copy-done.4
  76.6 2.8 %shard_map.80 = (f32[2,2,64,512]{3,2,1,0:T(8,128)S(1)}, bf16[2,2,64,512]{3,2,1,0:T(8,128)(2,1)S(1)}) custom-call(s32[1]{0:T(128)} %bitcast.3.me, bf16[128,1024]{1,0:T(8,128)(2,1)} %get-tuple-element.77.refs_0_, bf16[128,1024]{1,0:T(8,128)(2,1)} %get-tuple-element.78.refs_1_, bf16[128,1024]{1,0:T(8,128)(2,1)} %collective-permute-done.8.refs_2_, ...), custom_call_target="tpu_custom_call" | custom-call | flops 1 | bytes 1 | tf_op jit(solution)/shard_map/pallas_call | solution.py:21
  79.9 0.8 collective-permute-start.23
  80.6 1.6 %collective-permute-start.24 = (bf16[128,1024]{1,0:T(8,128)(2,1)}, bf16[128,1024]{1,0:T(8,128)(2,1)S(1)}, u32[]{:S(2)}, u32[]{:S(2)}) collective-permute-start(bf16[128,1024]{1,0:T(8,128)(2,1)} %collective-permute-done.22.refs_1_), channel_id=1, source_target_pairs={{0,1},{1,0},{2,3},{3,2},{4,5},{5,4},{6,7},{7,6},{8,9},{9,8},{10,11... | collective-permute-start | bytes 786440 | tf_op jit(solution)/shard_map/ppermute | solution.py:270
  82.3 2.7 %shard_map.82 = (f32[2,2,64,512]{3,2,1,0:T(8,128)S(1)}, bf16[2,2,64,512]{3,2,1,0:T(8,128)(2,1)S(1)}) custom-call(s32[1]{0:T(128)} %bitcast.3.me, bf16[128,1024]{1,0:T(8,128)(2,1)} %collective-permute-done.15.refs_0_, bf16[128,1024]{1,0:T(8,128)(2,1)} %collective-permute-done.16.refs_1_, bf16[128,1024]{1,0:T(8,128)(2,1)} %collective-permute-done.17.refs_2_, ...), custom_call_target="tpu_custom_call" | custom-call | flops 1 | bytes 1 | tf_op jit(solution)/shard_map/pallas_call | solution.py:21
  85.0 1.2 collective-permute-start.19
  86.2 2.7 %collective-permute-done.27.refs_0_ = bf16[128,1024]{1,0:T(8,128)(2,1)S(1)} collective-permute-done((bf16[128,1024]{1,0:T(8,128)(2,1)}, bf16[128,1024]{1,0:T(8,128)(2,1)S(1)}, u32[]{:S(2)}, u32[]{:S(2)}) %collective-permute-start.27) | collective-permute-done | bytes 262176 | tf_op jit(solution)/shard_map/ppermute | solution.py:263
  88.9 2.3 %collective-permute-start.28 = (bf16[128,1024]{1,0:T(8,128)(2,1)S(1)}, bf16[128,1024]{1,0:T(8,128)(2,1)S(1)}, u32[]{:S(2)}, u32[]{:S(2)}) collective-permute-start(bf16[128,1024]{1,0:T(8,128)(2,1)S(1)} %collective-permute-done.27.refs_0_), channel_id=1, source_target_pairs={{0,1},{1,0},{2,3},{3,2},{4,5},{5,4},{6,7},{7,6},{8,9},{9,8},{10,11... | collective-permute-start | bytes 786440 | tf_op jit(solution)/shard_map/ppermute | solution.py:270
  91.2 2.6 %shard_map.84 = (f32[2,2,64,512]{3,2,1,0:T(8,128)S(1)}, bf16[2,2,64,512]{3,2,1,0:T(8,128)(2,1)S(1)}) custom-call(s32[1]{0:T(128)} %bitcast.3.me, bf16[128,1024]{1,0:T(8,128)(2,1)} %collective-permute-done.21.refs_0_, bf16[128,1024]{1,0:T(8,128)(2,1)} %collective-permute-done.22.refs_1_, bf16[128,1024]{1,0:T(8,128)(2,1)S(1)} %collective-permute-done.23.refs_2_, ...), custom_call_target="tpu_custom_call" | custom-call | flops 1 | bytes 1 | tf_op jit(solution)/shard_map/pallas_call | solution.py:21
  93.8 1.4 collective-permute-start.25
  96.0 0.7 shard_map.83
  96.9 1.0 shard_map.86
  97.8 1.4 %collective-permute-start.29 = (bf16[1,2,64,512]{3,2,1,0:T(8,128)(2,1)S(1)}, bf16[1,2,64,512]{3,2,1,0:T(8,128)(2,1)S(1)}, u32[]{:S(2)}, u32[]{:S(2)}) collective-permute-start(bf16[1,2,64,512]{3,2,1,0:T(8,128)(2,1)S(1)} %get-tuple-element.90), channel_id=1, source_target_pairs={{0,2},{1,3},{2,0},{3,1},{4,6},{5,7},{6,4},{7,5},{8,10},{9,11},{10,... | collective-permute-start | bytes 393224 | tf_op jit(solution)/shard_map/ppermute | solution.py:274
  99.2 2.7 %collective-permute-done.25.refs_0_ = bf16[2,2,64,512]{3,2,1,0:T(8,128)(2,1)S(1)} collective-permute-done((bf16[2,2,64,512]{3,2,1,0:T(8,128)(2,1)S(1)}, bf16[2,2,64,512]{3,2,1,0:T(8,128)(2,1)S(1)}, u32[]{:S(2)}, u32[]{:S(2)}) %collective-permute-start.25) | collective-permute-done | bytes 262176 | tf_op jit(solution)/shard_map/ppermute | solution.py:274
  101.9 0.8 shard_map.85
  102.7 4.7 %collective-permute-done.14.refs_0_ = bf16[2,2,64,512]{3,2,1,0:T(8,128)(2,1)S(1)} collective-permute-done((bf16[2,2,64,512]{3,2,1,0:T(8,128)(2,1)S(1)}, bf16[2,2,64,512]{3,2,1,0:T(8,128)(2,1)S(1)}, u32[]{:S(2)}, u32[]{:S(2)}) %collective-permute-start.14) | collective-permute-done | bytes 262176 | tf_op jit(solution)/shard_map/ppermute | solution.py:274
  107.5 1.6 %shard_map.89 = (f32[1,2,64,512]{3,2,1,0:T(8,128)S(1)}, bf16[1,2,64,512]{3,2,1,0:T(8,128)(2,1)}) custom-call(s32[1]{0:T(128)} %bitcast.3.me, bf16[128,1024]{1,0:T(8,128)(2,1)S(1)} %collective-permute-done.34.refs_0_, bf16[128,1024]{1,0:T(8,128)(2,1)S(1)} %collective-permute-done.35.refs_1_, bf16[512,512]{1,0:T(8,128)(2,1)S(1)} %get-tuple-element.58.refs_4_.refs_2_, ...), custom_call_target="tpu_custom_call" | custom-call | flops 1 | bytes 1 | tf_op jit(solution)/shard_map/pallas_call | solution.py:21
  109.1 0.7 copy-done.18
  109.8 1.3 collective-permute-start.36
  111.3 3.0 %collective-permute-done.36.refs_0_ = bf16[1,2,64,512]{3,2,1,0:T(8,128)(2,1)S(1)} collective-permute-done((bf16[1,2,64,512]{3,2,1,0:T(8,128)(2,1)}, bf16[1,2,64,512]{3,2,1,0:T(8,128)(2,1)S(1)}, u32[]{:S(2)}, u32[]{:S(2)}) %collective-permute-start.36) | collective-permute-done | bytes 131104 | tf_op jit(solution)/shard_map/ppermute | solution.py:274
  114.3 0.9 copy-done.19
  115.3 2.1 %collective-permute-done.26.refs_2_ = bf16[2,2,64,512]{3,2,1,0:T(8,128)(2,1)} collective-permute-done((bf16[2,2,64,512]{3,2,1,0:T(8,128)(2,1)}, bf16[2,2,64,512]{3,2,1,0:T(8,128)(2,1)}, u32[]{:S(2)}, u32[]{:S(2)}) %collective-permute-start.26) | collective-permute-done | bytes 262176 | tf_op jit(solution)/shard_map/ppermute | solution.py:263
  117.5 0.9 copy-done.8
  118.4 1.1 shard_map.88
  119.5 2.8 %collective-permute-start.31 = (bf16[2,64,512]{2,1,0:T(8,128)(2,1)S(1)}, bf16[2,64,512]{2,1,0:T(8,128)(2,1)S(1)}, u32[]{:S(2)}, u32[]{:S(2)}) collective-permute-start(bf16[2,64,512]{2,1,0:T(8,128)(2,1)S(1)} %get-tuple-element.92), channel_id=1, source_target_pairs={{0,1},{1,2},{2,3},{3,0},{4,5},{5,6},{6,7},{7,4},{8,9},{9,10},{10,1... | collective-permute-start | bytes 393224 | tf_op jit(solution)/shard_map/ppermute | solution.py:277
  122.9 1.1 shard_map.91
  124.0 2.3 %collective-permute-start.38 = (bf16[2,64,512]{2,1,0:T(8,128)(2,1)S(1)}, bf16[2,64,512]{2,1,0:T(8,128)(2,1)S(1)}, u32[]{:S(2)}, u32[]{:S(2)}) collective-permute-start(bf16[2,64,512]{2,1,0:T(8,128)(2,1)S(1)} %get-tuple-element.100), channel_id=1, source_target_pairs={{0,1},{1,2},{2,3},{3,0},{4,5},{5,6},{6,7},{7,4},{8,9},{9,10},{10,1... | collective-permute-start | bytes 393224 | tf_op jit(solution)/shard_map/ppermute | solution.py:277
  126.9 2.0 %collective-permute-done.32.refs_2_ = bf16[2,64,512]{2,1,0:T(8,128)(2,1)S(1)} collective-permute-done((bf16[2,64,512]{2,1,0:T(8,128)(2,1)S(1)}, bf16[2,64,512]{2,1,0:T(8,128)(2,1)S(1)}, u32[]{:S(2)}, u32[]{:S(2)}) %collective-permute-start.32) | collective-permute-done | bytes 131104 | tf_op jit(solution)/shard_map/ppermute | solution.py:277
  128.9 1.5 %collective-permute-done.33.refs_3_ = bf16[2,64,512]{2,1,0:T(8,128)(2,1)S(1)} collective-permute-done((bf16[2,64,512]{2,1,0:T(8,128)(2,1)S(1)}, bf16[2,64,512]{2,1,0:T(8,128)(2,1)S(1)}, u32[]{:S(2)}, u32[]{:S(2)}) %collective-permute-start.33) | collective-permute-done | bytes 131104 | tf_op jit(solution)/shard_map/ppermute | solution.py:277
  130.6 3.9 %collective-permute-done.39.refs_6_ = bf16[2,64,512]{2,1,0:T(8,128)(2,1)S(1)} collective-permute-done((bf16[2,64,512]{2,1,0:T(8,128)(2,1)S(1)}, bf16[2,64,512]{2,1,0:T(8,128)(2,1)S(1)}, u32[]{:S(2)}, u32[]{:S(2)}) %collective-permute-start.39) | collective-permute-done | bytes 131104 | tf_op jit(solution)/shard_map/ppermute | solution.py:277
  135.1 1.6 %shard_map.92 = bf16[256,2048]{1,0:T(8,128)(2,1)} custom-call(s32[2]{0:T(128)S(1)} %pad_add_fusion.me, bf16[2,64,512]{2,1,0:T(8,128)(2,1)S(1)} %get-tuple-element.91.refs_0_, bf16[2,64,512]{2,1,0:T(8,128)(2,1)S(1)} %collective-permute-done.31.refs_1_, bf16[2,64,512]{2,1,0:T(8,128)(2,1)S(1)} %collective-permute-done.32.refs_2_, ...), custom_call_target="tpu_custom_call" | custom-call | flops 1 | bytes 1 | tf_op jit(solution)/shard_map/pallas_call | solution.py:21
  (82 shorter events, 6.3 us)
Async XLA Ops:
  0.8 8.1 %copy-start.12 = (f32[256,16]{1,0:T(8,128)}, f32[256,16]{1,0:T(8,128)S(1)}, u32[]{:S(2)}) copy-start(f32[256,16]{1,0:T(8,128)S(1)} %copy.8.logs) | copy-start | bytes 49156
  0.8 1.1 copy-start.10
  1.9 0.9 copy-start.16
  5.0 8.5 %collective-permute-start = (bf16[272,512]{1,0:T(8,128)(2,1)S(1)}, bf16[272,512]{1,0:T(8,128)(2,1)S(1)}, u32[]{:S(2)}, u32[]{:S(2)}) collective-permute-start(bf16[272,512]{1,0:T(8,128)(2,1)S(1)} %get-tuple-element.55), channel_id=1, source_target_pairs={{0,4},{4,0},{8,12},{12,8},{16,20},{20,16},{24,28},{28,24},{1,5},{5... | collective-permute-start | bytes 835592 | tf_op jit(solution)/shard_map/ppermute | solution.py:259
  7.1 1.6 %copy-start.9 = (bf16[1024,1024]{1,0:T(8,128)(2,1)S(1)}, bf16[1024,1024]{1,0:T(8,128)(2,1)}, u32[]{:S(2)}) copy-start(bf16[1024,1024]{1,0:T(8,128)(2,1)} %w_out) | copy-start | bytes 6291460
  8.9 38.5 %copy-start.11 = (bf16[256,1024]{1,0:T(8,128)(2,1)S(1)}, bf16[256,1024]{1,0:T(8,128)(2,1)}, u32[]{:S(2)}) copy-start(bf16[256,1024]{1,0:T(8,128)(2,1)} %x.3) | copy-start | bytes 1572868
  8.9 38.5 %copy-start.14 = (bf16[256,1024]{1,0:T(8,128)(2,1)S(1)}, bf16[256,1024]{1,0:T(8,128)(2,1)}, u32[]{:S(2)}) copy-start(bf16[256,1024]{1,0:T(8,128)(2,1)} %z) | copy-start | bytes 1572868
  8.9 38.5 %copy-start.15 = (bf16[256,1,256]{2,0,1:T(8,128)(2,1)S(1)}, bf16[256,1,256]{2,0,1:T(8,128)(2,1)}, u32[]{:S(2)}) copy-start(bf16[256,1,256]{2,0,1:T(8,128)(2,1)} %param.10) | copy-start | bytes 393220
  8.9 38.5 %copy-start.17 = (bf16[256,1,256]{2,0,1:T(8,128)(2,1)S(1)}, bf16[256,1,256]{2,0,1:T(8,128)(2,1)}, u32[]{:S(2)}) copy-start(bf16[256,1,256]{2,0,1:T(8,128)(2,1)} %param.9) | copy-start | bytes 393220
  8.9 38.5 %copy-start.13 = (f32[256,16]{1,0:T(8,128)S(1)}, f32[256,16]{1,0:T(8,128)}, u32[]{:S(2)}) copy-start(f32[256,16]{1,0:T(8,128)} %copy-done.12) | copy-start | bytes 49156
  8.9 15.8 %collective-permute-start.2 = (bf16[512,512]{1,0:T(8,128)(2,1)S(1)}, bf16[512,512]{1,0:T(8,128)(2,1)S(1)}, u32[]{:S(2)}, u32[]{:S(2)}) collective-permute-start(bf16[512,512]{1,0:T(8,128)(2,1)S(1)} %get-tuple-element.58.refs_4_.refs_2_), channel_id=1, source_target_pairs={{0,4},{4,0},{8,12},{12,8},{16,20},{20,16},{24,28},{28,24},{1,5},{5... | collective-permute-start | bytes 1572872 | tf_op jit(solution)/shard_map/ppermute | solution.py:259
  9.0 9.0 %collective-permute-start.5 = (bf16[384,512]{1,0:T(8,128)(2,1)S(1)}, bf16[384,512]{1,0:T(8,128)(2,1)S(1)}, u32[]{:S(2)}, u32[]{:S(2)}) collective-permute-start(bf16[384,512]{1,0:T(8,128)(2,1)S(1)} %get-tuple-element.60), channel_id=1, source_target_pairs={{0,1},{1,0},{2,3},{3,2},{4,5},{5,4},{6,7},{7,6},{8,9},{9,8},{10,11... | collective-permute-start | bytes 1179656 | tf_op jit(solution)/shard_map/ppermute | solution.py:270
  13.5 11.2 %copy-start.5 = (bf16[272,512]{1,0:T(8,128)(2,1)}, bf16[272,512]{1,0:T(8,128)(2,1)S(1)}, u32[]{:S(2)}) copy-start(bf16[272,512]{1,0:T(8,128)(2,1)S(1)} %collective-permute-done.refs_1_) | copy-start | bytes 835588
  13.6 6.6 %collective-permute-start.1 = (bf16[272,512]{1,0:T(8,128)(2,1)S(1)}, bf16[272,512]{1,0:T(8,128)(2,1)S(1)}, u32[]{:S(2)}, u32[]{:S(2)}) collective-permute-start(bf16[272,512]{1,0:T(8,128)(2,1)S(1)} %get-tuple-element.63), channel_id=1, source_target_pairs={{0,8},{4,12},{8,16},{12,20},{16,24},{20,28},{1,9},{5,13},{9,17},{1... | collective-permute-start | bytes 835592 | tf_op jit(solution)/shard_map/ppermute | solution.py:267
  16.8 19.2 %collective-permute-start.4 = (bf16[512,512]{1,0:T(8,128)(2,1)S(1)}, bf16[512,512]{1,0:T(8,128)(2,1)S(1)}, u32[]{:S(2)}, u32[]{:S(2)}) collective-permute-start(bf16[512,512]{1,0:T(8,128)(2,1)S(1)} %get-tuple-element.59.refs_5_.refs_3_), channel_id=1, source_target_pairs={{0,4},{4,0},{8,12},{12,8},{16,20},{20,16},{24,28},{28,24},{1,5},{5... | collective-permute-start | bytes 1572872 | tf_op jit(solution)/shard_map/ppermute | solution.py:259
  18.0 26.4 %collective-permute-start.6 = (bf16[384,512]{1,0:T(8,128)(2,1)S(1)}, bf16[384,512]{1,0:T(8,128)(2,1)S(1)}, u32[]{:S(2)}, u32[]{:S(2)}) collective-permute-start(bf16[384,512]{1,0:T(8,128)(2,1)S(1)} %collective-permute-done.5.refs_6_.refs_4_), channel_id=1, source_target_pairs={{0,4},{4,0},{8,12},{12,8},{16,20},{20,16},{24,28},{28,24},{1,5},{5... | collective-permute-start | bytes 1179656 | tf_op jit(solution)/shard_map/ppermute | solution.py:259
  20.2 30.8 %copy-start.20 = (f32[1024]{0:T(1024)S(1)}, f32[1024]{0:T(1024)}, u32[]{:S(2)}) copy-start(f32[1024]{0:T(1024)} %param.12) | copy-start | bytes 12292
  24.8 7.7 %collective-permute-start.3 = (bf16[272,512]{1,0:T(8,128)(2,1)S(1)}, bf16[272,512]{1,0:T(8,128)(2,1)S(1)}, u32[]{:S(2)}, u32[]{:S(2)}) collective-permute-start(bf16[272,512]{1,0:T(8,128)(2,1)S(1)} %get-tuple-element.67), channel_id=1, source_target_pairs={{0,16},{4,20},{8,24},{12,28},{1,17},{5,21},{9,25},{13,29},{2,18},{... | collective-permute-start | bytes 835592 | tf_op jit(solution)/shard_map/ppermute | solution.py:267
  28.9 21.4 %collective-permute-start.11 = (bf16[384,512]{1,0:T(8,128)(2,1)S(1)}, bf16[384,512]{1,0:T(8,128)(2,1)S(1)}, u32[]{:S(2)}, u32[]{:S(2)}) collective-permute-start(bf16[384,512]{1,0:T(8,128)(2,1)S(1)} %get-tuple-element.62), channel_id=1, source_target_pairs={{0,1},{1,0},{2,3},{3,2},{4,5},{5,4},{6,7},{7,6},{8,9},{9,8},{10,11... | collective-permute-start | bytes 1179656 | tf_op jit(solution)/shard_map/ppermute | solution.py:270
  32.4 1.0 copy-start.6
  44.4 6.6 %collective-permute-start.7 = (bf16[256,512]{1,0:T(8,128)(2,1)S(1)}, bf16[256,512]{1,0:T(8,128)(2,1)S(1)}, u32[]{:S(2)}, u32[]{:S(2)}) collective-permute-start(bf16[256,512]{1,0:T(8,128)(2,1)S(1)} %get-tuple-element.76), channel_id=1, source_target_pairs={{0,4},{4,0},{8,12},{12,8},{16,20},{20,16},{24,28},{28,24},{1,5},{5... | collective-permute-start | bytes 786440 | tf_op jit(solution)/shard_map/ppermute | solution.py:259
  45.6 10.1 %collective-permute-start.10 = (bf16[256,512]{1,0:T(8,128)(2,1)S(1)}, bf16[256,512]{1,0:T(8,128)(2,1)S(1)}, u32[]{:S(2)}, u32[]{:S(2)}) collective-permute-start(bf16[256,512]{1,0:T(8,128)(2,1)S(1)} %get-tuple-element.61), channel_id=1, source_target_pairs={{0,1},{1,0},{2,3},{3,2},{4,5},{5,4},{6,7},{7,6},{8,9},{9,8},{10,11... | collective-permute-start | bytes 786440 | tf_op jit(solution)/shard_map/ppermute | solution.py:270
  52.3 7.8 %collective-permute-start.15 = (bf16[128,1024]{1,0:T(8,128)(2,1)}, bf16[128,1024]{1,0:T(8,128)(2,1)}, u32[]{:S(2)}, u32[]{:S(2)}) collective-permute-start(bf16[128,1024]{1,0:T(8,128)(2,1)} %get-tuple-element.77.refs_0_), channel_id=1, source_target_pairs={{0,8},{4,12},{8,16},{12,20},{16,24},{20,28},{24,0},{28,4},{1,9},{5... | collective-permute-start | bytes 786440 | tf_op jit(solution)/shard_map/ppermute | solution.py:263
  53.2 12.6 %collective-permute-start.16 = (bf16[128,1024]{1,0:T(8,128)(2,1)}, bf16[128,1024]{1,0:T(8,128)(2,1)}, u32[]{:S(2)}, u32[]{:S(2)}) collective-permute-start(bf16[128,1024]{1,0:T(8,128)(2,1)} %get-tuple-element.78.refs_1_), channel_id=1, source_target_pairs={{0,8},{4,12},{8,16},{12,20},{16,24},{20,28},{24,0},{28,4},{1,9},{5... | collective-permute-start | bytes 786440 | tf_op jit(solution)/shard_map/ppermute | solution.py:263
  54.5 15.2 %collective-permute-start.13 = (bf16[384,512]{1,0:T(8,128)(2,1)S(1)}, bf16[384,512]{1,0:T(8,128)(2,1)S(1)}, u32[]{:S(2)}, u32[]{:S(2)}) collective-permute-start(bf16[384,512]{1,0:T(8,128)(2,1)S(1)} %collective-permute-done.11.refs_8_.refs_6_), channel_id=1, source_target_pairs={{0,4},{4,0},{8,12},{12,8},{16,20},{20,16},{24,28},{28,24},{1,5},{5... | collective-permute-start | bytes 1179656 | tf_op jit(solution)/shard_map/ppermute | solution.py:259
  55.7 12.1 %collective-permute-start.12 = (bf16[256,512]{1,0:T(8,128)(2,1)S(1)}, bf16[256,512]{1,0:T(8,128)(2,1)S(1)}, u32[]{:S(2)}, u32[]{:S(2)}) collective-permute-start(bf16[256,512]{1,0:T(8,128)(2,1)S(1)} %collective-permute-done.10.refs_7_.refs_5_), channel_id=1, source_target_pairs={{0,4},{4,0},{8,12},{12,8},{16,20},{20,16},{24,28},{28,24},{1,5},{5... | collective-permute-start | bytes 786440 | tf_op jit(solution)/shard_map/ppermute | solution.py:259
  56.0 18.7 %collective-permute-start.8 = (bf16[128,1024]{1,0:T(8,128)(2,1)}, bf16[128,1024]{1,0:T(8,128)(2,1)}, u32[]{:S(2)}, u32[]{:S(2)}) collective-permute-start(bf16[128,1024]{1,0:T(8,128)(2,1)} %get-tuple-element.77.refs_0_), channel_id=1, source_target_pairs={{0,1},{1,0},{2,3},{3,2},{4,5},{5,4},{6,7},{7,6},{8,9},{9,8},{10,11... | collective-permute-start | bytes 786440 | tf_op jit(solution)/shard_map/ppermute | solution.py:270
  60.0 14.7 %collective-permute-start.9 = (bf16[128,1024]{1,0:T(8,128)(2,1)}, bf16[128,1024]{1,0:T(8,128)(2,1)}, u32[]{:S(2)}, u32[]{:S(2)}) collective-permute-start(bf16[128,1024]{1,0:T(8,128)(2,1)} %get-tuple-element.78.refs_1_), channel_id=1, source_target_pairs={{0,1},{1,0},{2,3},{3,2},{4,5},{5,4},{6,7},{7,6},{8,9},{9,8},{10,11... | collective-permute-start | bytes 786440 | tf_op jit(solution)/shard_map/ppermute | solution.py:270
  65.8 13.7 %collective-permute-start.21 = (bf16[128,1024]{1,0:T(8,128)(2,1)}, bf16[128,1024]{1,0:T(8,128)(2,1)}, u32[]{:S(2)}, u32[]{:S(2)}) collective-permute-start(bf16[128,1024]{1,0:T(8,128)(2,1)} %collective-permute-done.15.refs_0_), channel_id=1, source_target_pairs={{0,8},{4,12},{8,16},{12,20},{16,24},{20,28},{24,0},{28,4},{1,9},{5... | collective-permute-start | bytes 786440 | tf_op jit(solution)/shard_map/ppermute | solution.py:263
  67.8 0.7 copy-start.3
  68.5 12.1 %collective-permute-start.22 = (bf16[128,1024]{1,0:T(8,128)(2,1)}, bf16[128,1024]{1,0:T(8,128)(2,1)}, u32[]{:S(2)}, u32[]{:S(2)}) collective-permute-start(bf16[128,1024]{1,0:T(8,128)(2,1)} %collective-permute-done.16.refs_1_), channel_id=1, source_target_pairs={{0,8},{4,12},{8,16},{12,20},{16,24},{20,28},{24,0},{28,4},{1,9},{5... | collective-permute-start | bytes 786440 | tf_op jit(solution)/shard_map/ppermute | solution.py:263
  69.7 0.7 copy-start
  70.4 11.8 %collective-permute-start.17 = (bf16[128,1024]{1,0:T(8,128)(2,1)}, bf16[128,1024]{1,0:T(8,128)(2,1)}, u32[]{:S(2)}, u32[]{:S(2)}) collective-permute-start(bf16[128,1024]{1,0:T(8,128)(2,1)} %collective-permute-done.15.refs_0_), channel_id=1, source_target_pairs={{0,1},{1,0},{2,3},{3,2},{4,5},{5,4},{6,7},{7,6},{8,9},{9,8},{10,11... | collective-permute-start | bytes 786440 | tf_op jit(solution)/shard_map/ppermute | solution.py:270
  74.7 7.6 %collective-permute-start.18 = (bf16[128,1024]{1,0:T(8,128)(2,1)}, bf16[128,1024]{1,0:T(8,128)(2,1)S(1)}, u32[]{:S(2)}, u32[]{:S(2)}) collective-permute-start(bf16[128,1024]{1,0:T(8,128)(2,1)} %collective-permute-done.16.refs_1_), channel_id=1, source_target_pairs={{0,1},{1,0},{2,3},{3,2},{4,5},{5,4},{6,7},{7,6},{8,9},{9,8},{10,11... | collective-permute-start | bytes 786440 | tf_op jit(solution)/shard_map/ppermute | solution.py:270
  74.7 1.0 copy-start.1
  75.7 0.9 copy-start.4
  76.6 5.6 %copy-start.2 = (bf16[384,512]{1,0:T(8,128)(2,1)S(1)}, bf16[384,512]{1,0:T(8,128)(2,1)}, u32[]{:S(2)}) copy-start(bf16[384,512]{1,0:T(8,128)(2,1)} %copy-done) | copy-start | bytes 1179652
  79.5 9.4 %collective-permute-start.27 = (bf16[128,1024]{1,0:T(8,128)(2,1)}, bf16[128,1024]{1,0:T(8,128)(2,1)S(1)}, u32[]{:S(2)}, u32[]{:S(2)}) collective-permute-start(bf16[128,1024]{1,0:T(8,128)(2,1)} %collective-permute-done.21.refs_0_), channel_id=1, source_target_pairs={{0,8},{4,12},{8,16},{12,20},{16,24},{20,28},{24,0},{28,4},{1,9},{5... | collective-permute-start | bytes 786440 | tf_op jit(solution)/shard_map/ppermute | solution.py:263
  79.9 11.4 %collective-permute-start.23 = (bf16[128,1024]{1,0:T(8,128)(2,1)}, bf16[128,1024]{1,0:T(8,128)(2,1)S(1)}, u32[]{:S(2)}, u32[]{:S(2)}) collective-permute-start(bf16[128,1024]{1,0:T(8,128)(2,1)} %collective-permute-done.21.refs_0_), channel_id=1, source_target_pairs={{0,1},{1,0},{2,3},{3,2},{4,5},{5,4},{6,7},{7,6},{8,9},{9,8},{10,11... | collective-permute-start | bytes 786440 | tf_op jit(solution)/shard_map/ppermute | solution.py:270
  80.6 10.6 %collective-permute-start.24 = (bf16[128,1024]{1,0:T(8,128)(2,1)}, bf16[128,1024]{1,0:T(8,128)(2,1)S(1)}, u32[]{:S(2)}, u32[]{:S(2)}) collective-permute-start(bf16[128,1024]{1,0:T(8,128)(2,1)} %collective-permute-done.22.refs_1_), channel_id=1, source_target_pairs={{0,1},{1,0},{2,3},{3,2},{4,5},{5,4},{6,7},{7,6},{8,9},{9,8},{10,11... | collective-permute-start | bytes 786440 | tf_op jit(solution)/shard_map/ppermute | solution.py:270
  82.2 13.1 %collective-permute-start.34 = (bf16[128,1024]{1,0:T(8,128)(2,1)}, bf16[128,1024]{1,0:T(8,128)(2,1)S(1)}, u32[]{:S(2)}, u32[]{:S(2)}) collective-permute-start(bf16[128,1024]{1,0:T(8,128)(2,1)} %collective-permute-done.22.refs_1_), channel_id=1, source_target_pairs={{0,8},{4,12},{8,16},{12,20},{16,24},{20,28},{24,0},{28,4},{1,9},{5... | collective-permute-start | bytes 786440 | tf_op jit(solution)/shard_map/ppermute | solution.py:263
  85.0 11.0 %collective-permute-start.19 = (bf16[2,2,64,512]{3,2,1,0:T(8,128)(2,1)S(1)}, bf16[2,2,64,512]{3,2,1,0:T(8,128)(2,1)S(1)}, u32[]{:S(2)}, u32[]{:S(2)}) collective-permute-start(bf16[2,2,64,512]{3,2,1,0:T(8,128)(2,1)S(1)} %get-tuple-element.84), channel_id=1, source_target_pairs={{0,2},{1,3},{2,0},{3,1},{4,6},{5,7},{6,4},{7,5},{8,10},{9,11},{10,... | collective-permute-start | bytes 786440 | tf_op jit(solution)/shard_map/ppermute | solution.py:274
  88.9 8.0 %collective-permute-start.28 = (bf16[128,1024]{1,0:T(8,128)(2,1)S(1)}, bf16[128,1024]{1,0:T(8,128)(2,1)S(1)}, u32[]{:S(2)}, u32[]{:S(2)}) collective-permute-start(bf16[128,1024]{1,0:T(8,128)(2,1)S(1)} %collective-permute-done.27.refs_0_), channel_id=1, source_target_pairs={{0,1},{1,0},{2,3},{3,2},{4,5},{5,4},{6,7},{7,6},{8,9},{9,8},{10,11... | collective-permute-start | bytes 786440 | tf_op jit(solution)/shard_map/ppermute | solution.py:270
  93.8 8.1 %collective-permute-start.25 = (bf16[2,2,64,512]{3,2,1,0:T(8,128)(2,1)S(1)}, bf16[2,2,64,512]{3,2,1,0:T(8,128)(2,1)S(1)}, u32[]{:S(2)}, u32[]{:S(2)}) collective-permute-start(bf16[2,2,64,512]{3,2,1,0:T(8,128)(2,1)S(1)} %get-tuple-element.86), channel_id=1, source_target_pairs={{0,2},{1,3},{2,0},{3,1},{4,6},{5,7},{6,4},{7,5},{8,10},{9,11},{10,... | collective-permute-start | bytes 786440 | tf_op jit(solution)/shard_map/ppermute | solution.py:274
  95.2 12.3 %collective-permute-start.14 = (bf16[2,2,64,512]{3,2,1,0:T(8,128)(2,1)S(1)}, bf16[2,2,64,512]{3,2,1,0:T(8,128)(2,1)S(1)}, u32[]{:S(2)}, u32[]{:S(2)}) collective-permute-start(bf16[2,2,64,512]{3,2,1,0:T(8,128)(2,1)S(1)} %get-tuple-element.82), channel_id=1, source_target_pairs={{0,2},{1,3},{2,0},{3,1},{4,6},{5,7},{6,4},{7,5},{8,10},{9,11},{10,... | collective-permute-start | bytes 786440 | tf_op jit(solution)/shard_map/ppermute | solution.py:274
  95.4 12.1 %collective-permute-start.35 = (bf16[128,1024]{1,0:T(8,128)(2,1)S(1)}, bf16[128,1024]{1,0:T(8,128)(2,1)S(1)}, u32[]{:S(2)}, u32[]{:S(2)}) collective-permute-start(bf16[128,1024]{1,0:T(8,128)(2,1)S(1)} %collective-permute-done.34.refs_0_), channel_id=1, source_target_pairs={{0,1},{1,0},{2,3},{3,2},{4,5},{5,4},{6,7},{7,6},{8,9},{9,8},{10,11... | collective-permute-start | bytes 786440 | tf_op jit(solution)/shard_map/ppermute | solution.py:270
  96.7 18.6 %collective-permute-start.20 = (bf16[2,2,64,512]{3,2,1,0:T(8,128)(2,1)}, bf16[2,2,64,512]{3,2,1,0:T(8,128)(2,1)}, u32[]{:S(2)}, u32[]{:S(2)}) collective-permute-start(bf16[2,2,64,512]{3,2,1,0:T(8,128)(2,1)} %shard_map.83), channel_id=1, source_target_pairs={{0,24},{4,28},{8,0},{12,4},{16,8},{20,12},{24,16},{28,20},{1,25},{... | collective-permute-start | bytes 786440 | tf_op jit(solution)/shard_map/ppermute | solution.py:263
  97.8 13.3 %collective-permute-start.29 = (bf16[1,2,64,512]{3,2,1,0:T(8,128)(2,1)S(1)}, bf16[1,2,64,512]{3,2,1,0:T(8,128)(2,1)S(1)}, u32[]{:S(2)}, u32[]{:S(2)}) collective-permute-start(bf16[1,2,64,512]{3,2,1,0:T(8,128)(2,1)S(1)} %get-tuple-element.90), channel_id=1, source_target_pairs={{0,2},{1,3},{2,0},{3,1},{4,6},{5,7},{6,4},{7,5},{8,10},{9,11},{10,... | collective-permute-start | bytes 393224 | tf_op jit(solution)/shard_map/ppermute | solution.py:274
  102.7 14.8 %collective-permute-start.26 = (bf16[2,2,64,512]{3,2,1,0:T(8,128)(2,1)}, bf16[2,2,64,512]{3,2,1,0:T(8,128)(2,1)}, u32[]{:S(2)}, u32[]{:S(2)}) collective-permute-start(bf16[2,2,64,512]{3,2,1,0:T(8,128)(2,1)} %shard_map.85), channel_id=1, source_target_pairs={{0,16},{4,20},{8,24},{12,28},{16,0},{20,4},{24,8},{28,12},{1,17},{... | collective-permute-start | bytes 786440 | tf_op jit(solution)/shard_map/ppermute | solution.py:263
  107.5 1.6 %copy-start.7 = (bf16[2,2,64,512]{3,2,1,0:T(8,128)(2,1)}, bf16[2,2,64,512]{3,2,1,0:T(8,128)(2,1)S(1)}, u32[]{:S(2)}) copy-start(bf16[2,2,64,512]{3,2,1,0:T(8,128)(2,1)S(1)} %shard_map.81.refs_0_) | copy-start | bytes 786436
  109.1 0.7 copy-start.18
  109.8 4.4 %collective-permute-start.36 = (bf16[1,2,64,512]{3,2,1,0:T(8,128)(2,1)}, bf16[1,2,64,512]{3,2,1,0:T(8,128)(2,1)S(1)}, u32[]{:S(2)}, u32[]{:S(2)}) collective-permute-start(bf16[1,2,64,512]{3,2,1,0:T(8,128)(2,1)} %get-tuple-element.98), channel_id=1, source_target_pairs={{0,2},{1,3},{2,0},{3,1},{4,6},{5,7},{6,4},{7,5},{8,10},{9,11},{10,... | collective-permute-start | bytes 393224 | tf_op jit(solution)/shard_map/ppermute | solution.py:274
  111.2 6.3 %collective-permute-start.30 = (bf16[1,2,64,512]{3,2,1,0:T(8,128)(2,1)S(1)}, bf16[1,2,64,512]{3,2,1,0:T(8,128)(2,1)S(1)}, u32[]{:S(2)}, u32[]{:S(2)}) collective-permute-start(bf16[1,2,64,512]{3,2,1,0:T(8,128)(2,1)S(1)} %shard_map.87), channel_id=1, source_target_pairs={{0,8},{4,12},{8,16},{12,20},{16,24},{20,28},{24,0},{28,4},{1,9},{5... | collective-permute-start | bytes 393224 | tf_op jit(solution)/shard_map/ppermute | solution.py:263
  114.3 1.0 copy-start.19
  115.3 7.7 %collective-permute-start.37 = (bf16[1,2,64,512]{3,2,1,0:T(8,128)(2,1)S(1)}, bf16[1,2,64,512]{3,2,1,0:T(8,128)(2,1)S(1)}, u32[]{:S(2)}, u32[]{:S(2)}) collective-permute-start(bf16[1,2,64,512]{3,2,1,0:T(8,128)(2,1)S(1)} %shard_map.90), channel_id=1, source_target_pairs={{0,8},{4,12},{8,16},{12,20},{16,24},{20,28},{24,0},{28,4},{1,9},{5... | collective-permute-start | bytes 393224 | tf_op jit(solution)/shard_map/ppermute | solution.py:263
  117.5 1.0 copy-start.8
  119.5 7.1 %collective-permute-start.31 = (bf16[2,64,512]{2,1,0:T(8,128)(2,1)S(1)}, bf16[2,64,512]{2,1,0:T(8,128)(2,1)S(1)}, u32[]{:S(2)}, u32[]{:S(2)}) collective-permute-start(bf16[2,64,512]{2,1,0:T(8,128)(2,1)S(1)} %get-tuple-element.92), channel_id=1, source_target_pairs={{0,1},{1,2},{2,3},{3,0},{4,5},{5,6},{6,7},{7,4},{8,9},{9,10},{10,1... | collective-permute-start | bytes 393224 | tf_op jit(solution)/shard_map/ppermute | solution.py:277
  122.3 6.6 %collective-permute-start.32 = (bf16[2,64,512]{2,1,0:T(8,128)(2,1)S(1)}, bf16[2,64,512]{2,1,0:T(8,128)(2,1)S(1)}, u32[]{:S(2)}, u32[]{:S(2)}) collective-permute-start(bf16[2,64,512]{2,1,0:T(8,128)(2,1)S(1)} %get-tuple-element.93), channel_id=1, source_target_pairs={{0,2},{1,3},{2,0},{3,1},{4,6},{5,7},{6,4},{7,5},{8,10},{9,11},{10,... | collective-permute-start | bytes 393224 | tf_op jit(solution)/shard_map/ppermute | solution.py:277
  122.9 7.5 %collective-permute-start.33 = (bf16[2,64,512]{2,1,0:T(8,128)(2,1)S(1)}, bf16[2,64,512]{2,1,0:T(8,128)(2,1)S(1)}, u32[]{:S(2)}, u32[]{:S(2)}) collective-permute-start(bf16[2,64,512]{2,1,0:T(8,128)(2,1)S(1)} %get-tuple-element.94), channel_id=1, source_target_pairs={{0,3},{1,0},{2,1},{3,2},{4,7},{5,4},{6,5},{7,6},{8,11},{9,8},{10,9... | collective-permute-start | bytes 393224 | tf_op jit(solution)/shard_map/ppermute | solution.py:277
  124.0 6.6 %collective-permute-start.38 = (bf16[2,64,512]{2,1,0:T(8,128)(2,1)S(1)}, bf16[2,64,512]{2,1,0:T(8,128)(2,1)S(1)}, u32[]{:S(2)}, u32[]{:S(2)}) collective-permute-start(bf16[2,64,512]{2,1,0:T(8,128)(2,1)S(1)} %get-tuple-element.100), channel_id=1, source_target_pairs={{0,1},{1,2},{2,3},{3,0},{4,5},{5,6},{6,7},{7,4},{8,9},{9,10},{10,1... | collective-permute-start | bytes 393224 | tf_op jit(solution)/shard_map/ppermute | solution.py:277
  126.3 8.2 %collective-permute-start.39 = (bf16[2,64,512]{2,1,0:T(8,128)(2,1)S(1)}, bf16[2,64,512]{2,1,0:T(8,128)(2,1)S(1)}, u32[]{:S(2)}, u32[]{:S(2)}) collective-permute-start(bf16[2,64,512]{2,1,0:T(8,128)(2,1)S(1)} %get-tuple-element.101), channel_id=1, source_target_pairs={{0,2},{1,3},{2,0},{3,1},{4,6},{5,7},{6,4},{7,5},{8,10},{9,11},{10,... | collective-permute-start | bytes 393224 | tf_op jit(solution)/shard_map/ppermute | solution.py:277
  126.6 8.5 %collective-permute-start.40 = (bf16[2,64,512]{2,1,0:T(8,128)(2,1)S(1)}, bf16[2,64,512]{2,1,0:T(8,128)(2,1)S(1)}, u32[]{:S(2)}, u32[]{:S(2)}) collective-permute-start(bf16[2,64,512]{2,1,0:T(8,128)(2,1)S(1)} %get-tuple-element.102), channel_id=1, source_target_pairs={{0,3},{1,0},{2,1},{3,2},{4,7},{5,4},{6,5},{7,6},{8,11},{9,8},{10,9... | collective-permute-start | bytes 393224 | tf_op jit(solution)/shard_map/ppermute | solution.py:277
